TPU v7x, 128 devices: a whole 4x4x4 slice. The times are simulated.
128 devices in a mesh: slab: 16 (over x_lo, y, core), col: 8 (over z, x_hi).
Axes of the slice: x: 4 (x_hi: 2, x_lo: 2; x = x_hi * 2 + x_lo), y: 4, z: 4, core: 2. Of those that a mesh axis runs over, the one named last changes fastest.
Arguments:
- rest_points: float32 [3, 16, 16, 128], P(None, 'slab', 'col'), may hold values from 0 to 16, as said below
- tile_fill: int32 [16, 16], P('slab', 'col'), may hold values from 32 to 128, as said below
- displacement: float32 [3, 16, 16, 128], P(None, 'slab', 'col'), may hold values from -0.6 to 0.6
- velocity: float32 [3, 16, 16, 128], P(None, 'slab', 'col'), may hold values from -0.6 to 0.6
- back_extension: bfloat16 [2, 16, 16, 9, 128, 128], P(None, 'slab', 'col'), may hold values from -0.59765625 to 0.59765625
Outputs:
- displacement_out: float32 [3, 16, 16, 128], P(None, 'slab', 'col')
- velocity_out: float32 [3, 16, 16, 128], P(None, 'slab', 'col')
- back_extension_out: bfloat16 [2, 16, 16, 9, 128, 128], P(None, 'slab', 'col')
Inputs may be any that keep to these rules, and one draw needn't show every extreme that they name: `tile_fill`: point slots of a tile are filled from the first one; at least a quarter of the 128 slots are live. `rest_points`: the points of tile (r, c) lie in its unit box: r plus [0, 1) along the first component, c plus [0, 1) along the second, [0, 1) along the third.
All inputs are finite; a program needn't handle non-finite values.
Results may differ from a plain program's by a relative error of at most 0.0051.
Values sent between devices are 32-bit elements; how exact they have to be, the bound alone decides.
No kernel may reach another device: no remote copies, remote signals or barrier semaphores. Data moves between devices by JAX's collectives and lax.ppermute only.
A program may use at most 128 MiB of HBM per device.

v0:
```python
import jax
import jax.numpy as jnp
from jax import lax
from jax.sharding import PartitionSpec as P

STEPS = 2


stencil_offsets = [(-1, -1), (-1, 0), (-1, 1), (0, -1), (0, 0), (0, 1), (1, -1), (1, 0), (1, 1)]


def with_halo(array, sides, width):
    for axis, dim in sides:
        peers, length = (lax.axis_size(axis), array.shape[dim])
        up = [(i, (i + 1) % peers) for i in range(peers - 1)]
        down = [(j, i) for i, j in up]
        last = lax.slice_in_dim(array, length - width, length, axis=dim)
        leading = lax.slice_in_dim(array, 0, width, axis=dim)
        before = lax.ppermute(last, axis, up)
        after = lax.ppermute(leading, axis, down)
        array = jnp.concatenate([before, array, after], axis=dim)
    return array


def pair_geometry(rest_halo, alive_halo, rows, cols, row_shift, col_shift):
    home_side = rest_halo[:, 1 : 1 + rows, 1 : 1 + cols, :, None]
    far_side = rest_halo[
        :, 1 + row_shift : 1 + row_shift + rows, 1 + col_shift : 1 + col_shift + cols, None, :
    ]
    bond = far_side - home_side
    length = jnp.sqrt(jnp.sum(bond * bond, axis=0))
    closeness = jnp.maximum(1.0 - length, 0.0)
    weight = closeness * closeness * alive_halo[1 : 1 + rows, 1 : 1 + cols, :, None]
    weight = (
        weight
        * alive_halo[
            1 + row_shift : 1 + row_shift + rows, 1 + col_shift : 1 + col_shift + cols, None, :
        ]
    )
    if row_shift == 0 and col_shift == 0:
        weight = weight * (1.0 - jnp.eye(weight.shape[-1], dtype=jnp.float32))
    return (length, weight)


def deformed(place_halo, length, rows, cols, row_shift, col_shift):
    home_side = place_halo[:, 1 : 1 + rows, 1 : 1 + cols, :, None]
    far_side = place_halo[
        :, 1 + row_shift : 1 + row_shift + rows, 1 + col_shift : 1 + col_shift + cols, None, :
    ]
    separation = far_side - home_side
    squared = jnp.sum(separation * separation, axis=0)
    stretch = jnp.sqrt(squared) - length
    bearing = separation * jax.lax.rsqrt(squared + 0.01)
    return (stretch, bearing)


def per_device(rest_points, tile_fill, displacement, velocity, back_extension):
    rows, cols, points = (rest_points.shape[1], rest_points.shape[2], rest_points.shape[3])
    alive = (jnp.arange(points, dtype=jnp.int32)[None, None, :] < tile_fill[:, :, None]).astype(
        jnp.float32
    )
    joined = jnp.concatenate([rest_points, alive[None]], 0)
    joined_halo = with_halo(joined, (("slab", 1), ("col", 2)), 1)
    rest_halo = joined_halo[:3]
    alive_halo = joined_halo[3]
    geometry = [
        pair_geometry(rest_halo, alive_halo, rows, cols, rs, cs) for rs, cs in stencil_offsets
    ]
    volume = jnp.zeros((rows, cols, points), jnp.float32)
    for length, weight in geometry:
        volume = volume + jnp.sum(weight * length * length, axis=-1)
    volume = jnp.maximum(volume, 1.0)
    history = back_extension
    for step_index in range(STEPS):
        moved_halo = with_halo(displacement, (("slab", 1), ("col", 2)), 1)
        place_halo = rest_halo + moved_halo
        shapes = [
            deformed(place_halo, geometry[index][0], rows, cols, rs, cs)
            for index, (rs, cs) in enumerate(stencil_offsets)
        ]
        dilatation = jnp.zeros((rows, cols, points), jnp.float32)
        for index in range(9):
            length, weight = geometry[index]
            dilatation = dilatation + jnp.sum(weight * length * shapes[index][0], axis=-1)
        dilatation = 3.0 * dilatation / volume
        forces, first_states, second_states = ([], [], [])
        for index in range(9):
            length, weight = geometry[index]
            deviator = shapes[index][0] - dilatation[..., None] * length / 3.0
            back_one = 0.6 * history[0, :, :, index].astype(jnp.float32) + 0.4 * deviator
            back_two = 0.95 * history[1, :, :, index].astype(jnp.float32) + 0.05 * deviator
            bond_force = 3.0 * dilatation[..., None] * weight * length / volume[..., None]
            bond_force = bond_force + 7.5 * weight / volume[..., None] * (
                0.4 * deviator + 0.35 * (deviator - back_one) + 0.25 * (deviator - back_two)
            )
            forces.append(bond_force)
            first_states.append(back_one)
            second_states.append(back_two)
        history = jnp.stack([jnp.stack(first_states, 2), jnp.stack(second_states, 2)], 0).astype(
            jnp.bfloat16
        )
        force_halo = with_halo(jnp.stack(forces, 0), (("slab", 1), ("col", 2)), 1)
        total_force = jnp.zeros((3, rows, cols, points), jnp.float32)
        for index, (rs, cs) in enumerate(stencil_offsets):
            reverse = force_halo[8 - index, 1 + rs : 1 + rs + rows, 1 + cs : 1 + cs + cols]
            reverse = jnp.swapaxes(reverse, -1, -2)
            total_force = total_force + jnp.sum(
                (forces[index] + reverse)[None] * shapes[index][1], axis=-1
            )
        velocity = velocity + 0.2 * total_force
        displacement = displacement + 0.2 * velocity
    return (displacement, velocity, history)


def solution(mesh):
    in_specs = (
        P(None, "slab", "col", None),
        P("slab", "col"),
        P(None, "slab", "col", None),
        P(None, "slab", "col", None),
        P(None, "slab", "col", None, None, None),
    )
    out_specs = (
        P(None, "slab", "col", None),
        P(None, "slab", "col", None),
        P(None, "slab", "col", None, None, None),
    )
    return jax.shard_map(
        per_device, mesh=mesh, in_specs=in_specs, out_specs=out_specs, check_vma=False
    )
```

profile of v0, /device:TPU:2, one launch (start us, length us, event | category | flops | bytes accessed | tf_op | source)
XLA Modules:
  0.0 350.5 jit_solution(3458902061684179129)
XLA Ops:
  0.6 4.3 %collective-permute-start.5 = (f32[3,1,2,128]{3,2,0,1:T(2,128)}, f32[3,1,2,128]{3,2,0,1:T(2,128)S(1)}, u32[]{:S(2)}, u32[]{:S(2)}) collective-permute-start(f32[3,1,2,128]{3,2,0,1:T(2,128)} %bitcast.2505), channel_id=1, source_target_pairs={{8,0},{16,8},{24,16},{32,24},{40,32},{48,40},{56,48},{64,56},{72,6... | collective-permute-start | bytes 9224 | tf_op jit(solution)/shard_map/ppermute | solution.py:20
  8.3 5.7 %collective-permute-start.1 = (f32[4,1,2,128]{3,2,0,1:T(2,128)S(1)}, f32[4,1,2,128]{3,2,0,1:T(2,128)S(1)}, u32[]{:S(2)}, u32[]{:S(2)}) collective-permute-start(f32[4,1,2,128]{3,2,0,1:T(2,128)S(1)} %pad_maximum_fusion.23), channel_id=1, source_target_pairs={{8,0},{16,8},{24,16},{32,24},{40,32},{48,40},{56,48},{64,56},{72,6... | collective-permute-start | bytes 12296 | tf_op jit(solution)/shard_map/ppermute | solution.py:20
  18.0 6.1 %collective-permute-start.6 = (f32[3,3,1,128]{3,2,0,1:T(1,128)S(1)}, f32[3,3,1,128]{3,2,0,1:T(1,128)S(1)}, u32[]{:S(2)}, u32[]{:S(2)}) collective-permute-start(f32[3,3,1,128]{3,2,0,1:T(1,128)S(1)} %get-tuple-element.244), channel_id=1, source_target_pairs={{0,1},{1,2},{2,3},{3,4},{4,5},{5,6},{6,7},{8,9},{9,10},{10,11},{11... | collective-permute-start | bytes 13832 | tf_op jit(solution)/shard_map/ppermute | solution.py:19
  26.1 6.1 %collective-permute-start.2 = (f32[4,3,1,128]{3,2,0,1:T(1,128)S(1)}, f32[4,3,1,128]{3,2,0,1:T(1,128)S(1)}, u32[]{:S(2)}, u32[]{:S(2)}) collective-permute-start(f32[4,3,1,128]{3,2,0,1:T(1,128)S(1)} %get-tuple-element.240), channel_id=1, source_target_pairs={{0,1},{1,2},{2,3},{3,4},{4,5},{5,6},{6,7},{8,9},{9,10},{10,11},{11... | collective-permute-start | bytes 18440 | tf_op jit(solution)/shard_map/ppermute | solution.py:19
  42.8 2.2 multiply_reduce_fusion.34
  51.4 2.4 fusion.450
  58.3 2.3 fusion.459
  65.9 4.7 %collective-permute-start.9 = (f32[9,1,2,128,128]{3,4,2,1,0:T(8,128)S(1)}, f32[9,1,2,128,128]{3,4,2,1,0:T(8,128)S(1)}, u32[]{:S(2)}, u32[]{:S(2)}) collective-permute-start(f32[9,1,2,128,128]{3,4,2,1,0:T(8,128)S(1)} %add_dynamic-update-slice_fusion), channel_id=1, source_target_pairs={{8,0},{16,8},{24,16},{32,24},{40,32},{48,40},{56,48},{64,56},{72,6... | collective-permute-start | bytes 3538952 | tf_op jit(solution)/shard_map/ppermute | solution.py:20
  73.3 11.1 %collective-permute-done.9 = f32[9,1,2,128,128]{3,4,2,1,0:T(8,128)S(1)} collective-permute-done((f32[9,1,2,128,128]{3,4,2,1,0:T(8,128)S(1)}, f32[9,1,2,128,128]{3,4,2,1,0:T(8,128)S(1)}, u32[]{:S(2)}, u32[]{:S(2)}) %collective-permute-start.9) | collective-permute-done | bytes 1179680 | tf_op jit(solution)/shard_map/ppermute | solution.py:20
  84.4 5.9 %collective-permute-done.8 = f32[9,1,2,128,128]{3,4,2,1,0:T(8,128)S(1)} collective-permute-done((f32[9,1,2,128,128]{3,4,2,1,0:T(8,128)S(1)}, f32[9,1,2,128,128]{3,4,2,1,0:T(8,128)S(1)}, u32[]{:S(2)}, u32[]{:S(2)}) %collective-permute-start.8) | collective-permute-done | bytes 1179680 | tf_op jit(solution)/shard_map/ppermute | solution.py:19
  90.8 2.1 fusion.595
  92.9 6.8 %collective-permute-start.10 = (f32[9,3,1,128,128]{3,4,2,1,0:T(8,128)}, f32[9,3,1,128,128]{3,4,2,1,0:T(8,128)}, u32[]{:S(2)}, u32[]{:S(2)}) collective-permute-start(f32[9,3,1,128,128]{3,4,2,1,0:T(8,128)} %get-tuple-element.117), channel_id=1, source_target_pairs={{0,1},{1,2},{2,3},{3,4},{4,5},{5,6},{6,7},{8,9},{9,10},{10,11},{11... | collective-permute-start | bytes 5308424 | tf_op jit(solution)/shard_map/ppermute | solution.py:19
  109.5 21.0 %collective-permute-done.10 = f32[9,3,1,128,128]{3,4,2,1,0:T(8,128)} collective-permute-done((f32[9,3,1,128,128]{3,4,2,1,0:T(8,128)}, f32[9,3,1,128,128]{3,4,2,1,0:T(8,128)}, u32[]{:S(2)}, u32[]{:S(2)}) %collective-permute-start.10) | collective-permute-done | bytes 1769504 | tf_op jit(solution)/shard_map/ppermute | solution.py:19
  130.6 2.1 fusion.374
  137.2 36.4 %collective-permute-done.11 = f32[9,3,1,128,128]{3,4,2,1,0:T(8,128)} collective-permute-done((f32[9,3,1,128,128]{3,4,2,1,0:T(8,128)}, f32[9,3,1,128,128]{3,4,2,1,0:T(8,128)}, u32[]{:S(2)}, u32[]{:S(2)}) %collective-permute-start.11) | collective-permute-done | bytes 1769504 | tf_op jit(solution)/shard_map/ppermute | solution.py:20
  181.7 5.4 %collective-permute-start.13 = (f32[3,1,2,128]{3,2,0,1:T(2,128)S(1)}, f32[3,1,2,128]{3,2,0,1:T(2,128)S(1)}, u32[]{:S(2)}, u32[]{:S(2)}) collective-permute-start(f32[3,1,2,128]{3,2,0,1:T(2,128)S(1)} %get-tuple-element.110), channel_id=1, source_target_pairs={{8,0},{16,8},{24,16},{32,24},{40,32},{48,40},{56,48},{64,56},{72,6... | collective-permute-start | bytes 9224 | tf_op jit(solution)/shard_map/ppermute | solution.py:20
  189.1 5.0 %collective-permute-done.12 = f32[3,1,2,128]{3,2,0,1:T(2,128)S(1)} collective-permute-done((f32[3,1,2,128]{3,2,0,1:T(2,128)S(1)}, f32[3,1,2,128]{3,2,0,1:T(2,128)S(1)}, u32[]{:S(2)}, u32[]{:S(2)}) %collective-permute-start.12) | collective-permute-done | bytes 3104 | tf_op jit(solution)/shard_map/ppermute | solution.py:19
  195.5 6.1 %collective-permute-start.14 = (f32[3,3,1,128]{3,2,0,1:T(1,128)S(1)}, f32[3,3,1,128]{3,2,0,1:T(1,128)S(1)}, u32[]{:S(2)}, u32[]{:S(2)}) collective-permute-start(f32[3,3,1,128]{3,2,0,1:T(1,128)S(1)} %get-tuple-element.242), channel_id=1, source_target_pairs={{0,1},{1,2},{2,3},{3,4},{4,5},{5,6},{6,7},{8,9},{9,10},{10,11},{11... | collective-permute-start | bytes 13832 | tf_op jit(solution)/shard_map/ppermute | solution.py:19
  211.5 2.1 multiply_reduce_fusion.16
  242.4 6.0 %collective-permute-start.17 = (f32[9,1,2,128,128]{3,4,2,1,0:T(8,128)S(1)}, f32[9,1,2,128,128]{3,4,2,1,0:T(8,128)S(1)}, u32[]{:S(2)}, u32[]{:S(2)}) collective-permute-start(f32[9,1,2,128,128]{3,4,2,1,0:T(8,128)S(1)} %copy.1559), channel_id=1, source_target_pairs={{8,0},{16,8},{24,16},{32,24},{40,32},{48,40},{56,48},{64,56},{72,6... | collective-permute-start | bytes 3538952 | tf_op jit(solution)/shard_map/ppermute | solution.py:20
  263.9 3.5 %collective-permute-start.18 = (f32[9,3,1,128,128]{3,4,2,1,0:T(8,128)S(1)}, f32[9,3,1,128,128]{3,4,2,1,0:T(8,128)S(1)}, u32[]{:S(2)}, u32[]{:S(2)}) collective-permute-start(f32[9,3,1,128,128]{3,4,2,1,0:T(8,128)S(1)} %get-tuple-element.115), channel_id=1, source_target_pairs={{0,1},{1,2},{2,3},{3,4},{4,5},{5,6},{6,7},{8,9},{9,10},{10,11},{11... | collective-permute-start | bytes 5308424 | tf_op jit(solution)/shard_map/ppermute | solution.py:19
  271.5 28.8 %collective-permute-done.18 = f32[9,3,1,128,128]{3,4,2,1,0:T(8,128)S(1)} collective-permute-done((f32[9,3,1,128,128]{3,4,2,1,0:T(8,128)S(1)}, f32[9,3,1,128,128]{3,4,2,1,0:T(8,128)S(1)}, u32[]{:S(2)}, u32[]{:S(2)}) %collective-permute-start.18) | collective-permute-done | bytes 1769504 | tf_op jit(solution)/shard_map/ppermute | solution.py:19
  310.3 2.4 fusion.157
  315.4 26.9 %collective-permute-done.19 = f32[9,3,1,128,128]{3,4,2,1,0:T(8,128)} collective-permute-done((f32[9,3,1,128,128]{3,4,2,1,0:T(8,128)}, f32[9,3,1,128,128]{3,4,2,1,0:T(8,128)}, u32[]{:S(2)}, u32[]{:S(2)}) %collective-permute-start.19) | collective-permute-done | bytes 1769504 | tf_op jit(solution)/shard_map/ppermute | solution.py:20
  (686 shorter events, 140.4 us)
Async XLA Ops:
  0.6 15.4 %collective-permute-start.5 = (f32[3,1,2,128]{3,2,0,1:T(2,128)}, f32[3,1,2,128]{3,2,0,1:T(2,128)S(1)}, u32[]{:S(2)}, u32[]{:S(2)}) collective-permute-start(f32[3,1,2,128]{3,2,0,1:T(2,128)} %bitcast.2505), channel_id=1, source_target_pairs={{8,0},{16,8},{24,16},{32,24},{40,32},{48,40},{56,48},{64,56},{72,6... | collective-permute-start | bytes 9224 | tf_op jit(solution)/shard_map/ppermute | solution.py:20
  5.0 11.0 %collective-permute-start.4 = (f32[3,1,2,128]{3,2,0,1:T(2,128)}, f32[3,1,2,128]{3,2,0,1:T(2,128)S(1)}, u32[]{:S(2)}, u32[]{:S(2)}) collective-permute-start(f32[3,1,2,128]{3,2,0,1:T(2,128)} %bitcast.2506), channel_id=1, source_target_pairs={{0,8},{8,16},{16,24},{24,32},{32,40},{40,48},{48,56},{56,64},{64,7... | collective-permute-start | bytes 9224 | tf_op jit(solution)/shard_map/ppermute | solution.py:19
  8.3 15.8 %collective-permute-start.1 = (f32[4,1,2,128]{3,2,0,1:T(2,128)S(1)}, f32[4,1,2,128]{3,2,0,1:T(2,128)S(1)}, u32[]{:S(2)}, u32[]{:S(2)}) collective-permute-start(f32[4,1,2,128]{3,2,0,1:T(2,128)S(1)} %pad_maximum_fusion.23), channel_id=1, source_target_pairs={{8,0},{16,8},{24,16},{32,24},{40,32},{48,40},{56,48},{64,56},{72,6... | collective-permute-start | bytes 12296 | tf_op jit(solution)/shard_map/ppermute | solution.py:20
  14.1 10.0 %collective-permute-start = (f32[4,1,2,128]{3,2,0,1:T(2,128)S(1)}, f32[4,1,2,128]{3,2,0,1:T(2,128)S(1)}, u32[]{:S(2)}, u32[]{:S(2)}) collective-permute-start(f32[4,1,2,128]{3,2,0,1:T(2,128)S(1)} %pad_maximum_fusion.23), channel_id=1, source_target_pairs={{0,8},{8,16},{16,24},{24,32},{32,40},{40,48},{48,56},{56,64},{64,7... | collective-permute-start | bytes 12296 | tf_op jit(solution)/shard_map/ppermute | solution.py:19
  16.7 15.5 %collective-permute-start.7 = (f32[3,3,1,128]{3,2,0,1:T(1,128)S(1)}, f32[3,3,1,128]{3,2,0,1:T(1,128)S(1)}, u32[]{:S(2)}, u32[]{:S(2)}) collective-permute-start(f32[3,3,1,128]{3,2,0,1:T(1,128)S(1)} %get-tuple-element.245), channel_id=1, source_target_pairs={{1,0},{2,1},{3,2},{4,3},{5,4},{6,5},{7,6},{9,8},{10,9},{11,10},{12... | collective-permute-start | bytes 13832 | tf_op jit(solution)/shard_map/ppermute | solution.py:20
  18.0 14.2 %collective-permute-start.6 = (f32[3,3,1,128]{3,2,0,1:T(1,128)S(1)}, f32[3,3,1,128]{3,2,0,1:T(1,128)S(1)}, u32[]{:S(2)}, u32[]{:S(2)}) collective-permute-start(f32[3,3,1,128]{3,2,0,1:T(1,128)S(1)} %get-tuple-element.244), channel_id=1, source_target_pairs={{0,1},{1,2},{2,3},{3,4},{4,5},{5,6},{6,7},{8,9},{9,10},{10,11},{11... | collective-permute-start | bytes 13832 | tf_op jit(solution)/shard_map/ppermute | solution.py:19
  24.8 7.4 %collective-permute-start.3 = (f32[4,3,1,128]{3,2,0,1:T(1,128)S(1)}, f32[4,3,1,128]{3,2,0,1:T(1,128)S(1)}, u32[]{:S(2)}, u32[]{:S(2)}) collective-permute-start(f32[4,3,1,128]{3,2,0,1:T(1,128)S(1)} %get-tuple-element.241), channel_id=1, source_target_pairs={{1,0},{2,1},{3,2},{4,3},{5,4},{6,5},{7,6},{9,8},{10,9},{11,10},{12... | collective-permute-start | bytes 18440 | tf_op jit(solution)/shard_map/ppermute | solution.py:20
  26.1 7.4 %collective-permute-start.2 = (f32[4,3,1,128]{3,2,0,1:T(1,128)S(1)}, f32[4,3,1,128]{3,2,0,1:T(1,128)S(1)}, u32[]{:S(2)}, u32[]{:S(2)}) collective-permute-start(f32[4,3,1,128]{3,2,0,1:T(1,128)S(1)} %get-tuple-element.240), channel_id=1, source_target_pairs={{0,1},{1,2},{2,3},{3,4},{4,5},{5,6},{6,7},{8,9},{9,10},{10,11},{11... | collective-permute-start | bytes 18440 | tf_op jit(solution)/shard_map/ppermute | solution.py:19
  65.9 18.5 %collective-permute-start.9 = (f32[9,1,2,128,128]{3,4,2,1,0:T(8,128)S(1)}, f32[9,1,2,128,128]{3,4,2,1,0:T(8,128)S(1)}, u32[]{:S(2)}, u32[]{:S(2)}) collective-permute-start(f32[9,1,2,128,128]{3,4,2,1,0:T(8,128)S(1)} %add_dynamic-update-slice_fusion), channel_id=1, source_target_pairs={{8,0},{16,8},{24,16},{32,24},{40,32},{48,40},{56,48},{64,56},{72,6... | collective-permute-start | bytes 3538952 | tf_op jit(solution)/shard_map/ppermute | solution.py:20
  70.7 19.6 %collective-permute-start.8 = (f32[9,1,2,128,128]{3,4,2,1,0:T(8,128)S(1)}, f32[9,1,2,128,128]{3,4,2,1,0:T(8,128)S(1)}, u32[]{:S(2)}, u32[]{:S(2)}) collective-permute-start(f32[9,1,2,128,128]{3,4,2,1,0:T(8,128)S(1)} %add_dynamic-update-slice_fusion), channel_id=1, source_target_pairs={{0,8},{8,16},{16,24},{24,32},{32,40},{40,48},{48,56},{56,64},{64,7... | collective-permute-start | bytes 3538952 | tf_op jit(solution)/shard_map/ppermute | solution.py:19
  92.9 37.7 %collective-permute-start.10 = (f32[9,3,1,128,128]{3,4,2,1,0:T(8,128)}, f32[9,3,1,128,128]{3,4,2,1,0:T(8,128)}, u32[]{:S(2)}, u32[]{:S(2)}) collective-permute-start(f32[9,3,1,128,128]{3,4,2,1,0:T(8,128)} %get-tuple-element.117), channel_id=1, source_target_pairs={{0,1},{1,2},{2,3},{3,4},{4,5},{5,6},{6,7},{8,9},{9,10},{10,11},{11... | collective-permute-start | bytes 5308424 | tf_op jit(solution)/shard_map/ppermute | solution.py:19
  100.2 73.4 %collective-permute-start.11 = (f32[9,3,1,128,128]{3,4,2,1,0:T(8,128)}, f32[9,3,1,128,128]{3,4,2,1,0:T(8,128)}, u32[]{:S(2)}, u32[]{:S(2)}) collective-permute-start(f32[9,3,1,128,128]{3,4,2,1,0:T(8,128)} %get-tuple-element.118), channel_id=1, source_target_pairs={{1,0},{2,1},{3,2},{4,3},{5,4},{6,5},{7,6},{9,8},{10,9},{11,10},{12... | collective-permute-start | bytes 5308424 | tf_op jit(solution)/shard_map/ppermute | solution.py:20
  137.2 39.0 %copy-start.43 = (f32[2,128,128]{2,1,0:T(8,128)S(1)}, f32[2,128,128]{2,1,0:T(8,128)}, u32[]{:S(2)}) copy-start(f32[2,128,128]{2,1,0:T(8,128)} %copy-done.41) | copy-start | bytes 393220
  137.2 39.0 %copy-start.70 = (f32[2,128,128]{2,1,0:T(8,128)S(1)}, f32[2,128,128]{2,1,0:T(8,128)}, u32[]{:S(2)}) copy-start(f32[2,128,128]{2,1,0:T(8,128)} %copy-done.68) | copy-start | bytes 393220
  181.7 7.4 %collective-permute-start.13 = (f32[3,1,2,128]{3,2,0,1:T(2,128)S(1)}, f32[3,1,2,128]{3,2,0,1:T(2,128)S(1)}, u32[]{:S(2)}, u32[]{:S(2)}) collective-permute-start(f32[3,1,2,128]{3,2,0,1:T(2,128)S(1)} %get-tuple-element.110), channel_id=1, source_target_pairs={{8,0},{16,8},{24,16},{32,24},{40,32},{48,40},{56,48},{64,56},{72,6... | collective-permute-start | bytes 9224 | tf_op jit(solution)/shard_map/ppermute | solution.py:20
  187.1 7.0 %collective-permute-start.12 = (f32[3,1,2,128]{3,2,0,1:T(2,128)S(1)}, f32[3,1,2,128]{3,2,0,1:T(2,128)S(1)}, u32[]{:S(2)}, u32[]{:S(2)}) collective-permute-start(f32[3,1,2,128]{3,2,0,1:T(2,128)S(1)} %get-tuple-element.110), channel_id=1, source_target_pairs={{0,8},{8,16},{16,24},{24,32},{32,40},{40,48},{48,56},{56,64},{64,7... | collective-permute-start | bytes 9224 | tf_op jit(solution)/shard_map/ppermute | solution.py:19
  194.2 15.9 %collective-permute-start.15 = (f32[3,3,1,128]{3,2,0,1:T(1,128)S(1)}, f32[3,3,1,128]{3,2,0,1:T(1,128)S(1)}, u32[]{:S(2)}, u32[]{:S(2)}) collective-permute-start(f32[3,3,1,128]{3,2,0,1:T(1,128)S(1)} %get-tuple-element.243), channel_id=1, source_target_pairs={{1,0},{2,1},{3,2},{4,3},{5,4},{6,5},{7,6},{9,8},{10,9},{11,10},{12... | collective-permute-start | bytes 13832 | tf_op jit(solution)/shard_map/ppermute | solution.py:20
  195.5 14.6 %collective-permute-start.14 = (f32[3,3,1,128]{3,2,0,1:T(1,128)S(1)}, f32[3,3,1,128]{3,2,0,1:T(1,128)S(1)}, u32[]{:S(2)}, u32[]{:S(2)}) collective-permute-start(f32[3,3,1,128]{3,2,0,1:T(1,128)S(1)} %get-tuple-element.242), channel_id=1, source_target_pairs={{0,1},{1,2},{2,3},{3,4},{4,5},{5,6},{6,7},{8,9},{9,10},{10,11},{11... | collective-permute-start | bytes 13832 | tf_op jit(solution)/shard_map/ppermute | solution.py:19
  210.8 39.3 %copy-start.93 = (f32[2,128,128]{2,1,0:T(8,128)}, f32[2,128,128]{2,1,0:T(8,128)S(1)}, u32[]{:S(2)}) copy-start(f32[2,128,128]{2,1,0:T(8,128)S(1)} %get-tuple-element.45) | copy-start | bytes 393220
  210.8 44.8 %copy-start.95 = (f32[2,128,128]{2,1,0:T(8,128)}, f32[2,128,128]{2,1,0:T(8,128)S(1)}, u32[]{:S(2)}) copy-start(f32[2,128,128]{2,1,0:T(8,128)S(1)} %get-tuple-element.53) | copy-start | bytes 393220
  238.8 19.9 %collective-permute-start.16 = (f32[9,1,2,128,128]{4,3,2,1,0:T(8,128)}, f32[9,1,2,128,128]{4,3,2,1,0:T(8,128)}, u32[]{:S(2)}, u32[]{:S(2)}) collective-permute-start(f32[9,1,2,128,128]{4,3,2,1,0:T(8,128)} %constant_dynamic-update-slice_fusion.26), channel_id=1, source_target_pairs={{0,8},{8,16},{16,24},{24,32},{32,40},{40,48},{48,56},{56,64},{64,7... | collective-permute-start | bytes 3538952 | tf_op jit(solution)/shard_map/ppermute | solution.py:19
  242.4 19.5 %collective-permute-start.17 = (f32[9,1,2,128,128]{3,4,2,1,0:T(8,128)S(1)}, f32[9,1,2,128,128]{3,4,2,1,0:T(8,128)S(1)}, u32[]{:S(2)}, u32[]{:S(2)}) collective-permute-start(f32[9,1,2,128,128]{3,4,2,1,0:T(8,128)S(1)} %copy.1559), channel_id=1, source_target_pairs={{8,0},{16,8},{24,16},{32,24},{40,32},{48,40},{56,48},{64,56},{72,6... | collective-permute-start | bytes 3538952 | tf_op jit(solution)/shard_map/ppermute | solution.py:20
  263.9 36.3 %collective-permute-start.18 = (f32[9,3,1,128,128]{3,4,2,1,0:T(8,128)S(1)}, f32[9,3,1,128,128]{3,4,2,1,0:T(8,128)S(1)}, u32[]{:S(2)}, u32[]{:S(2)}) collective-permute-start(f32[9,3,1,128,128]{3,4,2,1,0:T(8,128)S(1)} %get-tuple-element.115), channel_id=1, source_target_pairs={{0,1},{1,2},{2,3},{3,4},{4,5},{5,6},{6,7},{8,9},{9,10},{10,11},{11... | collective-permute-start | bytes 5308424 | tf_op jit(solution)/shard_map/ppermute | solution.py:19
  268.3 74.0 %collective-permute-start.19 = (f32[9,3,1,128,128]{3,4,2,1,0:T(8,128)}, f32[9,3,1,128,128]{3,4,2,1,0:T(8,128)}, u32[]{:S(2)}, u32[]{:S(2)}) collective-permute-start(f32[9,3,1,128,128]{3,4,2,1,0:T(8,128)} %get-tuple-element.116), channel_id=1, source_target_pairs={{1,0},{2,1},{3,2},{4,3},{5,4},{6,5},{7,6},{9,8},{10,9},{11,10},{12... | collective-permute-start | bytes 5308424 | tf_op jit(solution)/shard_map/ppermute | solution.py:20
  (251 other events, 2403.7 us)
where the time goes:
time: 353 us; the launch traced here: 351 us
  waiting for transfers between devices  138 us (39%)
  starting transfers between devices  70.9 us (20%)
  local copies, waits for them, and re-layouts  69.3 us (20%)
  other arithmetic  67.4 us (19%)
  between operations  4.74 us (1%)
    ppermute x10, waiting for transfers between devices, with_halo(): after = lax.ppermute(leading, axis, down)  75.8 us
    ppermute x10, waiting for transfers between devices, with_halo(): before = lax.ppermute(last, axis, up)  62.4 us
    ppermute x10, starting transfers between devices, with_halo(): before = lax.ppermute(last, axis, up)  38.1 us
    ppermute x10, starting transfers between devices, with_halo(): after = lax.ppermute(leading, axis, down)  32.8 us
    mul x12, other arithmetic, per_device(): (forces[index] + reverse)[None] * shapes[index][1]  16.3 us
    add x14, local copies, waits for them, and re-layouts, per_device(): bond_force + 7.5 * weight / volume[..., None] * (0.4 * deviator + 0.35 *...  12.8 us
    add x7, other arithmetic, per_device(): bond_force + 7.5 * weight / volume[..., None] * (0.4 * deviator + 0.35 *...  12.7 us
    unnamed x524, local copies, waits for them, and re-layouts  10.1 us
  transfers between devices with their start and end apart: 20, of which 10 were waited for; matrix products, arithmetic and copies ran while one was open for 16% of the time, Pallas kernels for 0%

commit v1 on v0

v1 whole, which is shorter than its diff:
```python
import functools

import jax
import jax.numpy as jnp
from jax import lax
from jax.experimental import pallas as pl
from jax.experimental.pallas import tpu as pltpu
from jax.sharding import PartitionSpec as P

OFFSETS = [(-1, -1), (-1, 0), (-1, 1), (0, -1), (0, 0), (0, 1), (1, -1), (1, 0), (1, 1)]
LANES = 128
CHUNK = 16
DEAD = -1e9


def root(squared):
    return squared * lax.rsqrt(jnp.maximum(squared, 1e-36))


def step_kernel(first, *refs):
    if first:
        halo, old, push, new, rows, cols, geo, coef, row_sum, col_sum = refs
    else:
        halo, pull, old, push, new, own, rows, cols, geo, coef, row_sum, col_sum = refs
    for r in range(3):
        for c in range(4):
            rest, disp = halo[r, c, 0:3], halo[r, c, 3:6]
            alive = halo[r, c, 9:10]
            if not first:
                speed = halo[r, c, 6:9] + 0.2 * (pull[r, 4 * c : 4 * c + 3] * alive)
                disp = disp + 0.2 * speed
                if r == 1 and c in (1, 2):
                    own[c - 1, 0:3] = disp
                    own[c - 1, 3:6] = speed
            t = r * 4 + c
            rows[t, 0:3] = rest
            rows[t, 3:6] = rest + disp
            rows[t, 6:7] = jnp.where(alive > 0.5, 1.0, DEAD)
            rows[t, 7:8] = alive
    for h in range(2):
        cols[h] = jnp.transpose(rows[5 + h])
    col_sum[...] = jnp.zeros_like(col_sum)

    for h in range(2):

        def measure(i, carry, h=h):
            at = pl.ds(pl.multiple_of(i * CHUNK, CHUNK), CHUNK)
            home = [jnp.broadcast_to(cols[h, at, j : j + 1], (CHUNK, LANES)) for j in range(6)]
            here = cols[h, at, 7:8]
            volume = jnp.zeros((CHUNK, LANES), jnp.float32)
            swell = jnp.zeros((CHUNK, LANES), jnp.float32)
            for k, (dr, dc) in enumerate(OFFSETS):
                t = (1 + dr) * 4 + 1 + h + dc
                bond = [rows[t, j : j + 1] - home[j] for j in range(3)]
                length = root(bond[0] * bond[0] + bond[1] * bond[1] + bond[2] * bond[2])
                close = jnp.maximum(rows[t, 6:7] - length, 0.0)
                weight = close * close
                gap = [rows[t, 3 + j : 4 + j] - home[3 + j] for j in range(3)]
                squared = gap[0] * gap[0] + gap[1] * gap[1] + gap[2] * gap[2]
                stretch = root(squared) - length
                lever = weight * length
                volume = volume + lever * length
                swell = swell + lever * stretch
                geo[0, h * 9 + k, at] = length
                geo[1, h * 9 + k, at] = weight
                geo[2, h * 9 + k, at] = stretch
                geo[3, h * 9 + k, at] = lax.rsqrt(squared + 0.01)
            mass = jnp.maximum(here * jnp.sum(volume, axis=1, keepdims=True), 1.0)
            dilatation = 3.0 * (here * jnp.sum(swell, axis=1, keepdims=True)) / mass
            share = here / mass
            coef[3 * h, at] = jnp.broadcast_to(dilatation / 3.0, (CHUNK, LANES))
            coef[3 * h + 1, at] = jnp.broadcast_to(3.0 * dilatation * share, (CHUNK, LANES))
            coef[3 * h + 2, at] = jnp.broadcast_to(7.5 * share, (CHUNK, LANES))
            return carry

        lax.fori_loop(0, LANES // CHUNK, measure, 0)

    for h in range(2):

        def push_pull(i, carry, h=h):
            at = pl.ds(pl.multiple_of(i * CHUNK, CHUNK), CHUNK)
            home = [jnp.broadcast_to(cols[h, at, j : j + 1], (CHUNK, LANES)) for j in range(3, 6)]
            third, bulk, shear = coef[3 * h, at], coef[3 * h + 1, at], coef[3 * h + 2, at]
            total = [jnp.zeros((CHUNK, LANES), jnp.float32) for _ in range(3)]
            for k, (dr, dc) in enumerate(OFFSETS):
                t = (1 + dr) * 4 + 1 + h + dc
                length = geo[0, h * 9 + k, at]
                deviator = geo[2, h * 9 + k, at] - third * length
                one = old[0, 0, h, k, at].astype(jnp.float32)
                two = old[1, 0, h, k, at].astype(jnp.float32)
                new[0, 0, h, k, at] = (0.6 * one + 0.4 * deviator).astype(jnp.bfloat16)
                new[1, 0, h, k, at] = (0.95 * two + 0.05 * deviator).astype(jnp.bfloat16)
                mixed = 0.8475 * deviator - 0.21 * one - 0.2375 * two
                force = geo[1, h * 9 + k, at] * (length * bulk + shear * mixed)
                force = force * geo[3, h * 9 + k, at]
                for j in range(3):
                    part = force * (rows[t, 3 + j : 4 + j] - home[j])
                    total[j] = total[j] + part
                    col_sum[3 * t + j] += part[0:8] + part[8:16]
            for j in range(3):
                row_sum[3 * h + j, at] = total[j]
            return carry

        lax.fori_loop(0, LANES // CHUNK, push_pull, 0)

    ones = jnp.ones((8, LANES), jnp.float32)
    for r in range(3):
        for c in range(4):
            t = r * 4 + c
            for j in range(3):
                value = -jnp.sum(col_sum[3 * t + j], axis=0, keepdims=True)
                if r == 1 and c in (1, 2):
                    sums = lax.dot_general(
                        ones,
                        row_sum[3 * (c - 1) + j],
                        (((1,), (1,)), ((), ())),
                        precision=lax.Precision.HIGHEST,
                        preferred_element_type=jnp.float32,
                    )
                    value = value + sums[0:1]
                push[r, 4 * c + j : 4 * c + j + 1] = value
            push[r, 4 * c + 3 : 4 * c + 4] = jnp.zeros((1, LANES), jnp.float32)


def run_step(first, operands, history):
    f32 = jnp.float32
    outs = [jax.ShapeDtypeStruct((3, 16, LANES), f32), jax.ShapeDtypeStruct(history.shape, history.dtype)]
    if not first:
        outs.append(jax.ShapeDtypeStruct((2, 6, LANES), f32))
    vmem = pl.BlockSpec(memory_space=pltpu.VMEM)
    return pl.pallas_call(
        functools.partial(step_kernel, first),
        out_shape=outs,
        in_specs=[vmem] * (len(operands) + 1),
        out_specs=[vmem] * len(outs),
        scratch_shapes=[
            pltpu.VMEM((12, 8, LANES), f32),
            pltpu.VMEM((2, LANES, 8), f32),
            pltpu.VMEM((4, 18, LANES, LANES), f32),
            pltpu.VMEM((6, LANES, LANES), f32),
            pltpu.VMEM((6, LANES, LANES), f32),
            pltpu.VMEM((36, 8, LANES), f32),
        ],
        compiler_params=pltpu.CompilerParams(vmem_limit_bytes=24 * 1024 * 1024),
        name="step_one" if first else "step_two",
    )(*operands, history)


def swap_pairs(size, parity):
    pairs = []
    for i in range(size):
        pairs.append((i, (i + 1) % size if i % 2 == parity else (i - 1) % size))
    return pairs


def per_device(slabs, columns, rest_points, tile_fill, displacement, velocity, back_extension):
    s, c = lax.axis_index("slab"), lax.axis_index("col")
    s_odd, c_odd = s % 2 == 1, c % 2 == 1
    slab_near, slab_far = swap_pairs(slabs, 0), swap_pairs(slabs, 1)
    col_near, col_far = swap_pairs(columns, 0), swap_pairs(columns, 1)

    alive = (jnp.arange(LANES, dtype=jnp.int32)[None, None, :] < tile_fill[0][:, None, None]).astype(jnp.float32)
    own = jnp.concatenate(
        [jnp.swapaxes(a[:, 0], 0, 1) for a in (rest_points, displacement, velocity)]
        + [alive, jnp.zeros((2, 6, LANES), jnp.float32)],
        axis=1,
    )
    near = lax.ppermute(own, "slab", slab_near)
    far = lax.ppermute(own, "slab", slab_far)
    before = jnp.where(s > 0, jnp.where(s_odd, near, far), 0.0)
    after = jnp.where(s < slabs - 1, jnp.where(s_odd, far, near), 0.0)
    tiles = jnp.stack([before, own, after])
    near = lax.ppermute(jnp.where(c_odd, tiles[:, 0], tiles[:, 1]), "col", col_near)
    far = lax.ppermute(jnp.where(c_odd, tiles[:, 1], tiles[:, 0]), "col", col_far)
    left = jnp.where(c > 0, jnp.where(c_odd, near, far), 0.0)
    right = jnp.where(c < columns - 1, jnp.where(c_odd, far, near), 0.0)
    halo = jnp.stack([left, tiles[:, 0], tiles[:, 1], right], 1)

    def across(sums):
        half_l, half_r = sums[..., :8, :], sums[..., 8:, :]
        near = lax.ppermute(jnp.where(c_odd, half_l, half_r), "col", col_near)
        far = lax.ppermute(jnp.where(c_odd, half_r, half_l), "col", col_far)
        half_l = half_l + jnp.where(c_odd, near, far)
        half_r = half_r + jnp.where(c_odd, far, near)
        return jnp.concatenate([half_l, half_r], axis=-2)

    push, history = run_step(True, (halo,), back_extension)
    got = lax.ppermute(jnp.where(s_odd, push[0], push[2]), "slab", slab_near)
    two = jnp.where(s_odd, jnp.stack([push[1] + got, push[2]]), jnp.stack([push[0], push[1] + got]))
    two = two + lax.ppermute(two, "slab", slab_far)
    got = lax.ppermute(jnp.where(s_odd, two[0], two[1]), "slab", slab_near)
    three = jnp.where(s_odd, jnp.stack([got, two[0], two[1]]), jnp.stack([two[0], two[1], got]))
    pull = across(three)

    push, history, state = run_step(False, (halo, pull), history)
    near = lax.ppermute(jnp.where(s_odd, push[0], push[2]), "slab", slab_near)
    far = lax.ppermute(jnp.where(s_odd, push[2], push[0]), "slab", slab_far)
    total = across(push[1] + near + far)
    total = jnp.stack([total[4:7], total[8:11]], axis=1)
    state = jnp.swapaxes(state, 0, 1)
    velocity = state[3:6] + 0.2 * total
    displacement = state[0:3] + 0.2 * velocity
    return (displacement[:, None], velocity[:, None], history)


def solution(mesh):
    in_specs = (
        P(None, "slab", "col", None),
        P("slab", "col"),
        P(None, "slab", "col", None),
        P(None, "slab", "col", None),
        P(None, "slab", "col", None, None, None),
    )
    out_specs = (
        P(None, "slab", "col", None),
        P(None, "slab", "col", None),
        P(None, "slab", "col", None, None, None),
    )
    return jax.shard_map(
        functools.partial(per_device, mesh.shape["slab"], mesh.shape["col"]),
        mesh=mesh,
        in_specs=in_specs,
        out_specs=out_specs,
        check_vma=False,
    )
```

time: 353 us -> 67.6 us (0.19)
  waiting for transfers between devices: 138 us -> 18.4 us
  other arithmetic: 67.4 us -> 0.85 us
  local copies, waits for them, and re-layouts: 69.3 us -> 3.95 us
  starting transfers between devices: 70.9 us -> 26.6 us
  Pallas kernels: 0 us -> 15.8 us
  between operations: 4.74 us -> 0.71 us
    ppermute x20 -> x13, waiting for transfers between devices: 138 us -> 18.4 us  [the longest x2 4.14 us: across(): far = lax.ppermute(jnp.where(c_odd, half_r, half_l), 'col', col_far)]
    ppermute x20 -> x13, starting transfers between devices: 70.9 us -> 26.6 us  [the longest x2 10.5 us: across(): far = lax.ppermute(jnp.where(c_odd, half_r, half_l), 'col', col_far)]
    mul x20 -> x0, other arithmetic: 21.2 us -> none  [the longest x12 16.3 us: per_device(): (forces[index] + reverse)[None] * shapes[index][1]]
    pallas_call x0 -> x2, Pallas kernels: none -> 15.8 us  [run_step(): pl.pallas_call(functools.partial(step_kernel, first), out_shape=outs, in_...]
    add x11 -> x4, other arithmetic: 15.6 us -> 0.02 us  [the longest x2 0.01 us: across(): half_l = half_l + jnp.where(c_odd, near, far)]
    add x16 -> x0, local copies, waits for them, and re-layouts: 14.5 us -> none  [the longest x14 12.8 us: per_device(): bond_force + 7.5 * weight / volume[..., None] * (0.4 * deviator + 0.35 *...]
    mul x15 -> x0, local copies, waits for them, and re-layouts: 14.4 us -> none  [the longest x3 4.37 us: per_device(): 3.0 * dilatation[..., None] * weight * length / volume[..., None]]
    reduce_sum x10 -> x0, other arithmetic: 12.7 us -> none  [the longest x4 7.29 us: per_device(): jnp.sum(weight * length * shapes[index][0], axis=-1)]
  transfers between devices with their start and end apart: 20 -> 13, of which waited for: 10 -> 8; matrix products, arithmetic and copies ran while one was open for 16% -> 0% of each run, Pallas kernels for 0% -> 0%
where the time goes in v1:
time: 67.6 us; the launch traced here: 66.4 us
  starting transfers between devices  26.6 us (39%)
  waiting for transfers between devices  18.4 us (27%)
  Pallas kernels  15.8 us (23%)
  local copies, waits for them, and re-layouts  3.95 us (6%)
  other arithmetic  0.85 us (1%)
  between operations  0.71 us (1%)
    pallas_call x2, Pallas kernels, run_step(): pl.pallas_call(functools.partial(step_kernel, first), out_shape=outs, in_...  15.8 us
    ppermute x2, starting transfers between devices, across(): far = lax.ppermute(jnp.where(c_odd, half_r, half_l), 'col', col_far)  10.5 us
    ppermute x1, starting transfers between devices, per_device(): lax.ppermute(jnp.where(c_odd, tiles[:, 1], tiles[:, 0]), 'col', col_far)  4.88 us
    ppermute x2, waiting for transfers between devices, across(): far = lax.ppermute(jnp.where(c_odd, half_r, half_l), 'col', col_far)  4.14 us
    ppermute x1, waiting for transfers between devices, per_device(): two = two + lax.ppermute(two, 'slab', slab_far)  3.38 us
    ppermute x1, waiting for transfers between devices, per_device(): far = lax.ppermute(jnp.where(s_odd, push[2], push[0]), 'slab', slab_far)  3.16 us
    unnamed x5, local copies, waits for them, and re-layouts  3.11 us
    ppermute x1, waiting for transfers between devices, per_device(): far = lax.ppermute(own, 'slab', slab_far)  2.84 us
  transfers between devices with their start and end apart: 13, of which 8 were waited for; matrix products, arithmetic and copies ran while one was open for 0% of the time, Pallas kernels for 0%

profile of v1, /device:TPU:2, one launch (start us, length us, event | category | flops | bytes accessed | tf_op | source)
XLA Modules:
  0.0 66.4 jit_solution(1709499698559549936)
XLA Ops:
  0.6 0.7 %compare_convert_fusion = f32[2,1,128]{2,1,0:T(1,128)S(1)} fusion(s32[2]{0:T(128)} %bitcast.74), kind=kLoop, calls=%fused_computation.35 | loop fusion | flops 512 | bytes 1032 | tf_op jit(solution)/shard_map/convert_element_type | solution.py:162
  1.4 0.7 %copy.21 = f32[3,1,2,128]{3,0,2,1:T(4,128)S(1)} copy(f32[3,1,2,128]{3,2,1,0:T(2,128)} %param.5) | data formatting | bytes 6144 | tf_op args[0]
  2.0 0.7 %copy_bitcast_fusion = (f32[2,3,128]{2,1,0:T(4,128)S(1)}, f32[2,3,128]{2,1,0:T(4,128)S(1)}) fusion(f32[3,1,2,128]{3,2,1,0:T(2,128)} %param.8, f32[3,1,2,128]{3,2,1,0:T(2,128)} %param.7), kind=kLoop, calls=%fused_computation.30 | loop fusion | bytes 12288 | tf_op jit(solution)/shard_map/transpose | solution.py:164
  2.9 2.5 %collective-permute-start.1 = (f32[2,16,128]{2,1,0:T(8,128)S(1)}, f32[2,16,128]{2,1,0:T(8,128)S(1)}, u32[]{:S(2)}, u32[]{:S(2)}) collective-permute-start(f32[2,16,128]{2,1,0:T(8,128)S(1)} %concatenate.6), channel_id=1, source_target_pairs={{0,120},{8,16},{16,8},{24,32},{32,24},{40,48},{48,40},{56,64},{64,... | collective-permute-start | bytes 49160 | tf_op jit(solution)/shard_map/ppermute | solution.py:169
  5.4 2.8 %collective-permute-done.1 = f32[2,16,128]{2,1,0:T(8,128)S(1)} collective-permute-done((f32[2,16,128]{2,1,0:T(8,128)S(1)}, f32[2,16,128]{2,1,0:T(8,128)S(1)}, u32[]{:S(2)}, u32[]{:S(2)}) %collective-permute-start.1) | collective-permute-done | bytes 16416 | tf_op jit(solution)/shard_map/ppermute | solution.py:169
  8.3 2.2 %collective-permute-start.2 = (f32[3,16,128]{2,1,0:T(8,128)S(1)}, f32[3,16,128]{2,1,0:T(8,128)S(1)}, u32[]{:S(2)}, u32[]{:S(2)}) collective-permute-start(f32[3,16,128]{2,1,0:T(8,128)S(1)} %get-tuple-element.20), channel_id=1, source_target_pairs={{0,1},{1,0},{2,3},{3,2},{4,5},{5,4},{6,7},{7,6},{8,9},{9,8},{10,11... | collective-permute-start | bytes 73736 | tf_op jit(solution)/shard_map/ppermute | solution.py:173
  10.5 4.9 %collective-permute-start.3 = (f32[3,16,128]{2,1,0:T(8,128)S(1)}, f32[3,16,128]{2,1,0:T(8,128)S(1)}, u32[]{:S(2)}, u32[]{:S(2)}) collective-permute-start(f32[3,16,128]{2,1,0:T(8,128)S(1)} %get-tuple-element.21), channel_id=1, source_target_pairs={{0,7},{1,2},{2,1},{3,4},{4,3},{5,6},{6,5},{7,0},{8,15},{9,10},{10,... | collective-permute-start | bytes 73736 | tf_op jit(solution)/shard_map/ppermute | solution.py:174
  15.3 2.6 %collective-permute-done.3 = f32[3,16,128]{2,1,0:T(8,128)S(1)} collective-permute-done((f32[3,16,128]{2,1,0:T(8,128)S(1)}, f32[3,16,128]{2,1,0:T(8,128)S(1)}, u32[]{:S(2)}, u32[]{:S(2)}) %collective-permute-start.3) | collective-permute-done | bytes 24608 | tf_op jit(solution)/shard_map/ppermute | solution.py:174
  17.9 1.3 %copy-done = bf16[2,1,2,9,128,128]{5,4,3,2,1,0:T(8,128)(2,1)S(1)} copy-done((bf16[2,1,2,9,128,128]{5,4,3,2,1,0:T(8,128)(2,1)S(1)}, bf16[2,1,2,9,128,128]{5,4,3,2,1,0:T(8,128)(2,1)}, u32[]{:S(2)}) %copy-start) | copy-done | bytes 1179672
  19.2 7.8 %step_one.1 = (f32[3,16,128]{2,1,0:T(8,128)S(1)}, bf16[2,1,2,9,128,128]{5,4,3,2,1,0:T(8,128)(2,1)S(1)}) custom-call(f32[3,4,16,128]{3,2,1,0:T(8,128)S(1)} %pad_maximum_fusion.refs_0_, bf16[2,1,2,9,128,128]{5,4,3,2,1,0:T(8,128)(2,1)S(1)} %copy-done), custom_call_target="tpu_custom_call" | custom-call | tf_op jit(solution)/shard_map/step_one/pallas_call | solution.py:131
  27.1 1.2 %collective-permute-done.4 = f32[16,128]{1,0:T(8,128)S(1)} collective-permute-done((f32[16,128]{1,0:T(8,128)S(1)}, f32[16,128]{1,0:T(8,128)S(1)}, u32[]{:S(2)}, u32[]{:S(2)}) %collective-permute-start.4) | collective-permute-done | bytes 8224 | tf_op jit(solution)/shard_map/ppermute | solution.py:188
  28.2 2.0 %collective-permute-start.5 = (f32[2,16,128]{2,1,0:T(8,128)S(1)}, f32[2,16,128]{2,1,0:T(8,128)S(1)}, u32[]{:S(2)}, u32[]{:S(2)}) collective-permute-start(f32[2,16,128]{2,1,0:T(8,128)S(1)} %maximum_select_fusion.1), channel_id=1, source_target_pairs={{0,120},{8,16},{16,8},{24,32},{32,24},{40,48},{48,40},{56,64},{64,... | collective-permute-start | bytes 49160 | tf_op jit(solution)/shard_map/ppermute | solution.py:190
  30.2 3.4 %collective-permute-done.5 = f32[2,16,128]{2,1,0:T(8,128)S(1)} collective-permute-done((f32[2,16,128]{2,1,0:T(8,128)S(1)}, f32[2,16,128]{2,1,0:T(8,128)S(1)}, u32[]{:S(2)}, u32[]{:S(2)}) %collective-permute-start.5) | collective-permute-done | bytes 16416 | tf_op jit(solution)/shard_map/ppermute | solution.py:190
  33.7 1.2 %collective-permute-done.6 = f32[16,128]{1,0:T(8,128)S(1)} collective-permute-done((f32[16,128]{1,0:T(8,128)S(1)}, f32[16,128]{1,0:T(8,128)S(1)}, u32[]{:S(2)}, u32[]{:S(2)}) %collective-permute-start.6) | collective-permute-done | bytes 8224 | tf_op jit(solution)/shard_map/ppermute | solution.py:191
  35.1 5.6 %collective-permute-start.8 = (f32[3,8,128]{2,1,0:T(8,128)S(1)}, f32[3,8,128]{2,1,0:T(8,128)S(1)}, u32[]{:S(2)}, u32[]{:S(2)}) collective-permute-start(f32[3,8,128]{2,1,0:T(8,128)S(1)} %get-tuple-element.27), channel_id=1, source_target_pairs={{0,7},{1,2},{2,1},{3,4},{4,3},{5,6},{6,5},{7,0},{8,15},{9,10},{10,... | collective-permute-start | bytes 36872 | tf_op jit(solution)/shard_map/ppermute | solution.py:182
  40.7 1.8 %collective-permute-done.8 = f32[3,8,128]{2,1,0:T(8,128)S(1)} collective-permute-done((f32[3,8,128]{2,1,0:T(8,128)S(1)}, f32[3,8,128]{2,1,0:T(8,128)S(1)}, u32[]{:S(2)}, u32[]{:S(2)}) %collective-permute-start.8) | collective-permute-done | bytes 12320 | tf_op jit(solution)/shard_map/ppermute | solution.py:182
  42.6 8.0 %step_two.1 = (f32[3,16,128]{2,1,0:T(8,128)S(1)}, bf16[2,1,2,9,128,128]{5,4,3,2,1,0:T(8,128)(2,1)}, f32[2,6,128]{2,1,0:T(8,128)S(1)}) custom-call(f32[3,4,16,128]{3,2,1,0:T(8,128)S(1)} %pad_maximum_fusion.refs_0_, f32[3,16,128]{2,1,0:T(8,128)S(1)} %pad_maximum_fusion.2.refs_1_, bf16[2,1,2,9,128,128]{5,4,3,2,1,0:T(8,128)(2,1)S(1)} %get-tuple-element.9.refs_2_), custom_call_target="tpu_custom_call" | custom-call | tf_op jit(solution)/shard_map/step_two/pallas_call | solution.py:131
  50.6 2.1 %collective-permute-start.10 = (f32[16,128]{1,0:T(8,128)S(1)}, f32[16,128]{1,0:T(8,128)S(1)}, u32[]{:S(2)}, u32[]{:S(2)}) collective-permute-start(f32[16,128]{1,0:T(8,128)S(1)} %get-tuple-element.25), channel_id=1, source_target_pairs={{0,120},{8,16},{16,8},{24,32},{32,24},{40,48},{48,40},{56,64},{64,... | collective-permute-start | bytes 24584 | tf_op jit(solution)/shard_map/ppermute | solution.py:197
  52.7 3.2 %collective-permute-done.10 = f32[16,128]{1,0:T(8,128)S(1)} collective-permute-done((f32[16,128]{1,0:T(8,128)S(1)}, f32[16,128]{1,0:T(8,128)S(1)}, u32[]{:S(2)}, u32[]{:S(2)}) %collective-permute-start.10) | collective-permute-done | bytes 8224 | tf_op jit(solution)/shard_map/ppermute | solution.py:197
  55.8 2.1 %collective-permute-start.11 = (f32[8,128]{1,0:T(8,128)S(1)}, f32[8,128]{1,0:T(8,128)S(1)}, u32[]{:S(2)}, u32[]{:S(2)}) collective-permute-start(f32[8,128]{1,0:T(8,128)S(1)} %get-tuple-element.35), channel_id=1, source_target_pairs={{0,1},{1,0},{2,3},{3,2},{4,5},{5,4},{6,7},{7,6},{8,9},{9,8},{10,11... | collective-permute-start | bytes 12296 | tf_op jit(solution)/shard_map/ppermute | solution.py:181
  58.0 4.9 %collective-permute-start.12 = (f32[8,128]{1,0:T(8,128)S(1)}, f32[8,128]{1,0:T(8,128)S(1)}, u32[]{:S(2)}, u32[]{:S(2)}) collective-permute-start(f32[8,128]{1,0:T(8,128)S(1)} %get-tuple-element.36), channel_id=1, source_target_pairs={{0,7},{1,2},{2,1},{3,4},{4,3},{5,6},{6,5},{7,0},{8,15},{9,10},{10,... | collective-permute-start | bytes 12296 | tf_op jit(solution)/shard_map/ppermute | solution.py:182
  62.8 2.3 %collective-permute-done.12 = f32[8,128]{1,0:T(8,128)S(1)} collective-permute-done((f32[8,128]{1,0:T(8,128)S(1)}, f32[8,128]{1,0:T(8,128)S(1)}, u32[]{:S(2)}, u32[]{:S(2)}) %collective-permute-start.12) | collective-permute-done | bytes 4128 | tf_op jit(solution)/shard_map/ppermute | solution.py:182
  65.2 0.6 copy.15
  65.8 0.6 copy.14
  (34 shorter events, 0.7 us)
Async XLA Ops:
  2.9 5.3 %collective-permute-start.1 = (f32[2,16,128]{2,1,0:T(8,128)S(1)}, f32[2,16,128]{2,1,0:T(8,128)S(1)}, u32[]{:S(2)}, u32[]{:S(2)}) collective-permute-start(f32[2,16,128]{2,1,0:T(8,128)S(1)} %concatenate.6), channel_id=1, source_target_pairs={{0,120},{8,16},{16,8},{24,32},{32,24},{40,48},{48,40},{56,64},{64,... | collective-permute-start | bytes 49160 | tf_op jit(solution)/shard_map/ppermute | solution.py:169
  5.4 2.9 %collective-permute-start = (f32[2,16,128]{2,1,0:T(8,128)S(1)}, f32[2,16,128]{2,1,0:T(8,128)S(1)}, u32[]{:S(2)}, u32[]{:S(2)}) collective-permute-start(f32[2,16,128]{2,1,0:T(8,128)S(1)} %concatenate.6), channel_id=1, source_target_pairs={{0,8},{8,0},{16,24},{24,16},{32,40},{40,32},{48,56},{56,48},{64,72... | collective-permute-start | bytes 49160 | tf_op jit(solution)/shard_map/ppermute | solution.py:168
  8.3 7.1 %collective-permute-start.2 = (f32[3,16,128]{2,1,0:T(8,128)S(1)}, f32[3,16,128]{2,1,0:T(8,128)S(1)}, u32[]{:S(2)}, u32[]{:S(2)}) collective-permute-start(f32[3,16,128]{2,1,0:T(8,128)S(1)} %get-tuple-element.20), channel_id=1, source_target_pairs={{0,1},{1,0},{2,3},{3,2},{4,5},{5,4},{6,7},{7,6},{8,9},{9,8},{10,11... | collective-permute-start | bytes 73736 | tf_op jit(solution)/shard_map/ppermute | solution.py:173
  10.5 7.4 %collective-permute-start.3 = (f32[3,16,128]{2,1,0:T(8,128)S(1)}, f32[3,16,128]{2,1,0:T(8,128)S(1)}, u32[]{:S(2)}, u32[]{:S(2)}) collective-permute-start(f32[3,16,128]{2,1,0:T(8,128)S(1)} %get-tuple-element.21), channel_id=1, source_target_pairs={{0,7},{1,2},{2,1},{3,4},{4,3},{5,6},{6,5},{7,0},{8,15},{9,10},{10,... | collective-permute-start | bytes 73736 | tf_op jit(solution)/shard_map/ppermute | solution.py:174
  17.9 1.3 %copy-start = (bf16[2,1,2,9,128,128]{5,4,3,2,1,0:T(8,128)(2,1)S(1)}, bf16[2,1,2,9,128,128]{5,4,3,2,1,0:T(8,128)(2,1)}, u32[]{:S(2)}) copy-start(bf16[2,1,2,9,128,128]{5,4,3,2,1,0:T(8,128)(2,1)} %refs_1_.1) | copy-start | bytes 3538948
  27.0 1.2 %collective-permute-start.4 = (f32[16,128]{1,0:T(8,128)S(1)}, f32[16,128]{1,0:T(8,128)S(1)}, u32[]{:S(2)}, u32[]{:S(2)}) collective-permute-start(f32[16,128]{1,0:T(8,128)S(1)} %get-tuple-element.29), channel_id=1, source_target_pairs={{0,8},{8,0},{16,24},{24,16},{32,40},{40,32},{48,56},{56,48},{64,72... | collective-permute-start | bytes 24584 | tf_op jit(solution)/shard_map/ppermute | solution.py:188
  28.2 5.4 %collective-permute-start.5 = (f32[2,16,128]{2,1,0:T(8,128)S(1)}, f32[2,16,128]{2,1,0:T(8,128)S(1)}, u32[]{:S(2)}, u32[]{:S(2)}) collective-permute-start(f32[2,16,128]{2,1,0:T(8,128)S(1)} %maximum_select_fusion.1), channel_id=1, source_target_pairs={{0,120},{8,16},{16,8},{24,32},{32,24},{40,48},{48,40},{56,64},{64,... | collective-permute-start | bytes 49160 | tf_op jit(solution)/shard_map/ppermute | solution.py:190
  33.6 1.2 %collective-permute-start.6 = (f32[16,128]{1,0:T(8,128)S(1)}, f32[16,128]{1,0:T(8,128)S(1)}, u32[]{:S(2)}, u32[]{:S(2)}) collective-permute-start(f32[16,128]{1,0:T(8,128)S(1)} %fusion), channel_id=1, source_target_pairs={{0,8},{8,0},{16,24},{24,16},{32,40},{40,32},{48,56},{56,48},{64,72... | collective-permute-start | bytes 24584 | tf_op jit(solution)/shard_map/ppermute | solution.py:191
  34.9 5.9 %collective-permute-start.7 = (f32[3,8,128]{2,1,0:T(8,128)S(1)}, f32[3,8,128]{2,1,0:T(8,128)S(1)}, u32[]{:S(2)}, u32[]{:S(2)}) collective-permute-start(f32[3,8,128]{2,1,0:T(8,128)S(1)} %get-tuple-element.26), channel_id=1, source_target_pairs={{0,1},{1,0},{2,3},{3,2},{4,5},{5,4},{6,7},{7,6},{8,9},{9,8},{10,11... | collective-permute-start | bytes 36872 | tf_op jit(solution)/shard_map/ppermute | solution.py:181
  35.1 7.4 %collective-permute-start.8 = (f32[3,8,128]{2,1,0:T(8,128)S(1)}, f32[3,8,128]{2,1,0:T(8,128)S(1)}, u32[]{:S(2)}, u32[]{:S(2)}) collective-permute-start(f32[3,8,128]{2,1,0:T(8,128)S(1)} %get-tuple-element.27), channel_id=1, source_target_pairs={{0,7},{1,2},{2,1},{3,4},{4,3},{5,6},{6,5},{7,0},{8,15},{9,10},{10,... | collective-permute-start | bytes 36872 | tf_op jit(solution)/shard_map/ppermute | solution.py:182
  50.6 2.1 %collective-permute-start.9 = (f32[16,128]{1,0:T(8,128)S(1)}, f32[16,128]{1,0:T(8,128)S(1)}, u32[]{:S(2)}, u32[]{:S(2)}) collective-permute-start(f32[16,128]{1,0:T(8,128)S(1)} %get-tuple-element.24), channel_id=1, source_target_pairs={{0,8},{8,0},{16,24},{24,16},{32,40},{40,32},{48,56},{56,48},{64,72... | collective-permute-start | bytes 24584 | tf_op jit(solution)/shard_map/ppermute | solution.py:196
  50.6 5.2 %collective-permute-start.10 = (f32[16,128]{1,0:T(8,128)S(1)}, f32[16,128]{1,0:T(8,128)S(1)}, u32[]{:S(2)}, u32[]{:S(2)}) collective-permute-start(f32[16,128]{1,0:T(8,128)S(1)} %get-tuple-element.25), channel_id=1, source_target_pairs={{0,120},{8,16},{16,8},{24,32},{32,24},{40,48},{48,40},{56,64},{64,... | collective-permute-start | bytes 24584 | tf_op jit(solution)/shard_map/ppermute | solution.py:197
  55.8 7.0 %collective-permute-start.11 = (f32[8,128]{1,0:T(8,128)S(1)}, f32[8,128]{1,0:T(8,128)S(1)}, u32[]{:S(2)}, u32[]{:S(2)}) collective-permute-start(f32[8,128]{1,0:T(8,128)S(1)} %get-tuple-element.35), channel_id=1, source_target_pairs={{0,1},{1,0},{2,3},{3,2},{4,5},{5,4},{6,7},{7,6},{8,9},{9,8},{10,11... | collective-permute-start | bytes 12296 | tf_op jit(solution)/shard_map/ppermute | solution.py:181
  58.0 7.2 %collective-permute-start.12 = (f32[8,128]{1,0:T(8,128)S(1)}, f32[8,128]{1,0:T(8,128)S(1)}, u32[]{:S(2)}, u32[]{:S(2)}) collective-permute-start(f32[8,128]{1,0:T(8,128)S(1)} %get-tuple-element.36), channel_id=1, source_target_pairs={{0,7},{1,2},{2,1},{3,4},{4,3},{5,6},{6,5},{7,0},{8,15},{9,10},{10,... | collective-permute-start | bytes 12296 | tf_op jit(solution)/shard_map/ppermute | solution.py:182

commit v2 on v0

v2 whole, which is shorter than its diff:
```python
import functools

import jax
import jax.numpy as jnp
from jax import lax
from jax.experimental import pallas as pl
from jax.experimental.pallas import tpu as pltpu
from jax.sharding import PartitionSpec as P

OFFSETS = [(-1, -1), (-1, 0), (-1, 1), (0, -1), (0, 0), (0, 1), (1, -1), (1, 0), (1, 1)]
N = 128
CHUNK = 16
F32 = jnp.float32
VMEM = pl.BlockSpec(memory_space=pltpu.VMEM)
PAIRS = [(h, k) for h in range(2) for k in range(9)]
INNER = [(h, k) for h, k in PAIRS if 0 <= h + OFFSETS[k][1] <= 1]
OUTER = [(h, k) for h, k in PAIRS if not 0 <= h + OFFSETS[k][1] <= 1]


def root(squared):
    return squared * lax.rsqrt(jnp.maximum(squared, 1e-36))


def block(*shape):
    return jax.ShapeDtypeStruct(shape, F32)


def call(body, name, outs, operands, scratch=(), specs=None, work=0, limit=24):
    cost = pl.CostEstimate(flops=work, bytes_accessed=1 << 16, transcendentals=0) if work else None
    return pl.pallas_call(
        body,
        out_shape=outs,
        in_specs=specs or [VMEM] * len(operands),
        out_specs=[VMEM] * len(outs),
        scratch_shapes=list(scratch),
        compiler_params=pltpu.CompilerParams(vmem_limit_bytes=limit and limit * 1024 * 1024),
        cost_estimate=cost,
        name=name,
    )(*operands)


def each_chunk(body, unroll=1):
    def step(i, carry):
        body(pl.ds(pl.multiple_of(i * CHUNK, CHUNK), CHUNK))
        return carry

    lax.fori_loop(0, N // CHUNK, step, 0, unroll=unroll)


def across(ref, at, j):
    return jnp.broadcast_to(ref[at, j : j + 1], (CHUNK, N))


def pack_body(fill_far, rest_far, displacement_far, velocity_far, own, state, fill, rest, displacement, velocity, sems):
    pairs = ((fill_far, fill), (rest_far, rest), (displacement_far, displacement), (velocity_far, velocity))
    copies = [pltpu.make_async_copy(a, b, sems.at[i]) for i, (a, b) in enumerate(pairs)]
    for copy in copies:
        copy.start()
    for copy in copies:
        copy.wait()
    lane = lax.broadcasted_iota(jnp.int32, (1, N), 1)
    for t in range(2):
        for j in range(3):
            spot, shift = rest[j, 0, t : t + 1], displacement[j, 0, t : t + 1]
            speed = velocity[j, 0, t : t + 1]
            own[t, j : j + 1] = spot
            own[t, 3 + j : 4 + j] = spot + shift
            state[t, j : j + 1] = shift + 0.2 * speed
            state[t, 3 + j : 4 + j] = speed
        own[t, 6:7] = jnp.where(lane < fill[0, t], 1.0, 0.0)
        own[t, 7:8] = jnp.ones((1, N), F32)
        state[t, 6:8] = jnp.zeros((2, N), F32)


def recall_body(far, held, mixed, sems):
    copies = {}
    for h in range(2):
        for j in range(2):
            copies[j, h] = pltpu.make_async_copy(far.at[j, 0, h], held.at[j, 0, h], sems.at[j, h])
            copies[j, h].start()
    for h in range(2):
        copies[0, h].wait()
        copies[1, h].wait()

        def body(at, h=h):
            for k in range(9):
                one, two = held[0, 0, h, k, at].astype(F32), held[1, 0, h, k, at].astype(F32)
                mixed[9 * h + k, at] = 0.21 * one + 0.2375 * two

        each_chunk(body)


def measure(at, blocks, target, home, mixed, volume, swell, length_, lever_, weight_, pull_, rest_, stretch_):
    for n, (h, k) in enumerate(blocks):
        t = target(h, k)
        bond = [t[j : j + 1] - home[h][j] for j in range(3)]
        length = root(bond[0] * bond[0] + bond[1] * bond[1] + bond[2] * bond[2])
        close = jnp.maximum(t[6:7] - length, 0.0)
        weight = close * close
        gap = [t[3 + j : 4 + j] - home[h][3 + j] for j in range(3)]
        squared = gap[0] * gap[0] + gap[1] * gap[1] + gap[2] * gap[2]
        stretch = root(squared) - length
        lever = weight * length
        volume[h] = volume[h] + lever * length
        swell[h] = swell[h] + lever * stretch
        length_[n, at] = length
        lever_[n, at] = lever
        weight_[n, at] = weight
        pull_[n, at] = weight * lax.rsqrt(squared + 0.01)
        rest_[n, at] = 0.8475 * stretch - mixed[9 * h + k, at]
        stretch_[n, at] = stretch


def inner_body(tiles, mixed, cols, volume_, swell_, *geo):
    for h in range(2):
        cols[h] = jnp.transpose(tiles[1, h])

    def target(h, k):
        return tiles.at[1 + OFFSETS[k][0], h + OFFSETS[k][1]]

    def body(at):
        home = [[across(cols.at[h], at, j) for j in range(6)] for h in range(2)]
        volume = [jnp.zeros((CHUNK, N), F32)] * 2
        swell = [jnp.zeros((CHUNK, N), F32)] * 2
        measure(at, INNER, target, home, mixed, volume, swell, *geo)
        for h in range(2):
            volume_[h, at] = volume[h]
            swell_[h, at] = swell[h]

    each_chunk(body)


def side(left, right, r, h):
    return right.at[r] if h else left.at[r]


def force_sums(pulls, gaps, push, row_sum, col_sum, base):
    lane = lax.broadcasted_iota(jnp.int32, (N, N), 1)
    table = jnp.zeros((N, N), F32)
    for q in range(6):
        table = jnp.where(lane == q, jnp.sum(row_sum[q], axis=1, keepdims=True), table)
    table = jnp.transpose(table)
    for r in range(3):
        for c in range(4):
            for j in range(3):
                value = -jnp.sum(col_sum[12 * r + 3 * c + j], axis=0, keepdims=True)
                if r == 1 and c in (1, 2):
                    q = 3 * (c - 1) + j
                    value = value + table[q : q + 1]
                if base is not None:
                    value = 0.04 * value
                    if r == 1 and c in (1, 2):
                        value = value + base[c - 1, j : j + 1]
                push[r, 4 * c + j : 4 * c + j + 1] = value
            push[r, 4 * c + 3 : 4 * c + 4] = jnp.zeros((1, N), F32)


def add_force(at, h, k, force, gap, total, col_sum):
    t = (1 + OFFSETS[k][0]) * 4 + 1 + h + OFFSETS[k][1]
    for j in range(3):
        part = force * gap[j]
        total[h][j] = total[h][j] + part
        col_sum[3 * t + j] += part[0:8] + part[8:16]


def first_body(tiles, left, right, mixed, state, cols, volume_, swell_, *refs):
    inner, (push, third_, shear_), refs = refs[:6], refs[6:9], refs[9:]
    outer, (vol, swl, bulk, row_sum, col_sum) = refs[:6], refs[6:]

    def measure_outer(at):
        home = [[across(cols.at[h], at, j) for j in range(6)] for h in range(2)]
        volume = [volume_[h, at] for h in range(2)]
        swell = [swell_[h, at] for h in range(2)]
        measure(
            at, OUTER, lambda h, k: side(left, right, 1 + OFFSETS[k][0], h), home, mixed, volume, swell, *outer
        )
        for h in range(2):
            vol[h, at] = volume[h]
            swl[h, at] = swell[h]

    each_chunk(measure_outer)
    for h in range(2):
        here = cols[h, :, 6:7]
        mass = jnp.maximum(here * jnp.sum(vol[h], axis=1, keepdims=True), 1.0)
        dilatation = 3.0 * (here * jnp.sum(swl[h], axis=1, keepdims=True)) / mass
        shear = 7.5 * here / mass
        third_[h] = jnp.broadcast_to(dilatation / 3.0, (N, N))
        shear_[h] = jnp.broadcast_to(shear, (N, N))
        bulk[h] = jnp.broadcast_to(0.1175 * dilatation * shear, (N, N))
    col_sum[...] = jnp.zeros_like(col_sum)

    def forces(at):
        total = [[jnp.zeros((CHUNK, N), F32)] * 3 for _ in range(2)]
        for h in range(2):
            home = [across(cols.at[h], at, 3 + j) for j in range(3)]
            flat, tall = shear_[h, at], bulk[h, at]
            for k, (dr, dc) in enumerate(OFFSETS):
                if (h, k) in INNER:
                    geo, n, t = inner, INNER.index((h, k)), tiles.at[1 + dr, h + dc]
                else:
                    geo, n, t = outer, OUTER.index((h, k)), side(left, right, 1 + dr, h)
                force = geo[3][n, at] * (geo[0][n, at] * tall + geo[4][n, at] * flat)
                gap = [t[3 + j : 4 + j] - home[j] for j in range(3)]
                add_force(at, h, k, force, gap, total, col_sum)
            for j in range(3):
                row_sum[3 * h + j, at] = total[h][j]

    each_chunk(forces)
    force_sums(None, None, push, row_sum, col_sum, state)


def relax_body(held, third, shear, len_i, len_o, wgt_i, wgt_o, str_i, str_o, new, mixed, firm):
    def body(at):
        for h in range(2):
            lean, flat = third[h, at], shear[h, at]
            for k in range(9):
                if (h, k) in INNER:
                    n, length, weight, stretch = INNER.index((h, k)), len_i, wgt_i, str_i
                else:
                    n, length, weight, stretch = OUTER.index((h, k)), len_o, wgt_o, str_o
                deviator = stretch[n, at] - lean * length[n, at]
                one = (0.6 * held[0, 0, h, k, at].astype(F32) + 0.4 * deviator).astype(jnp.bfloat16)
                two = (0.95 * held[1, 0, h, k, at].astype(F32) + 0.05 * deviator).astype(jnp.bfloat16)
                new[0, 0, h, k, at] = one
                new[1, 0, h, k, at] = two
                mixed[9 * h + k, at] = 0.21 * one.astype(F32) + 0.2375 * two.astype(F32)
                firm[9 * h + k, at] = weight[n, at] * flat

    each_chunk(body)


def second_body(tiles, left, right, pull, state, shear_, mixed, firm, len_i, len_o, lev_i, lev_o, *refs):
    push, third_, stretch_, own, rows, cols, swl, bulk, kernel_, rest_, row_sum, col_sum = refs
    for r in range(3):
        for c in range(4):
            t = tiles.at[r, c - 1] if c in (1, 2) else (right if c else left).at[r]
            shift = pull[r, 4 * c : 4 * c + 3] * t[7:8]
            rows[4 * r + c, 0:3] = t[0:3] + shift
            rows[4 * r + c, 3:8] = jnp.zeros((5, N), F32)
            if r == 1 and c in (1, 2):
                own[c - 1, 0:3] = shift
                own[c - 1, 3:6] = state[c - 1, 3:6] + 5.0 * (shift - state[c - 1, 0:3])
                own[c - 1, 6:8] = jnp.zeros((2, N), F32)
    for h in range(2):
        cols[h] = jnp.transpose(rows[5 + h])

    def lengths(h, k):
        if (h, k) in INNER:
            return INNER.index((h, k)), len_i, lev_i
        return OUTER.index((h, k)), len_o, lev_o

    def stretches(at):
        for h in range(2):
            home = [across(cols.at[h], at, j) for j in range(3)]
            swell = jnp.zeros((CHUNK, N), F32)
            for k, (dr, dc) in enumerate(OFFSETS):
                n, length, lever = lengths(h, k)
                t, m = (1 + dr) * 4 + 1 + h + dc, 9 * h + k
                gap = [rows[t, j : j + 1] - home[j] for j in range(3)]
                squared = gap[0] * gap[0] + gap[1] * gap[1] + gap[2] * gap[2]
                stretch = root(squared) - length[n, at]
                swell = swell + lever[n, at] * stretch
                stretch_[m, at] = stretch
                kernel_[m, at] = firm[m, at] * lax.rsqrt(squared + 0.01)
                rest_[m, at] = 0.8475 * stretch - mixed[m, at]
            swl[h, at] = swell

    each_chunk(stretches)
    for h in range(2):
        dilatation = 0.4 * shear_[h] * jnp.sum(swl[h], axis=1, keepdims=True)
        third_[h] = dilatation / 3.0
        bulk[h] = 0.1175 * dilatation
    col_sum[...] = jnp.zeros_like(col_sum)

    def forces(at):
        total = [[jnp.zeros((CHUNK, N), F32)] * 3 for _ in range(2)]
        for h in range(2):
            home = [across(cols.at[h], at, j) for j in range(3)]
            tall = bulk[h, at]
            for k, (dr, dc) in enumerate(OFFSETS):
                n, length, _ = lengths(h, k)
                t, m = (1 + dr) * 4 + 1 + h + dc, 9 * h + k
                force = kernel_[m, at] * (length[n, at] * tall + rest_[m, at])
                gap = [rows[t, j : j + 1] - home[j] for j in range(3)]
                add_force(at, h, k, force, gap, total, col_sum)
            for j in range(3):
                row_sum[3 * h + j, at] = total[h][j]

    each_chunk(forces)
    force_sums(None, None, push, row_sum, col_sum, None)


def settle_body(held, third, len_i, len_o, stretch, new):
    def body(at):
        for h in range(2):
            lean = third[h, at]
            for k in range(9):
                length = len_i[INNER.index((h, k)), at] if (h, k) in INNER else len_o[OUTER.index((h, k)), at]
                deviator = stretch[9 * h + k, at] - lean * length
                one, two = held[0, 0, h, k, at].astype(F32), held[1, 0, h, k, at].astype(F32)
                new[0, 0, h, k, at] = (0.6 * one + 0.4 * deviator).astype(jnp.bfloat16)
                new[1, 0, h, k, at] = (0.95 * two + 0.05 * deviator).astype(jnp.bfloat16)

    each_chunk(body)


def finish_body(total, own, displacement, velocity):
    for t in range(2):
        for j in range(3):
            q = 4 * (t + 1) + j
            speed = own[t, 3 + j : 4 + j] + 0.2 * total[q : q + 1]
            velocity[j, 0, t : t + 1] = speed
            displacement[j, 0, t : t + 1] = own[t, j : j + 1] + 0.2 * speed


def swap_pairs(size, parity):
    return [(i, (i + 1) % size if i % 2 == parity else (i - 1) % size) for i in range(size)]


def inner_swaps(slabs, columns):
    pairs = []
    for s in range(slabs):
        for c in range(columns):
            if c in (0, columns - 1):
                pairs.append((s * columns + c, (s ^ 1) * columns + c))
            else:
                pairs.append((s * columns + c, s * columns + (c + 1 if c % 2 else c - 1)))
    return pairs


def per_device(slabs, columns, rest_points, tile_fill, displacement, velocity, back_extension):
    s, c = lax.axis_index("slab"), lax.axis_index("col")
    s_odd, c_odd = s % 2 == 1, c % 2 == 1
    slab_near, slab_far = swap_pairs(slabs, 0), swap_pairs(slabs, 1)
    col_near, col_far = swap_pairs(columns, 0), inner_swaps(slabs, columns)

    def over_slab(to_near, to_far):
        return lax.ppermute(to_near, "slab", slab_near), lax.ppermute(to_far, "slab", slab_far)

    def over_col(to_left, to_right):
        near = lax.ppermute(jnp.where(c_odd, to_left, to_right), "col", col_near)
        far = lax.ppermute(jnp.where(c_odd, to_right, to_left), ("slab", "col"), col_far)
        from_left = jnp.where(c > 0, jnp.where(c_odd, near, far), 0.0)
        from_right = jnp.where(c < columns - 1, jnp.where(c_odd, far, near), 0.0)
        return from_left, from_right

    history = jax.ShapeDtypeStruct(back_extension.shape, back_extension.dtype)
    hbm = pl.BlockSpec(memory_space=pl.ANY)
    own, state = call(
        pack_body,
        "pack",
        [block(2, 8, N), block(2, 8, N)],
        (tile_fill, rest_points, displacement, velocity),
        scratch=[pltpu.SMEM(tile_fill.shape, jnp.int32)]
        + [pltpu.VMEM(rest_points.shape, F32)] * 3
        + [pltpu.SemaphoreType.DMA((4,))],
        specs=[hbm] * 4,
        limit=None,
    )
    near, far = over_slab(own, own)
    held, mixed = call(
        recall_body,
        "recall",
        [history, block(18, N, N)],
        (back_extension,),
        scratch=[pltpu.SemaphoreType.DMA((2, 2))],
        specs=[hbm],
        work=2_000_000,
    )
    near, far, held, mixed = lax.optimization_barrier((near, far, held, mixed))
    before = jnp.where(s > 0, jnp.where(s_odd, near, far), 0.0)
    after = jnp.where(s < slabs - 1, jnp.where(s_odd, far, near), 0.0)
    tiles = jnp.stack([before, own, after])
    left, right = over_col(tiles[:, 0], tiles[:, 1])
    cols, volume, swell, *inner = call(
        inner_body,
        "inner",
        [block(2, N, 8)] + [block(2, N, N)] * 2 + [block(12, N, N)] * 6,
        (tiles, mixed),
        work=6_000_000,
    )
    sums = [pltpu.VMEM((6, N, N), F32), pltpu.VMEM((36, 8, N), F32)]
    push, third, shear, *outer = call(
        first_body,
        "first",
        [block(3, 16, N), block(2, N, N), block(2, N, N)] + [block(6, N, N)] * 6,
        (tiles, left, right, mixed, state, cols, volume, swell, *inner),
        scratch=[pltpu.VMEM((2, N, N), F32)] * 3 + sums,
        work=8_000_000,
    )
    got = lax.ppermute(jnp.where(s_odd, push[0], push[2]), "slab", slab_near)
    two = jnp.where(s_odd, jnp.stack([push[1] + got, push[2]]), jnp.stack([push[0], push[1] + got]))
    back = lax.ppermute(two, "slab", slab_far)
    held, mixed, firm = call(
        relax_body,
        "relax",
        [history, block(18, N, N), block(18, N, N)],
        (held, third, shear, inner[0], outer[0], inner[2], outer[2], inner[5], outer[5]),
        work=4_000_000,
    )
    back, held, mixed, firm = lax.optimization_barrier((back, held, mixed, firm))
    two = two + back
    got = lax.ppermute(jnp.where(s_odd, two[0], two[1]), "slab", slab_near)
    three = jnp.where(s_odd, jnp.stack([got, two[0], two[1]]), jnp.stack([two[0], two[1], got]))
    lo, hi = three[:, :8], three[:, 8:]
    left_sum, right_sum = over_col(lo, hi)
    pull = jnp.concatenate([lo + left_sum, hi + right_sum], axis=1)

    push, third, stretch, own = call(
        second_body,
        "second",
        [block(3, 16, N), block(2, N, N), block(18, N, N), block(2, 8, N)],
        (tiles, left, right, pull, state, shear, mixed, firm, inner[0], outer[0], inner[1], outer[1]),
        scratch=[pltpu.VMEM((12, 8, N), F32), pltpu.VMEM((2, N, 8), F32)]
        + [pltpu.VMEM((2, N, N), F32)] * 2
        + [pltpu.VMEM((18, N, N), F32)] * 2
        + sums,
        work=8_000_000,
    )
    (held,) = call(settle_body, "settle", [history], (held, third, inner[0], outer[0], stretch), work=3_000_000)
    near, far = over_slab(jnp.where(s_odd, push[0], push[2]), jnp.where(s_odd, push[2], push[0]))
    total = push[1] + near + far
    lo, hi = total[:8], total[8:]
    left_sum, right_sum = over_col(lo, hi)
    total = jnp.concatenate([lo + left_sum, hi + right_sum], axis=0)
    shape = block(*rest_points.shape)
    displacement, velocity = call(finish_body, "finish", [shape, shape], (total, own))
    return (displacement, velocity, held)


def solution(mesh):
    in_specs = (
        P(None, "slab", "col", None),
        P("slab", "col"),
        P(None, "slab", "col", None),
        P(None, "slab", "col", None),
        P(None, "slab", "col", None, None, None),
    )
    out_specs = (
        P(None, "slab", "col", None),
        P(None, "slab", "col", None),
        P(None, "slab", "col", None, None, None),
    )
    return jax.shard_map(
        functools.partial(per_device, mesh.shape["slab"], mesh.shape["col"]),
        mesh=mesh,
        in_specs=in_specs,
        out_specs=out_specs,
        check_vma=False,
    )
```

time: 353 us -> 51.6 us (0.15)
  the two profiles are of different devices: /device:TPU:2 before, /device:TPU:38 now
where the time goes in v2:
time: 51.6 us; the launch traced here: 51.4 us
  waiting for transfers between devices  18.9 us (37%)
  starting transfers between devices  17.7 us (34%)
  Pallas kernels  12.7 us (25%)
  local copies, waits for them, and re-layouts  1.28 us (2%)
  between operations  0.74 us (1%)
    pallas_call x8, Pallas kernels, call(): pl.pallas_call(body, out_shape=outs, in_specs=specs or [VMEM] * len(opera...  12.7 us
    ppermute x3, starting transfers between devices, over_col(): lax.ppermute(jnp.where(c_odd, to_right, to_left), ('slab', 'col'), col_far)  8.79 us
    ppermute x3, waiting for transfers between devices, over_col(): lax.ppermute(jnp.where(c_odd, to_right, to_left), ('slab', 'col'), col_far)  5.32 us
    ppermute x2, waiting for transfers between devices, over_slab(): lax.ppermute(to_far, 'slab', slab_far)  4.66 us
    ppermute x2, starting transfers between devices, over_slab(): lax.ppermute(to_far, 'slab', slab_far)  4.24 us
    ppermute x1, waiting for transfers between devices, per_device(): back = lax.ppermute(two, 'slab', slab_far)  4.16 us
    ppermute x3, starting transfers between devices, over_col(): near = lax.ppermute(jnp.where(c_odd, to_left, to_right), 'col', col_near)  4 us
    ppermute x3, waiting for transfers between devices, over_col(): near = lax.ppermute(jnp.where(c_odd, to_left, to_right), 'col', col_near)  2.47 us
  transfers between devices with their start and end apart: 13, of which 10 were waited for; matrix products, arithmetic and copies ran while one was open for 0% of the time, Pallas kernels for 9%

profile of v2, /device:TPU:38, one launch (start us, length us, event | category | flops | bytes accessed | tf_op | source)
XLA Modules:
  0.0 51.4 jit_solution(5720179881892674548)
XLA Ops:
  0.6 1.4 %pack.1 = (f32[2,8,128]{2,1,0:T(8,128)}, f32[2,8,128]{2,1,0:T(8,128)}) custom-call(s32[1,2]{1,0:T(1,128)} %fill_far.1, f32[3,1,2,128]{3,2,1,0:T(2,128)} %rest_far.1, f32[3,1,2,128]{3,2,1,0:T(2,128)} %displacement_far.1, f32[3,1,2,128]{3,2,1,0:T(2,128)} %velocity_far.1), custom_call_target="tpu_custom_call" | custom-call | tf_op jit(solution)/shard_map/pack/pallas_call | solution.py:30
  2.0 2.8 %collective-permute-start.1 = (f32[2,8,128]{2,1,0:T(8,128)}, f32[2,8,128]{2,1,0:T(8,128)S(1)}, u32[]{:S(2)}, u32[]{:S(2)}) collective-permute-start(f32[2,8,128]{2,1,0:T(8,128)} %get-tuple-element.40), channel_id=1, source_target_pairs={{0,120},{8,16},{16,8},{24,32},{32,24},{40,48},{48,40},{56,64},{64,... | collective-permute-start | bytes 24584 | tf_op jit(solution)/shard_map/ppermute | solution.py:338
  4.8 1.3 %copy-done = bf16[2,1,2,9,128,128]{5,4,3,2,1,0:T(8,128)(2,1)S(1)} copy-done((bf16[2,1,2,9,128,128]{5,4,3,2,1,0:T(8,128)(2,1)S(1)}, bf16[2,1,2,9,128,128]{5,4,3,2,1,0:T(8,128)(2,1)}, u32[]{:S(2)}) %copy-start) | copy-done | bytes 1179672
  6.6 0.8 %collective-permute-done.1 = f32[2,8,128]{2,1,0:T(8,128)S(1)} collective-permute-done((f32[2,8,128]{2,1,0:T(8,128)}, f32[2,8,128]{2,1,0:T(8,128)S(1)}, u32[]{:S(2)}, u32[]{:S(2)}) %collective-permute-start.1) | collective-permute-done | bytes 8224 | tf_op jit(solution)/shard_map/ppermute | solution.py:338
  7.5 2.8 %collective-permute-start.3 = (f32[3,8,128]{2,1,0:T(8,128)S(1)}, f32[3,8,128]{2,1,0:T(8,128)S(1)}, u32[]{:S(2)}, u32[]{:S(2)}) collective-permute-start(f32[3,8,128]{2,1,0:T(8,128)S(1)} %get-tuple-element.88), channel_id=1, source_target_pairs={{0,8},{1,2},{2,1},{3,4},{4,3},{5,6},{6,5},{7,15},{8,0},{9,10},{10,... | collective-permute-start | bytes 36872 | tf_op jit(solution)/shard_map/ppermute | solution.py:342
  10.7 1.7 %inner.1 = (f32[2,128,8]{2,1,0:T(8,128)S(1)}, f32[2,128,128]{2,1,0:T(8,128)S(1)}, f32[2,128,128]{2,1,0:T(8,128)S(1)}, f32[12,128,128]{2,1,0:T(8,128)S(1)}, f32[1...) custom-call(f32[3,2,8,128]{3,2,1,0:T(8,128)S(1)} %copy.11.tiles, ...), custom_call_target="tpu_custom_call" | custom-call | flops 6000000 | bytes 65536 | tf_op jit(solution)/shard_map/inner/pallas_call | solution.py:30
  12.5 1.3 %collective-permute-done.3 = f32[3,8,128]{2,1,0:T(8,128)S(1)} collective-permute-done((f32[3,8,128]{2,1,0:T(8,128)S(1)}, f32[3,8,128]{2,1,0:T(8,128)S(1)}, u32[]{:S(2)}, u32[]{:S(2)}) %collective-permute-start.3) | collective-permute-done | bytes 12320 | tf_op jit(solution)/shard_map/ppermute | solution.py:342
  13.7 1.9 %collective-permute-done.2 = f32[3,8,128]{2,1,0:T(8,128)S(1)} collective-permute-done((f32[3,8,128]{2,1,0:T(8,128)S(1)}, f32[3,8,128]{2,1,0:T(8,128)S(1)}, u32[]{:S(2)}, u32[]{:S(2)}) %collective-permute-start.2) | collective-permute-done | bytes 12320 | tf_op jit(solution)/shard_map/ppermute | solution.py:341
  15.6 3.3 %first.1 = (f32[3,16,128]{2,1,0:T(8,128)S(1)}, f32[2,128,128]{2,1,0:T(8,128)S(1)}, f32[2,128,128]{2,1,0:T(8,128)S(1)}, f32[6,128,128]{2,1,0:T(8,128)S(1)}, f32[6...) custom-call(f32[3,2,8,128]{3,2,1,0:T(8,128)S(1)} %copy.11.tiles, ...), custom_call_target="tpu_custom_call" | custom-call | flops 8000000 | bytes 65536 | tf_op jit(solution)/shard_map/first/pallas_call | solution.py:30
  18.9 1.2 %collective-permute-done.4 = f32[16,128]{1,0:T(8,128)S(1)} collective-permute-done((f32[16,128]{1,0:T(8,128)S(1)}, f32[16,128]{1,0:T(8,128)S(1)}, u32[]{:S(2)}, u32[]{:S(2)}) %collective-permute-start.4) | collective-permute-done | bytes 8224 | tf_op jit(solution)/shard_map/ppermute | solution.py:391
  20.6 0.7 %relax.1 = (bf16[2,1,2,9,128,128]{5,4,3,2,1,0:T(8,128)(2,1)S(1)}, f32[18,128,128]{2,1,0:T(8,128)S(1)}, f32[18,128,128]{2,1,0:T(8,128)S(1)}) custom-call(bf16[2,1,2,9,128,128]{5,4,3,2,1,0:T(8,128)(2,1)S(1)} %get-tuple-element.57.held, f32[2,128,128]{2,1,0:T(8,128)S(1)} %get-tuple-element.58.third, f32[2,128,128]{2,1,0:T(8,128)S(1)} %get-tuple-element.59.shear.shear_, ...), custom_call_target="tpu_custom_call" | custom-call | flops 4000000 | bytes 65536 | tf_op jit(solution)/shard_map/relax/pallas_call | solution.py:30
  21.3 4.2 %collective-permute-done.5 = f32[2,16,128]{2,1,0:T(8,128)S(1)} collective-permute-done((f32[2,16,128]{2,1,0:T(8,128)S(1)}, f32[2,16,128]{2,1,0:T(8,128)S(1)}, u32[]{:S(2)}, u32[]{:S(2)}) %collective-permute-start.5) | collective-permute-done | bytes 16416 | tf_op jit(solution)/shard_map/ppermute | solution.py:393
  25.6 1.2 %collective-permute-done.6 = f32[16,128]{1,0:T(8,128)S(1)} collective-permute-done((f32[16,128]{1,0:T(8,128)S(1)}, f32[16,128]{1,0:T(8,128)S(1)}, u32[]{:S(2)}, u32[]{:S(2)}) %collective-permute-start.6) | collective-permute-done | bytes 8224 | tf_op jit(solution)/shard_map/ppermute | solution.py:403
  27.1 4.3 %collective-permute-start.8 = (f32[3,8,128]{2,1,0:T(8,128)S(1)}, f32[3,8,128]{2,1,0:T(8,128)S(1)}, u32[]{:S(2)}, u32[]{:S(2)}) collective-permute-start(f32[3,8,128]{2,1,0:T(8,128)S(1)} %get-tuple-element.82), channel_id=1, source_target_pairs={{0,8},{1,2},{2,1},{3,4},{4,3},{5,6},{6,5},{7,15},{8,0},{9,10},{10,... | collective-permute-start | bytes 36872 | tf_op jit(solution)/shard_map/ppermute | solution.py:342
  31.4 0.6 %collective-permute-done.7 = f32[3,8,128]{2,1,0:T(8,128)S(1)} collective-permute-done((f32[3,8,128]{2,1,0:T(8,128)S(1)}, f32[3,8,128]{2,1,0:T(8,128)S(1)}, u32[]{:S(2)}, u32[]{:S(2)}) %collective-permute-start.7) | collective-permute-done | bytes 12320 | tf_op jit(solution)/shard_map/ppermute | solution.py:341
  32.0 1.2 %collective-permute-done.8 = f32[3,8,128]{2,1,0:T(8,128)S(1)} collective-permute-done((f32[3,8,128]{2,1,0:T(8,128)S(1)}, f32[3,8,128]{2,1,0:T(8,128)S(1)}, u32[]{:S(2)}, u32[]{:S(2)}) %collective-permute-start.8) | collective-permute-done | bytes 12320 | tf_op jit(solution)/shard_map/ppermute | solution.py:342
  33.3 2.9 %second.1 = (f32[3,16,128]{2,1,0:T(8,128)S(1)}, f32[2,128,128]{2,1,0:T(8,128)S(1)}, f32[18,128,128]{2,1,0:T(8,128)S(1)}, f32[2,8,128]{2,1,0:T(8,128)S(1)}) custom-call(f32[3,2,8,128]{3,2,1,0:T(8,128)S(1)} %copy.11.tiles, f32[3,8,128]{2,1,0:T(8,128)S(1)} %get-tuple-element.87.left, f32[3,8,128]{2,1,0:T(8,128)S(1)} %get-tuple-element.86.right, ...), custom_call_target="tpu_custom_call" | custom-call | flops 8000000 | bytes 65536 | tf_op jit(solution)/shard_map/second/pallas_call | solution.py:30
  36.3 1.4 %collective-permute-start.10 = (f32[16,128]{1,0:T(8,128)S(1)}, f32[16,128]{1,0:T(8,128)S(1)}, u32[]{:S(2)}, u32[]{:S(2)}) collective-permute-start(f32[16,128]{1,0:T(8,128)S(1)} %get-tuple-element.80), channel_id=1, source_target_pairs={{0,120},{8,16},{16,8},{24,32},{32,24},{40,48},{48,40},{56,64},{64,... | collective-permute-start | bytes 24584 | tf_op jit(solution)/shard_map/ppermute | solution.py:338
  37.7 3.8 %collective-permute-done.10 = f32[16,128]{1,0:T(8,128)S(1)} collective-permute-done((f32[16,128]{1,0:T(8,128)S(1)}, f32[16,128]{1,0:T(8,128)S(1)}, u32[]{:S(2)}, u32[]{:S(2)}) %collective-permute-start.10) | collective-permute-done | bytes 8224 | tf_op jit(solution)/shard_map/ppermute | solution.py:338
  41.5 3.3 %collective-permute-start.11 = (f32[8,128]{1,0:T(8,128)S(1)}, f32[8,128]{1,0:T(8,128)S(1)}, u32[]{:S(2)}, u32[]{:S(2)}) collective-permute-start(f32[8,128]{1,0:T(8,128)S(1)} %get-tuple-element.94), channel_id=1, source_target_pairs={{0,1},{1,0},{2,3},{3,2},{4,5},{5,4},{6,7},{7,6},{8,9},{9,8},{10,11... | collective-permute-start | bytes 12296 | tf_op jit(solution)/shard_map/ppermute | solution.py:341
  44.8 1.7 %collective-permute-start.12 = (f32[8,128]{1,0:T(8,128)S(1)}, f32[8,128]{1,0:T(8,128)S(1)}, u32[]{:S(2)}, u32[]{:S(2)}) collective-permute-start(f32[8,128]{1,0:T(8,128)S(1)} %get-tuple-element.95), channel_id=1, source_target_pairs={{0,8},{1,2},{2,1},{3,4},{4,3},{5,6},{6,5},{7,15},{8,0},{9,10},{10,... | collective-permute-start | bytes 12296 | tf_op jit(solution)/shard_map/ppermute | solution.py:342
  46.5 1.5 %settle.1 = bf16[2,1,2,9,128,128]{5,4,3,2,1,0:T(8,128)(2,1)} custom-call(bf16[2,1,2,9,128,128]{5,4,3,2,1,0:T(8,128)(2,1)S(1)} %get-tuple-element.74.held, f32[2,128,128]{2,1,0:T(8,128)S(1)} %get-tuple-element.75.third, f32[12,128,128]{2,1,0:T(8,128)S(1)} %get-tuple-element.50.refs_0_.len_i, f32[6,128,128]{2,1,0:T(8,128)S(1)} %get-tuple-element.60.len_o, ...), custom_call_target="tpu_custom_call" | custom-call | flops 3000000 | bytes 65536 | tf_op jit(solution)/shard_map/settle/pallas_call | solution.py:30
  48.0 2.8 %collective-permute-done.12 = f32[8,128]{1,0:T(8,128)S(1)} collective-permute-done((f32[8,128]{1,0:T(8,128)S(1)}, f32[8,128]{1,0:T(8,128)S(1)}, u32[]{:S(2)}, u32[]{:S(2)}) %collective-permute-start.12) | collective-permute-done | bytes 4128 | tf_op jit(solution)/shard_map/ppermute | solution.py:342
  50.9 0.6 %finish.1 = (f32[3,1,2,128]{3,2,1,0:T(2,128)}, f32[3,1,2,128]{3,2,1,0:T(2,128)}) custom-call(f32[16,128]{1,0:T(8,128)S(1)} %pad_maximum_fusion.2.total, f32[2,8,128]{2,1,0:T(8,128)S(1)} %get-tuple-element.71.own), custom_call_target="tpu_custom_call" | custom-call | tf_op jit(solution)/shard_map/finish/pallas_call | solution.py:30
  (35 shorter events, 2.0 us)
Async XLA Ops:
  2.0 5.5 %copy-start.2 = (f32[2,8,128]{2,1,0:T(8,128)S(1)}, f32[2,8,128]{2,1,0:T(8,128)}, u32[]{:S(2)}) copy-start(f32[2,8,128]{2,1,0:T(8,128)} %get-tuple-element.40) | copy-start | bytes 24580
  2.0 5.5 %collective-permute-start.1 = (f32[2,8,128]{2,1,0:T(8,128)}, f32[2,8,128]{2,1,0:T(8,128)S(1)}, u32[]{:S(2)}, u32[]{:S(2)}) collective-permute-start(f32[2,8,128]{2,1,0:T(8,128)} %get-tuple-element.40), channel_id=1, source_target_pairs={{0,120},{8,16},{16,8},{24,32},{32,24},{40,48},{48,40},{56,64},{64,... | collective-permute-start | bytes 24584 | tf_op jit(solution)/shard_map/ppermute | solution.py:338
  4.8 2.7 %collective-permute-start = (f32[2,8,128]{2,1,0:T(8,128)}, f32[2,8,128]{2,1,0:T(8,128)S(1)}, u32[]{:S(2)}, u32[]{:S(2)}) collective-permute-start(f32[2,8,128]{2,1,0:T(8,128)} %get-tuple-element.40), channel_id=1, source_target_pairs={{0,8},{8,0},{16,24},{24,16},{32,40},{40,32},{48,56},{56,48},{64,72... | collective-permute-start | bytes 24584 | tf_op jit(solution)/shard_map/ppermute | solution.py:338
  4.8 1.3 %copy-start = (bf16[2,1,2,9,128,128]{5,4,3,2,1,0:T(8,128)(2,1)S(1)}, bf16[2,1,2,9,128,128]{5,4,3,2,1,0:T(8,128)(2,1)}, u32[]{:S(2)}) copy-start(bf16[2,1,2,9,128,128]{5,4,3,2,1,0:T(8,128)(2,1)} %far.1) | copy-start | bytes 3538948
  6.1 9.5 %copy-start.1 = (f32[2,8,128]{2,1,0:T(8,128)S(1)}, f32[2,8,128]{2,1,0:T(8,128)}, u32[]{:S(2)}) copy-start(f32[2,8,128]{2,1,0:T(8,128)} %get-tuple-element.46.state) | copy-start | bytes 24580
  7.5 6.2 %collective-permute-start.3 = (f32[3,8,128]{2,1,0:T(8,128)S(1)}, f32[3,8,128]{2,1,0:T(8,128)S(1)}, u32[]{:S(2)}, u32[]{:S(2)}) collective-permute-start(f32[3,8,128]{2,1,0:T(8,128)S(1)} %get-tuple-element.88), channel_id=1, source_target_pairs={{0,8},{1,2},{2,1},{3,4},{4,3},{5,6},{6,5},{7,15},{8,0},{9,10},{10,... | collective-permute-start | bytes 36872 | tf_op jit(solution)/shard_map/ppermute | solution.py:342
  10.4 5.2 %collective-permute-start.2 = (f32[3,8,128]{2,1,0:T(8,128)S(1)}, f32[3,8,128]{2,1,0:T(8,128)S(1)}, u32[]{:S(2)}, u32[]{:S(2)}) collective-permute-start(f32[3,8,128]{2,1,0:T(8,128)S(1)} %get-tuple-element.89), channel_id=1, source_target_pairs={{0,1},{1,0},{2,3},{3,2},{4,5},{5,4},{6,7},{7,6},{8,9},{9,8},{10,11... | collective-permute-start | bytes 36872 | tf_op jit(solution)/shard_map/ppermute | solution.py:341
  18.9 1.2 %collective-permute-start.4 = (f32[16,128]{1,0:T(8,128)S(1)}, f32[16,128]{1,0:T(8,128)S(1)}, u32[]{:S(2)}, u32[]{:S(2)}) collective-permute-start(f32[16,128]{1,0:T(8,128)S(1)} %get-tuple-element.84), channel_id=1, source_target_pairs={{0,8},{8,0},{16,24},{24,16},{32,40},{40,32},{48,56},{56,48},{64,72... | collective-permute-start | bytes 24584 | tf_op jit(solution)/shard_map/ppermute | solution.py:391
  20.1 5.4 %collective-permute-start.5 = (f32[2,16,128]{2,1,0:T(8,128)S(1)}, f32[2,16,128]{2,1,0:T(8,128)S(1)}, u32[]{:S(2)}, u32[]{:S(2)}) collective-permute-start(f32[2,16,128]{2,1,0:T(8,128)S(1)} %maximum_select_fusion.1), channel_id=1, source_target_pairs={{0,120},{8,16},{16,8},{24,32},{32,24},{40,48},{48,40},{56,64},{64,... | collective-permute-start | bytes 49160 | tf_op jit(solution)/shard_map/ppermute | solution.py:393
  25.5 1.3 %collective-permute-start.6 = (f32[16,128]{1,0:T(8,128)S(1)}, f32[16,128]{1,0:T(8,128)S(1)}, u32[]{:S(2)}, u32[]{:S(2)}) collective-permute-start(f32[16,128]{1,0:T(8,128)S(1)} %fusion), channel_id=1, source_target_pairs={{0,8},{8,0},{16,24},{24,16},{32,40},{40,32},{48,56},{56,48},{64,72... | collective-permute-start | bytes 24584 | tf_op jit(solution)/shard_map/ppermute | solution.py:403
  26.7 5.3 %collective-permute-start.7 = (f32[3,8,128]{2,1,0:T(8,128)S(1)}, f32[3,8,128]{2,1,0:T(8,128)S(1)}, u32[]{:S(2)}, u32[]{:S(2)}) collective-permute-start(f32[3,8,128]{2,1,0:T(8,128)S(1)} %get-tuple-element.81), channel_id=1, source_target_pairs={{0,1},{1,0},{2,3},{3,2},{4,5},{5,4},{6,7},{7,6},{8,9},{9,8},{10,11... | collective-permute-start | bytes 36872 | tf_op jit(solution)/shard_map/ppermute | solution.py:341
  27.1 6.1 %collective-permute-start.8 = (f32[3,8,128]{2,1,0:T(8,128)S(1)}, f32[3,8,128]{2,1,0:T(8,128)S(1)}, u32[]{:S(2)}, u32[]{:S(2)}) collective-permute-start(f32[3,8,128]{2,1,0:T(8,128)S(1)} %get-tuple-element.82), channel_id=1, source_target_pairs={{0,8},{1,2},{2,1},{3,4},{4,3},{5,6},{6,5},{7,15},{8,0},{9,10},{10,... | collective-permute-start | bytes 36872 | tf_op jit(solution)/shard_map/ppermute | solution.py:342
  36.2 1.5 %collective-permute-start.9 = (f32[16,128]{1,0:T(8,128)S(1)}, f32[16,128]{1,0:T(8,128)S(1)}, u32[]{:S(2)}, u32[]{:S(2)}) collective-permute-start(f32[16,128]{1,0:T(8,128)S(1)} %get-tuple-element.79), channel_id=1, source_target_pairs={{0,8},{8,0},{16,24},{24,16},{32,40},{40,32},{48,56},{56,48},{64,72... | collective-permute-start | bytes 24584 | tf_op jit(solution)/shard_map/ppermute | solution.py:338
  36.3 5.3 %collective-permute-start.10 = (f32[16,128]{1,0:T(8,128)S(1)}, f32[16,128]{1,0:T(8,128)S(1)}, u32[]{:S(2)}, u32[]{:S(2)}) collective-permute-start(f32[16,128]{1,0:T(8,128)S(1)} %get-tuple-element.80), channel_id=1, source_target_pairs={{0,120},{8,16},{16,8},{24,32},{32,24},{40,48},{48,40},{56,64},{64,... | collective-permute-start | bytes 24584 | tf_op jit(solution)/shard_map/ppermute | solution.py:338
  41.5 6.5 %collective-permute-start.11 = (f32[8,128]{1,0:T(8,128)S(1)}, f32[8,128]{1,0:T(8,128)S(1)}, u32[]{:S(2)}, u32[]{:S(2)}) collective-permute-start(f32[8,128]{1,0:T(8,128)S(1)} %get-tuple-element.94), channel_id=1, source_target_pairs={{0,1},{1,0},{2,3},{3,2},{4,5},{5,4},{6,7},{7,6},{8,9},{9,8},{10,11... | collective-permute-start | bytes 12296 | tf_op jit(solution)/shard_map/ppermute | solution.py:341
  44.8 6.0 %collective-permute-start.12 = (f32[8,128]{1,0:T(8,128)S(1)}, f32[8,128]{1,0:T(8,128)S(1)}, u32[]{:S(2)}, u32[]{:S(2)}) collective-permute-start(f32[8,128]{1,0:T(8,128)S(1)} %get-tuple-element.95), channel_id=1, source_target_pairs={{0,8},{1,2},{2,1},{3,4},{4,3},{5,6},{6,5},{7,15},{8,0},{9,10},{10,... | collective-permute-start | bytes 12296 | tf_op jit(solution)/shard_map/ppermute | solution.py:342

commit v3 on v2

v3 whole, which is shorter than its diff:
```python
import functools

import jax
import jax.numpy as jnp
from jax import lax
from jax.experimental import pallas as pl
from jax.experimental.pallas import tpu as pltpu
from jax.sharding import PartitionSpec as P


N = 128
CHUNK = 16
F32 = jnp.float32
VMEM = pl.BlockSpec(memory_space=pltpu.VMEM)
BLOCKS = [(i, h, e) for i in range(3) for h in range(2) for e in range(3)]
INNER = [b for b in BLOCKS if 1 <= b[1] + b[2] <= 2]
OUTER = [b for b in BLOCKS if not 1 <= b[1] + b[2] <= 2]


def root(squared):
    return squared * lax.rsqrt(jnp.maximum(squared, 1e-36))


def block(*shape):
    return jax.ShapeDtypeStruct(shape, F32)


def call(body, outs, operands, scratch=(), specs=None, work=0, limit=24):
    cost = pl.CostEstimate(flops=work, bytes_accessed=1 << 16, transcendentals=0) if work else None
    return pl.pallas_call(
        body,
        out_shape=outs,
        in_specs=specs or [VMEM] * len(operands),
        out_specs=[VMEM] * len(outs),
        scratch_shapes=list(scratch),
        compiler_params=pltpu.CompilerParams(vmem_limit_bytes=limit and limit * 1024 * 1024),
        cost_estimate=cost,
    )(*operands)


def each_chunk(body):
    def step(i, carry):
        body(pl.ds(pl.multiple_of(i * CHUNK, CHUNK), CHUNK))
        return carry

    lax.fori_loop(0, N // CHUNK, step, 0)


def first_offset(i):
    odd = lax.axis_index("slab") % 2
    return (6 * (1 - odd), 3, 6 * odd)[i]


def spread(homes, h, tile, count):
    columns = jnp.transpose(tile)
    for j in range(count):
        homes[h, j] = jnp.broadcast_to(columns[:, j : j + 1], (N, N))


def either(inner, outer, i, h, e):
    if (i, h, e) in INNER:
        return inner, INNER.index((i, h, e))
    return outer, OUTER.index((i, h, e))


def tile_of(tiles, left, right, i, h, e):
    c = h + e
    return tiles.at[i, c - 1] if c in (1, 2) else (right if c else left).at[i]


def pack_body(fill_far, rest_far, displacement_far, velocity_far, own, state, fill, rest, displacement, velocity, sems):
    pairs = ((fill_far, fill), (rest_far, rest), (displacement_far, displacement), (velocity_far, velocity))
    copies = [pltpu.make_async_copy(a, b, sems.at[i]) for i, (a, b) in enumerate(pairs)]
    for copy in copies:
        copy.start()
    for copy in copies:
        copy.wait()
    lane = lax.broadcasted_iota(jnp.int32, (1, N), 1)
    state[...] = jnp.zeros_like(state)
    for t in range(2):
        for j in range(3):
            spot, shift = rest[j, 0, t : t + 1], displacement[j, 0, t : t + 1]
            speed = velocity[j, 0, t : t + 1]
            own[t, j : j + 1] = spot
            own[t, 3 + j : 4 + j] = spot + shift
            state[0, 4 * t + 4 + j : 4 * t + 5 + j] = shift + 0.2 * speed
            state[1, 4 * t + 4 + j : 4 * t + 5 + j] = speed
        own[t, 6:7] = jnp.where(lane < fill[0, t], 1.0, 0.0)
        own[t, 7:8] = jnp.ones((1, N), F32)


def recall_body(states, held, mixed):
    def body(at):
        for n, (i, h, e) in enumerate(BLOCKS):
            one, two = (states[j, 0, h, first_offset(i) + e, at] for j in range(2))
            held[0, h, i, e, at] = one
            held[1, h, i, e, at] = two
            mixed[n, at] = 0.21 * one.astype(F32) + 0.2375 * two.astype(F32)

    each_chunk(body)


def measure(at, blocks, target, home, mixed, volume, swell, length_, lever_, weight_, pull_, rest_, stretch_):
    for n, (i, h, e) in enumerate(blocks):
        t = target(i, h, e)
        bond = [t[j : j + 1] - home[h][j] for j in range(3)]
        length = root(bond[0] * bond[0] + bond[1] * bond[1] + bond[2] * bond[2])
        close = jnp.maximum(t[6:7] - length, 0.0)
        weight = close * close
        gap = [t[3 + j : 4 + j] - home[h][3 + j] for j in range(3)]
        squared = gap[0] * gap[0] + gap[1] * gap[1] + gap[2] * gap[2]
        stretch = root(squared) - length
        lever = weight * length
        volume[h] = volume[h] + lever * length
        swell[h] = swell[h] + lever * stretch
        length_[n, at] = length
        lever_[n, at] = lever
        weight_[n, at] = weight
        pull_[n, at] = weight * lax.rsqrt(squared + 0.01)
        rest_[n, at] = 0.8475 * stretch - mixed[BLOCKS.index((i, h, e)), at]
        stretch_[n, at] = stretch


def inner_body(tiles, mixed, homes, volume_, swell_, *geo):
    for h in range(2):
        spread(homes, h, tiles[1, h], 7)

    def body(at):
        home = [[homes[h, j, at] for j in range(6)] for h in range(2)]
        volume = [jnp.zeros((CHUNK, N), F32)] * 2
        swell = [jnp.zeros((CHUNK, N), F32)] * 2
        measure(at, INNER, lambda i, h, e: tiles.at[i, h + e - 1], home, mixed, volume, swell, *geo)
        for h in range(2):
            volume_[h, at] = volume[h]
            swell_[h, at] = swell[h]

    each_chunk(body)


def press(which, force_of, place, homes, first_home, row_in, row_out, col_sum):
    col_sum[...] = jnp.zeros_like(col_sum)

    def body(at):
        for h in range(2):
            home = [homes[h, first_home + j, at] for j in range(3)]
            total = [jnp.zeros((CHUNK, N), F32) if row_in is None else row_in[3 * h + j, at] for j in range(3)]
            force = force_of(h, at)
            for n, i in enumerate(which):
                for e in range(3):
                    strength = force(i, e)
                    for j in range(3):
                        part = strength * (place(i, h, e, j) - home[j])
                        total[j] = total[j] + part
                        q = 128 * n + 32 * (h + e) + 8 * j
                        col_sum[q : q + 8] += part[0:8] + part[8:16]
            for j in range(3):
                row_out[3 * h + j, at] = total[j]

    each_chunk(body)


def by_other(col_sum, n):
    return -sum(col_sum[pl.ds(128 * n + k, 16, stride=8), :] for k in range(8))


def by_own(row_sum):
    lane = lax.broadcasted_iota(jnp.int32, (N, N), 1)
    table = jnp.zeros((N, N), F32)
    for h in range(2):
        for j in range(3):
            table = jnp.where(lane == 4 * h + 4 + j, jnp.sum(row_sum[3 * h + j], axis=1, keepdims=True), table)
    return jnp.transpose(table)[:16]


def first_forces(which, tiles, left, right, homes, shear, bulk, inner, outer, row_in, row_out, col_sum):
    def force_of(h, at):
        flat, tall = shear[h, at], bulk[h, at]

        def force(i, e):
            (length, pull, rest), n = either(inner, outer, i, h, e)
            return pull[n, at] * (length[n, at] * tall + rest[n, at] * flat)

        return force

    def place(i, h, e, j):
        return tile_of(tiles, left, right, i, h, e)[3 + j : 4 + j]

    press(which, force_of, place, homes, 3, row_in, row_out, col_sum)


def first_body(tiles, left, right, mixed, homes, volume_, swell_, *refs):
    inner, (push, third_, shear_, bulk, row_sum), refs = refs[:3], refs[3:8], refs[8:]
    outer, (vol, swl, col_sum) = refs[:6], refs[6:]

    def measure_outer(at):
        home = [[homes[h, j, at] for j in range(6)] for h in range(2)]
        volume = [volume_[h, at] for h in range(2)]
        swell = [swell_[h, at] for h in range(2)]
        measure(
            at, OUTER, lambda i, h, e: tile_of(tiles, left, right, i, h, e), home, mixed, volume, swell, *outer
        )
        for h in range(2):
            vol[h, at] = volume[h]
            swl[h, at] = swell[h]

    each_chunk(measure_outer)
    for h in range(2):
        here = homes[h, 6]
        mass = jnp.maximum(here * jnp.sum(vol[h], axis=1, keepdims=True), 1.0)
        share = here / mass
        dilatation = 3.0 * (share * jnp.sum(swl[h], axis=1, keepdims=True))
        shear = 7.5 * share
        third_[h] = dilatation / 3.0
        shear_[h] = shear
        bulk[h] = 0.1175 * dilatation * shear
    three = (outer[0], outer[3], outer[4])
    first_forces((0,), tiles, left, right, homes, shear_, bulk, inner, three, None, row_sum, col_sum)
    push[...] = 0.04 * by_other(col_sum, 0)


def first_rest_body(tiles, left, right, homes, state, shear, bulk, row_in, *refs):
    inner, outer, (push, row_sum, col_sum) = refs[:3], refs[3:6], refs[6:]
    first_forces((1, 2), tiles, left, right, homes, shear, bulk, inner, outer, row_in, row_sum, col_sum)
    push[0] = 0.04 * (by_own(row_sum) + by_other(col_sum, 0)) + state[0]
    push[1] = 0.04 * by_other(col_sum, 1)


def relax_body(held, third, shear, len_i, len_o, wgt_i, wgt_o, str_i, str_o, new, mixed, firm):
    def body(at):
        for h in range(2):
            lean, flat = third[h, at], shear[h, at]
            for i in range(3):
                for e in range(3):
                    (length, weight, stretch), n = either((len_i, wgt_i, str_i), (len_o, wgt_o, str_o), i, h, e)
                    m = BLOCKS.index((i, h, e))
                    deviator = stretch[n, at] - lean * length[n, at]
                    one = (0.6 * held[0, h, i, e, at].astype(F32) + 0.4 * deviator).astype(jnp.bfloat16)
                    two = (0.95 * held[1, h, i, e, at].astype(F32) + 0.05 * deviator).astype(jnp.bfloat16)
                    new[0, h, i, e, at] = one
                    new[1, h, i, e, at] = two
                    mixed[m, at] = 0.21 * one.astype(F32) + 0.2375 * two.astype(F32)
                    firm[m, at] = weight[n, at] * flat

    each_chunk(body)


def move(rows, tiles, left, right, pull, i, n):
    for c in range(4):
        t = tile_of(tiles, left, right, i, 0, c)
        rows[4 * n + c, 0:3] = t[0:3] + pull[4 * c : 4 * c + 3] * t[7:8]
        rows[4 * n + c, 3:8] = jnp.zeros((5, N), F32)


def stretches(which, rows, homes, swell_in, swell_out, mixed, firm, inner, outer, stretch_, kernel_, rest_):
    def body(at):
        for h in range(2):
            home = [homes[h, j, at] for j in range(3)]
            swell = jnp.zeros((CHUNK, N), F32) if swell_in is None else swell_in[h, at]
            for q, i in enumerate(which):
                for e in range(3):
                    (length, lever), n = either(inner, outer, i, h, e)
                    t, m, w = 4 * q + h + e, BLOCKS.index((i, h, e)), 6 * q + 3 * h + e
                    gap = [rows[t, j : j + 1] - home[j] for j in range(3)]
                    squared = gap[0] * gap[0] + gap[1] * gap[1] + gap[2] * gap[2]
                    stretch = root(squared) - length[n, at]
                    swell = swell + lever[n, at] * stretch
                    stretch_[w, at] = stretch
                    kernel_[w, at] = firm[m, at] * lax.rsqrt(squared + 0.01)
                    rest_[w, at] = 0.8475 * stretch - mixed[m, at]
            swell_out[h, at] = swell

    each_chunk(body)


def second_body(tiles, left, right, pull, state, mixed, firm, len_i, len_o, lev_i, lev_o, *refs):
    rows, homes, own, swell, stretch, kernel, rest = refs
    for n in range(2):
        move(rows, tiles, left, right, pull[n], 1 + n, n)
    own[0] = pull[0]
    own[1] = state[1] + 5.0 * (pull[0] - state[0])
    for h in range(2):
        spread(homes, h, rows[1 + h], 3)
    stretches((1, 2), rows, homes, None, swell, mixed, firm, (len_i, lev_i), (len_o, lev_o), stretch, kernel, rest)


def second_forces(which, rows, homes, bulk, inner, outer, geo, row_in, row_out, col_sum):
    def force_of(h, at):
        tall = bulk[h, at]

        def force(i, e):
            length, n = either(inner, outer, i, h, e)
            (kernel, rest), w = geo(i, h, e)
            return kernel[w, at] * (length[n, at] * tall + rest[w, at])

        return force

    def place(i, h, e, j):
        ref, n = rows(i)
        return ref[4 * n + h + e, j : j + 1]

    press(which, force_of, place, homes, 0, row_in, row_out, col_sum)


def second_side_body(
    tiles, left, right, pull, mixed, firm, len_i, len_o, lev_i, lev_o, shear, rows, homes, swell, kernel, rest, *refs
):
    push, third, bulk, row_sum, stretch_n, rows_n, swl, kernel_n, rest_n, col_sum = refs
    move(rows_n, tiles, left, right, pull, 0, 0)
    stretches(
        (0,), rows_n, homes, swell, swl, mixed, firm, (len_i, lev_i), (len_o, lev_o), stretch_n, kernel_n, rest_n
    )
    for h in range(2):
        dilatation = 0.4 * shear[h] * jnp.sum(swl[h], axis=1, keepdims=True)
        third[h] = dilatation / 3.0
        bulk[h] = 0.1175 * dilatation

    def geo(i, h, e):
        return ((kernel, rest), 6 + 3 * h + e) if i else ((kernel_n, rest_n), 3 * h + e)

    second_forces(
        (0, 2), lambda i: (rows, 1) if i else (rows_n, 0), homes, bulk, len_i, len_o, geo, None, row_sum, col_sum
    )
    for n in range(2):
        push[n] = by_other(col_sum, n)


def second_own_body(len_i, len_o, bulk, rows, homes, kernel, rest, row_in, push, row_sum, col_sum):
    def geo(i, h, e):
        return (kernel, rest), 3 * h + e

    second_forces((1,), lambda i: (rows, 0), homes, bulk, len_i, len_o, geo, row_in, row_sum, col_sum)
    push[...] = by_own(row_sum) + by_other(col_sum, 0)


def settle_body(held, third, len_i, len_o, stretch_n, stretch, new):
    def body(at):
        for h in range(2):
            lean = third[h, at]
            for i in range(3):
                for e in range(3):
                    length, n = either(len_i, len_o, i, h, e)
                    longer = stretch[6 * (i - 1) + 3 * h + e, at] if i else stretch_n[3 * h + e, at]
                    deviator = longer - lean * length[n, at]
                    one, two = held[0, h, i, e, at].astype(F32), held[1, h, i, e, at].astype(F32)
                    k = first_offset(i) + e
                    new[0, 0, h, k, at] = (0.6 * one + 0.4 * deviator).astype(jnp.bfloat16)
                    new[1, 0, h, k, at] = (0.95 * two + 0.05 * deviator).astype(jnp.bfloat16)

    each_chunk(body)


def finish_body(total, own, displacement, velocity):
    speed = own[1] + 0.2 * total[...]
    place = own[0] + 0.2 * speed
    for t in range(2):
        for j in range(3):
            q = 4 * (t + 1) + j
            velocity[j, 0, t : t + 1] = speed[q : q + 1]
            displacement[j, 0, t : t + 1] = place[q : q + 1]


def swap_pairs(size, parity):
    return [(i, (i + 1) % size if i % 2 == parity else (i - 1) % size) for i in range(size)]


def row_swaps(slabs, columns):
    pairs = []
    for s in range(slabs):
        for c in range(columns):
            if s in (0, slabs - 1):
                pairs.append((s * columns + c, s * columns + (c ^ 2)))
            else:
                pairs.append((s * columns + c, (s + 1 if s % 2 else s - 1) * columns + c))
    return pairs


def inner_swaps(slabs, columns):
    pairs = []
    for s in range(slabs):
        for c in range(columns):
            if c in (0, columns - 1):
                pairs.append((s * columns + c, (s ^ 1) * columns + c))
            else:
                pairs.append((s * columns + c, s * columns + (c + 1 if c % 2 else c - 1)))
    return pairs


def per_device(slabs, columns, rest_points, tile_fill, displacement, velocity, back_extension):
    s, c = lax.axis_index("slab"), lax.axis_index("col")
    c_odd, low, high = c % 2 == 1, c > 0, c < columns - 1
    inside = (s > 0) & (s < slabs - 1)
    c_odd, low, high, inside = lax.optimization_barrier((c_odd, low, high, inside))
    slab_near, slab_far = swap_pairs(slabs, 0), row_swaps(slabs, columns)
    col_near, col_far = swap_pairs(columns, 0), inner_swaps(slabs, columns)

    def to_near(values):
        return lax.ppermute(values, "slab", slab_near)

    def to_far(values):
        return lax.ppermute(values, ("slab", "col"), slab_far)

    def over_col(to_left, to_right):
        far = lax.ppermute(jnp.where(c_odd, to_right, to_left), ("slab", "col"), col_far)
        near = lax.ppermute(jnp.where(c_odd, to_left, to_right), "col", col_near)
        from_left = jnp.where(low, jnp.where(c_odd, near, far), 0.0)
        from_right = jnp.where(high, jnp.where(c_odd, far, near), 0.0)
        return from_left, from_right

    def add_over_col(sums):
        lo, hi = sums[..., :8, :], sums[..., 8:, :]
        from_left, from_right = over_col(lo, hi)
        return jnp.concatenate([lo + from_left, hi + from_right], axis=-2)

    history = jax.ShapeDtypeStruct((2, 2, 3, 3, N, N), back_extension.dtype)
    pages, big = block(2, N, N), block(6, N, N)
    column_sums = [pltpu.VMEM((128 * n, N), F32) for n in range(3)]
    row_sums = pltpu.VMEM((6, N, N), F32)
    hbm = pl.BlockSpec(memory_space=pl.ANY)
    own, state = call(
        pack_body,
        [block(2, 8, N), block(2, 16, N)],
        (tile_fill, rest_points, displacement, velocity),
        scratch=[pltpu.SMEM(tile_fill.shape, jnp.int32)]
        + [pltpu.VMEM(rest_points.shape, F32)] * 3
        + [pltpu.SemaphoreType.DMA((4,))],
        specs=[hbm] * 4,
        limit=None,
    )
    far = to_far(own)
    near = to_near(own)
    held, mixed = call(recall_body, [history, block(18, N, N)], (back_extension,), work=2_000_000)
    near, far, held, mixed = lax.optimization_barrier((near, far, held, mixed))
    tiles = jnp.stack([near, own, jnp.where(inside, far, 0.0)])
    left, right = over_col(tiles[:, 0], tiles[:, 1])
    homes, volume, swell, *inner = call(
        inner_body, [block(2, 7, N, N), pages, pages] + [block(12, N, N)] * 6, (tiles, mixed), work=6_000_000
    )
    three_i = (inner[0], inner[3], inner[4])
    push, third, shear, bulk, rows, *outer = call(
        first_body,
        [block(16, N), pages, pages, pages, big] + [big] * 6,
        (tiles, left, right, mixed, homes, volume, swell, *three_i),
        scratch=[pltpu.VMEM((2, N, N), F32)] * 2 + [column_sums[1]],
        work=4_000_000,
    )
    got = to_near(push)
    (push,) = call(
        first_rest_body,
        [block(2, 16, N)],
        (tiles, left, right, homes, state, shear, bulk, rows, *three_i, outer[0], outer[3], outer[4]),
        scratch=[row_sums, column_sums[2]],
        work=4_000_000,
    )
    got, push = lax.optimization_barrier((got, push))
    two = jnp.stack([push[0] + got, push[1]])
    back = to_far(two)
    held, mixed, firm = call(
        relax_body,
        [history, block(18, N, N), block(18, N, N)],
        (held, third, shear, inner[0], outer[0], inner[2], outer[2], inner[5], outer[5]),
        work=4_000_000,
    )
    back, held, mixed, firm = lax.optimization_barrier((back, held, mixed, firm))
    back = jnp.where(inside, back, 0.0)
    pull = add_over_col(two + jnp.stack([back[1], back[0]]))
    pull_near = to_near(pull[0])
    geometry = (mixed, firm, inner[0], outer[0], inner[1], outer[1])
    moved, homes, state, swell, stretch, kernel, rest = call(
        second_body,
        [block(8, 8, N), block(2, 3, N, N), block(2, 16, N), pages] + [block(12, N, N)] * 3,
        (tiles, left, right, pull, state, *geometry),
        work=4_000_000,
    )
    pull_near, swell = lax.optimization_barrier((pull_near, swell))
    push, third, bulk, rows, stretch_near = call(
        second_side_body,
        [block(2, 16, N), pages, pages, big, big],
        (tiles, left, right, pull_near, *geometry, shear, moved, homes, swell, kernel, rest),
        scratch=[pltpu.VMEM((4, 8, N), F32), pltpu.VMEM((2, N, N), F32), row_sums, row_sums, column_sums[2]],
        work=4_000_000,
    )
    far = to_far(push[1])
    near = to_near(push[0])
    (push,) = call(
        second_own_body,
        [block(16, N)],
        (inner[0], outer[0], bulk, moved, homes, kernel, rest, rows),
        scratch=[row_sums, column_sums[1]],
        work=4_000_000,
    )
    near, far, push = lax.optimization_barrier((near, far, push))
    total = add_over_col(push + near + jnp.where(inside, far, 0.0))
    (held,) = call(
        settle_body,
        [jax.ShapeDtypeStruct(back_extension.shape, back_extension.dtype)],
        (held, third, inner[0], outer[0], stretch_near, stretch),
        work=3_000_000,
    )
    shape = block(*rest_points.shape)
    displacement, velocity = call(finish_body, [shape, shape], (total, state))
    return (displacement, velocity, held)


def solution(mesh):
    in_specs = (
        P(None, "slab", "col", None),
        P("slab", "col"),
        P(None, "slab", "col", None),
        P(None, "slab", "col", None),
        P(None, "slab", "col", None, None, None),
    )
    out_specs = (
        P(None, "slab", "col", None),
        P(None, "slab", "col", None),
        P(None, "slab", "col", None, None, None),
    )
    return jax.shard_map(
        functools.partial(per_device, mesh.shape["slab"], mesh.shape["col"]),
        mesh=mesh,
        in_specs=in_specs,
        out_specs=out_specs,
        check_vma=False,
    )
```

time: 51.6 us -> 46.6 us (0.903)
  the two profiles are of different devices: /device:TPU:38 before, /device:TPU:66 now
where the time goes in v3:
time: 46.6 us; the launch traced here: 46.4 us
  starting transfers between devices  17.9 us (38%)
  waiting for transfers between devices  16.3 us (35%)
  Pallas kernels  10.1 us (22%)
  local copies, waits for them, and re-layouts  1.29 us (3%)
  between operations  0.79 us (2%)
    pallas_call x11, Pallas kernels, call(): pl.pallas_call(body, out_shape=outs, in_specs=specs or [VMEM] * len(opera...  10.1 us
    ppermute x3, waiting for transfers between devices, to_far(): return lax.ppermute(values, ('slab', 'col'), slab_far)  8.27 us
    ppermute x3, starting transfers between devices, over_col(): near = lax.ppermute(jnp.where(c_odd, to_left, to_right), 'col', col_near)  7.25 us
    ppermute x3, starting transfers between devices, over_col(): lax.ppermute(jnp.where(c_odd, to_right, to_left), ('slab', 'col'), col_far)  5.53 us
    ppermute x3, starting transfers between devices, to_far(): return lax.ppermute(values, ('slab', 'col'), slab_far)  4.56 us
    ppermute x3, waiting for transfers between devices, over_col(): lax.ppermute(jnp.where(c_odd, to_right, to_left), ('slab', 'col'), col_far)  4.23 us
    ppermute x3, waiting for transfers between devices, over_col(): near = lax.ppermute(jnp.where(c_odd, to_left, to_right), 'col', col_near)  3.12 us
    unnamed x6, local copies, waits for them, and re-layouts  1.28 us
  transfers between devices with their start and end apart: 13, of which 10 were waited for; matrix products, arithmetic and copies ran while one was open for 0% of the time, Pallas kernels for 13%

profile of v3, /device:TPU:66, one launch (start us, length us, event | category | flops | bytes accessed | tf_op | source)
XLA Modules:
  0.0 46.4 jit_solution(9965831389522516439)
XLA Ops:
  0.6 1.4 %shard_map.76 = (f32[2,8,128]{2,1,0:T(8,128)}, f32[2,16,128]{2,1,0:T(8,128)}) custom-call(s32[1,2]{1,0:T(1,128)} %fill_far.1, f32[3,1,2,128]{3,2,1,0:T(2,128)} %rest_far.1, f32[3,1,2,128]{3,2,1,0:T(2,128)} %displacement_far.1, f32[3,1,2,128]{3,2,1,0:T(2,128)} %velocity_far.1), custom_call_target="tpu_custom_call" | custom-call | tf_op jit(solution)/shard_map/pallas_call | solution.py:30
  2.0 2.5 %collective-permute-start.1 = (f32[2,8,128]{2,1,0:T(8,128)}, f32[2,8,128]{2,1,0:T(8,128)S(1)}, u32[]{:S(2)}, u32[]{:S(2)}) collective-permute-start(f32[2,8,128]{2,1,0:T(8,128)} %get-tuple-element.63), channel_id=1, source_target_pairs={{0,2},{1,3},{2,0},{3,1},{4,6},{5,7},{6,4},{7,5},{8,16},{9,17},{10,... | collective-permute-start | bytes 24584 | tf_op jit(solution)/shard_map/ppermute | solution.py:400
  4.5 1.3 %copy-done = bf16[2,1,2,9,128,128]{5,4,3,2,1,0:T(8,128)(2,1)S(1)} copy-done((bf16[2,1,2,9,128,128]{5,4,3,2,1,0:T(8,128)(2,1)S(1)}, bf16[2,1,2,9,128,128]{5,4,3,2,1,0:T(8,128)(2,1)}, u32[]{:S(2)}) %copy-start) | copy-done | bytes 1179672
  6.2 1.3 %collective-permute-done.1 = f32[2,8,128]{2,1,0:T(8,128)S(1)} collective-permute-done((f32[2,8,128]{2,1,0:T(8,128)}, f32[2,8,128]{2,1,0:T(8,128)S(1)}, u32[]{:S(2)}, u32[]{:S(2)}) %collective-permute-start.1) | collective-permute-done | bytes 8224 | tf_op jit(solution)/shard_map/ppermute | solution.py:400
  7.5 1.7 %collective-permute-start.3 = (f32[3,8,128]{2,1,0:T(8,128)S(1)}, f32[3,8,128]{2,1,0:T(8,128)S(1)}, u32[]{:S(2)}, u32[]{:S(2)}) collective-permute-start(f32[3,8,128]{2,1,0:T(8,128)S(1)} %select_bitcast_fusion), channel_id=1, source_target_pairs={{0,8},{1,2},{2,1},{3,4},{4,3},{5,6},{6,5},{7,15},{8,0},{9,10},{10,... | collective-permute-start | bytes 36872 | tf_op jit(solution)/shard_map/ppermute | solution.py:403
  9.3 2.9 %collective-permute-start.2 = (f32[3,8,128]{2,1,0:T(8,128)S(1)}, f32[3,8,128]{2,1,0:T(8,128)S(1)}, u32[]{:S(2)}, u32[]{:S(2)}) collective-permute-start(f32[3,8,128]{2,1,0:T(8,128)S(1)} %fusion), channel_id=1, source_target_pairs={{0,1},{1,0},{2,3},{3,2},{4,5},{5,4},{6,7},{7,6},{8,9},{9,8},{10,11... | collective-permute-start | bytes 36872 | tf_op jit(solution)/shard_map/ppermute | solution.py:404
  12.2 1.5 %shard_map.78 = (f32[2,7,128,128]{3,2,1,0:T(8,128)S(1)}, f32[2,128,128]{2,1,0:T(8,128)S(1)}, f32[2,128,128]{2,1,0:T(8,128)S(1)}, f32[12,128,128]{2,1,0:T(8,128)S...) custom-call(f32[3,2,8,128]{3,2,1,0:T(8,128)S(1)} %pad_maximum_fusion, ...), custom_call_target="tpu_custom_call" | custom-call | flops 6000000 | bytes 65536 | tf_op jit(solution)/shard_map/pallas_call | solution.py:30
  13.7 0.8 %collective-permute-done.2 = f32[3,8,128]{2,1,0:T(8,128)S(1)} collective-permute-done((f32[3,8,128]{2,1,0:T(8,128)S(1)}, f32[3,8,128]{2,1,0:T(8,128)S(1)}, u32[]{:S(2)}, u32[]{:S(2)}) %collective-permute-start.2) | collective-permute-done | bytes 12320 | tf_op jit(solution)/shard_map/ppermute | solution.py:404
  14.5 0.9 %shard_map.79 = (f32[16,128]{1,0:T(8,128)S(1)}, f32[2,128,128]{2,1,0:T(8,128)S(1)}, f32[2,128,128]{2,1,0:T(8,128)S(1)}, f32[2,128,128]{2,1,0:T(8,128)S(1)}, f32[...) custom-call(f32[3,2,8,128]{3,2,1,0:T(8,128)S(1)} %pad_maximum_fusion, ...), custom_call_target="tpu_custom_call" | custom-call | flops 4000000 | bytes 65536 | tf_op jit(solution)/shard_map/pallas_call | solution.py:30
  15.6 0.7 %shard_map.80 = f32[2,16,128]{2,1,0:T(8,128)S(1)} custom-call(f32[3,2,8,128]{3,2,1,0:T(8,128)S(1)} %pad_maximum_fusion.tiles, f32[3,8,128]{2,1,0:T(8,128)S(1)} %get-tuple-element.126.left, f32[3,8,128]{2,1,0:T(8,128)S(1)} %get-tuple-element.125.right, f32[2,7,128,128]{3,2,1,0:T(8,128)S(1)} %get-tuple-element.73.homes, f32[2,16,128]{2,1,0:T(8,128)S(1)} %copy-done.1, ...), custom_call_target="tpu_custom_call" | custom-call | flops 4000000 | bytes 65536 | tf_op jit(solution)/shard_map/pallas_call | solution.py:30
  16.7 2.0 %collective-permute-start.5 = (f32[2,16,128]{2,1,0:T(8,128)S(1)}, f32[2,16,128]{2,1,0:T(8,128)S(1)}, u32[]{:S(2)}, u32[]{:S(2)}) collective-permute-start(f32[2,16,128]{2,1,0:T(8,128)S(1)} %pad_maximum_fusion.2), channel_id=1, source_target_pairs={{0,2},{1,3},{2,0},{3,1},{4,6},{5,7},{6,4},{7,5},{8,16},{9,17},{10,... | collective-permute-start | bytes 49160 | tf_op jit(solution)/shard_map/ppermute | solution.py:400
  18.7 0.7 %shard_map.81 = (bf16[2,2,3,3,128,128]{5,4,3,2,1,0:T(8,128)(2,1)S(1)}, f32[18,128,128]{2,1,0:T(8,128)S(1)}, f32[18,128,128]{2,1,0:T(8,128)S(1)}) custom-call(bf16[2,2,3,3,128,128]{5,4,3,2,1,0:T(8,128)(2,1)S(1)} %get-tuple-element.89.held, f32[2,128,128]{2,1,0:T(8,128)S(1)} %get-tuple-element.90.third, f32[2,128,128]{2,1,0:T(8,128)S(1)} %get-tuple-element.81.shear, ...), custom_call_target="tpu_custom_call" | custom-call | flops 4000000 | bytes 65536 | tf_op jit(solution)/shard_map/pallas_call | solution.py:30
  19.4 2.7 %collective-permute-done.5 = f32[2,16,128]{2,1,0:T(8,128)S(1)} collective-permute-done((f32[2,16,128]{2,1,0:T(8,128)S(1)}, f32[2,16,128]{2,1,0:T(8,128)S(1)}, u32[]{:S(2)}, u32[]{:S(2)}) %collective-permute-start.5) | collective-permute-done | bytes 16416 | tf_op jit(solution)/shard_map/ppermute | solution.py:400
  22.1 2.8 %collective-permute-start.7 = (f32[2,8,128]{2,1,0:T(8,128)S(1)}, f32[2,8,128]{2,1,0:T(8,128)S(1)}, u32[]{:S(2)}, u32[]{:S(2)}) collective-permute-start(f32[2,8,128]{2,1,0:T(8,128)S(1)} %get-tuple-element.131), channel_id=1, source_target_pairs={{0,8},{1,2},{2,1},{3,4},{4,3},{5,6},{6,5},{7,15},{8,0},{9,10},{10,... | collective-permute-start | bytes 24584 | tf_op jit(solution)/shard_map/ppermute | solution.py:403
  24.9 2.1 %collective-permute-start.6 = (f32[2,8,128]{2,1,0:T(8,128)S(1)}, f32[2,8,128]{2,1,0:T(8,128)S(1)}, u32[]{:S(2)}, u32[]{:S(2)}) collective-permute-start(f32[2,8,128]{2,1,0:T(8,128)S(1)} %get-tuple-element.132), channel_id=1, source_target_pairs={{0,1},{1,0},{2,3},{3,2},{4,5},{5,4},{6,7},{7,6},{8,9},{9,8},{10,11... | collective-permute-start | bytes 24584 | tf_op jit(solution)/shard_map/ppermute | solution.py:404
  27.1 1.2 %collective-permute-done.7 = f32[2,8,128]{2,1,0:T(8,128)S(1)} collective-permute-done((f32[2,8,128]{2,1,0:T(8,128)S(1)}, f32[2,8,128]{2,1,0:T(8,128)S(1)}, u32[]{:S(2)}, u32[]{:S(2)}) %collective-permute-start.7) | collective-permute-done | bytes 8224 | tf_op jit(solution)/shard_map/ppermute | solution.py:403
  28.2 1.9 %collective-permute-done.6 = f32[2,8,128]{2,1,0:T(8,128)S(1)} collective-permute-done((f32[2,8,128]{2,1,0:T(8,128)S(1)}, f32[2,8,128]{2,1,0:T(8,128)S(1)}, u32[]{:S(2)}, u32[]{:S(2)}) %collective-permute-start.6) | collective-permute-done | bytes 8224 | tf_op jit(solution)/shard_map/ppermute | solution.py:404
  30.2 0.9 %shard_map.82 = (f32[8,8,128]{2,1,0:T(8,128)S(1)}, f32[2,3,128,128]{3,2,1,0:T(8,128)S(1)}, f32[2,16,128]{2,1,0:T(8,128)S(1)}, f32[2,128,128]{2,1,0:T(8,128)S(1)}...) custom-call(f32[3,2,8,128]{3,2,1,0:T(8,128)S(1)} %pad_maximum_fusion.tiles, ...), custom_call_target="tpu_custom_call" | custom-call | flops 4000000 | bytes 65536 | tf_op jit(solution)/shard_map/pallas_call | solution.py:30
  31.4 0.9 %shard_map.83 = (f32[2,16,128]{2,1,0:T(8,128)S(1)}, f32[2,128,128]{2,1,0:T(8,128)S(1)}, f32[2,128,128]{2,1,0:T(8,128)S(1)}, f32[6,128,128]{2,1,0:T(8,128)S(1)}, f32[6,128,128]{2,1,0:T(8,128)S(1)}) custom-call(f32[3,2,8,128]{3,2,1,0:T(8,128)S(1)} %pad_maximum_fusion.tiles, f32[3,8,128]{2,1,0:T(8,128)S(1)} %get-tuple-element.126.left, ...), custom_call_target="tpu_custom_call" | custom-call | flops 4000000 | bytes 65536 | tf_op jit(solution)/shard_map/pallas_call | solution.py:30
  33.2 4.3 %collective-permute-done.10 = f32[16,128]{1,0:T(8,128)S(1)} collective-permute-done((f32[16,128]{1,0:T(8,128)S(1)}, f32[16,128]{1,0:T(8,128)S(1)}, u32[]{:S(2)}, u32[]{:S(2)}) %collective-permute-start.10) | collective-permute-done | bytes 8224 | tf_op jit(solution)/shard_map/ppermute | solution.py:400
  37.6 2.2 %collective-permute-start.11 = (f32[8,128]{1,0:T(8,128)S(1)}, f32[8,128]{1,0:T(8,128)S(1)}, u32[]{:S(2)}, u32[]{:S(2)}) collective-permute-start(f32[8,128]{1,0:T(8,128)S(1)} %get-tuple-element.135), channel_id=1, source_target_pairs={{0,1},{1,0},{2,3},{3,2},{4,5},{5,4},{6,7},{7,6},{8,9},{9,8},{10,11... | collective-permute-start | bytes 12296 | tf_op jit(solution)/shard_map/ppermute | solution.py:404
  39.8 0.9 %collective-permute-start.12 = (f32[8,128]{1,0:T(8,128)S(1)}, f32[8,128]{1,0:T(8,128)S(1)}, u32[]{:S(2)}, u32[]{:S(2)}) collective-permute-start(f32[8,128]{1,0:T(8,128)S(1)} %get-tuple-element.136), channel_id=1, source_target_pairs={{0,8},{1,2},{2,1},{3,4},{4,3},{5,6},{6,5},{7,15},{8,0},{9,10},{10,... | collective-permute-start | bytes 12296 | tf_op jit(solution)/shard_map/ppermute | solution.py:403
  40.7 1.5 %shard_map.86 = bf16[2,1,2,9,128,128]{5,4,3,2,1,0:T(8,128)(2,1)} custom-call(bf16[2,2,3,3,128,128]{5,4,3,2,1,0:T(8,128)(2,1)S(1)} %get-tuple-element.119.held, f32[2,128,128]{2,1,0:T(8,128)S(1)} %get-tuple-element.120.third, f32[12,128,128]{2,1,0:T(8,128)S(1)} %get-tuple-element.76.refs_0_.len_i, f32[6,128,128]{2,1,0:T(8,128)S(1)} %get-tuple-element.84.refs_3_.len_o, ...), custom_call_target="tpu_custom_call" | custom-call | flops 3000000 | bytes 65536 | tf_op jit(solution)/shard_map/pallas_call | solution.py:30
  42.8 3.0 %collective-permute-done.12 = f32[8,128]{1,0:T(8,128)S(1)} collective-permute-done((f32[8,128]{1,0:T(8,128)S(1)}, f32[8,128]{1,0:T(8,128)S(1)}, u32[]{:S(2)}, u32[]{:S(2)}) %collective-permute-start.12) | collective-permute-done | bytes 4128 | tf_op jit(solution)/shard_map/ppermute | solution.py:403
  (39 shorter events, 3.4 us)
Async XLA Ops:
  2.0 5.5 %copy-start.2 = (f32[2,8,128]{2,1,0:T(8,128)S(1)}, f32[2,8,128]{2,1,0:T(8,128)}, u32[]{:S(2)}) copy-start(f32[2,8,128]{2,1,0:T(8,128)} %get-tuple-element.63) | copy-start | bytes 24580
  2.0 5.5 %collective-permute-start.1 = (f32[2,8,128]{2,1,0:T(8,128)}, f32[2,8,128]{2,1,0:T(8,128)S(1)}, u32[]{:S(2)}, u32[]{:S(2)}) collective-permute-start(f32[2,8,128]{2,1,0:T(8,128)} %get-tuple-element.63), channel_id=1, source_target_pairs={{0,2},{1,3},{2,0},{3,1},{4,6},{5,7},{6,4},{7,5},{8,16},{9,17},{10,... | collective-permute-start | bytes 24584 | tf_op jit(solution)/shard_map/ppermute | solution.py:400
  4.5 3.0 %collective-permute-start = (f32[2,8,128]{2,1,0:T(8,128)}, f32[2,8,128]{2,1,0:T(8,128)S(1)}, u32[]{:S(2)}, u32[]{:S(2)}) collective-permute-start(f32[2,8,128]{2,1,0:T(8,128)} %get-tuple-element.63), channel_id=1, source_target_pairs={{0,8},{8,0},{16,24},{24,16},{32,40},{40,32},{48,56},{56,48},{64,72... | collective-permute-start | bytes 24584 | tf_op jit(solution)/shard_map/ppermute | solution.py:397
  4.5 1.3 %copy-start = (bf16[2,1,2,9,128,128]{5,4,3,2,1,0:T(8,128)(2,1)S(1)}, bf16[2,1,2,9,128,128]{5,4,3,2,1,0:T(8,128)(2,1)}, u32[]{:S(2)}) copy-start(bf16[2,1,2,9,128,128]{5,4,3,2,1,0:T(8,128)(2,1)} %states.1) | copy-start | bytes 3538948
  7.5 6.2 %collective-permute-start.3 = (f32[3,8,128]{2,1,0:T(8,128)S(1)}, f32[3,8,128]{2,1,0:T(8,128)S(1)}, u32[]{:S(2)}, u32[]{:S(2)}) collective-permute-start(f32[3,8,128]{2,1,0:T(8,128)S(1)} %select_bitcast_fusion), channel_id=1, source_target_pairs={{0,8},{1,2},{2,1},{3,4},{4,3},{5,6},{6,5},{7,15},{8,0},{9,10},{10,... | collective-permute-start | bytes 36872 | tf_op jit(solution)/shard_map/ppermute | solution.py:403
  9.3 5.2 %collective-permute-start.2 = (f32[3,8,128]{2,1,0:T(8,128)S(1)}, f32[3,8,128]{2,1,0:T(8,128)S(1)}, u32[]{:S(2)}, u32[]{:S(2)}) collective-permute-start(f32[3,8,128]{2,1,0:T(8,128)S(1)} %fusion), channel_id=1, source_target_pairs={{0,1},{1,0},{2,3},{3,2},{4,5},{5,4},{6,7},{7,6},{8,9},{9,8},{10,11... | collective-permute-start | bytes 36872 | tf_op jit(solution)/shard_map/ppermute | solution.py:404
  14.5 1.1 %copy-start.1 = (f32[2,16,128]{2,1,0:T(8,128)S(1)}, f32[2,16,128]{2,1,0:T(8,128)}, u32[]{:S(2)}) copy-start(f32[2,16,128]{2,1,0:T(8,128)} %get-tuple-element.80.state) | copy-start | bytes 49156
  15.5 1.3 %collective-permute-start.4 = (f32[16,128]{1,0:T(8,128)S(1)}, f32[16,128]{1,0:T(8,128)S(1)}, u32[]{:S(2)}, u32[]{:S(2)}) collective-permute-start(f32[16,128]{1,0:T(8,128)S(1)} %get-tuple-element.79), channel_id=1, source_target_pairs={{0,8},{8,0},{16,24},{24,16},{32,40},{40,32},{48,56},{56,48},{64,72... | collective-permute-start | bytes 24584 | tf_op jit(solution)/shard_map/ppermute | solution.py:397
  16.7 5.4 %collective-permute-start.5 = (f32[2,16,128]{2,1,0:T(8,128)S(1)}, f32[2,16,128]{2,1,0:T(8,128)S(1)}, u32[]{:S(2)}, u32[]{:S(2)}) collective-permute-start(f32[2,16,128]{2,1,0:T(8,128)S(1)} %pad_maximum_fusion.2), channel_id=1, source_target_pairs={{0,2},{1,3},{2,0},{3,1},{4,6},{5,7},{6,4},{7,5},{8,16},{9,17},{10,... | collective-permute-start | bytes 49160 | tf_op jit(solution)/shard_map/ppermute | solution.py:400
  22.1 6.1 %collective-permute-start.7 = (f32[2,8,128]{2,1,0:T(8,128)S(1)}, f32[2,8,128]{2,1,0:T(8,128)S(1)}, u32[]{:S(2)}, u32[]{:S(2)}) collective-permute-start(f32[2,8,128]{2,1,0:T(8,128)S(1)} %get-tuple-element.131), channel_id=1, source_target_pairs={{0,8},{1,2},{2,1},{3,4},{4,3},{5,6},{6,5},{7,15},{8,0},{9,10},{10,... | collective-permute-start | bytes 24584 | tf_op jit(solution)/shard_map/ppermute | solution.py:403
  24.9 5.2 %collective-permute-start.6 = (f32[2,8,128]{2,1,0:T(8,128)S(1)}, f32[2,8,128]{2,1,0:T(8,128)S(1)}, u32[]{:S(2)}, u32[]{:S(2)}) collective-permute-start(f32[2,8,128]{2,1,0:T(8,128)S(1)} %get-tuple-element.132), channel_id=1, source_target_pairs={{0,1},{1,0},{2,3},{3,2},{4,5},{5,4},{6,7},{7,6},{8,9},{9,8},{10,11... | collective-permute-start | bytes 24584 | tf_op jit(solution)/shard_map/ppermute | solution.py:404
  30.1 1.3 %collective-permute-start.8 = (f32[16,128]{1,0:T(8,128)S(1)}, f32[16,128]{1,0:T(8,128)S(1)}, u32[]{:S(2)}, u32[]{:S(2)}) collective-permute-start(f32[16,128]{1,0:T(8,128)S(1)} %fusion.2), channel_id=1, source_target_pairs={{0,8},{8,0},{16,24},{24,16},{32,40},{40,32},{48,56},{56,48},{64,72... | collective-permute-start | bytes 24584 | tf_op jit(solution)/shard_map/ppermute | solution.py:397
  32.3 5.3 %collective-permute-start.10 = (f32[16,128]{1,0:T(8,128)S(1)}, f32[16,128]{1,0:T(8,128)S(1)}, u32[]{:S(2)}, u32[]{:S(2)}) collective-permute-start(f32[16,128]{1,0:T(8,128)S(1)} %get-tuple-element.129), channel_id=1, source_target_pairs={{0,2},{1,3},{2,0},{3,1},{4,6},{5,7},{6,4},{7,5},{8,16},{9,17},{10,... | collective-permute-start | bytes 24584 | tf_op jit(solution)/shard_map/ppermute | solution.py:400
  32.4 5.2 %collective-permute-start.9 = (f32[16,128]{1,0:T(8,128)S(1)}, f32[16,128]{1,0:T(8,128)S(1)}, u32[]{:S(2)}, u32[]{:S(2)}) collective-permute-start(f32[16,128]{1,0:T(8,128)S(1)} %get-tuple-element.130), channel_id=1, source_target_pairs={{0,8},{8,0},{16,24},{24,16},{32,40},{40,32},{48,56},{56,48},{64,72... | collective-permute-start | bytes 24584 | tf_op jit(solution)/shard_map/ppermute | solution.py:397
  37.6 5.2 %collective-permute-start.11 = (f32[8,128]{1,0:T(8,128)S(1)}, f32[8,128]{1,0:T(8,128)S(1)}, u32[]{:S(2)}, u32[]{:S(2)}) collective-permute-start(f32[8,128]{1,0:T(8,128)S(1)} %get-tuple-element.135), channel_id=1, source_target_pairs={{0,1},{1,0},{2,3},{3,2},{4,5},{5,4},{6,7},{7,6},{8,9},{9,8},{10,11... | collective-permute-start | bytes 12296 | tf_op jit(solution)/shard_map/ppermute | solution.py:404
  39.8 6.0 %collective-permute-start.12 = (f32[8,128]{1,0:T(8,128)S(1)}, f32[8,128]{1,0:T(8,128)S(1)}, u32[]{:S(2)}, u32[]{:S(2)}) collective-permute-start(f32[8,128]{1,0:T(8,128)S(1)} %get-tuple-element.136), channel_id=1, source_target_pairs={{0,8},{1,2},{2,1},{3,4},{4,3},{5,6},{6,5},{7,15},{8,0},{9,10},{10,... | collective-permute-start | bytes 12296 | tf_op jit(solution)/shard_map/ppermute | solution.py:403

commit v4 on v3

--- a/solution.py
+++ b/solution.py
@@ -68,23 +68,18 @@
     return tiles.at[i, c - 1] if c in (1, 2) else (right if c else left).at[i]
 
 
-def pack_body(fill_far, rest_far, displacement_far, velocity_far, own, state, fill, rest, displacement, velocity, sems):
-    pairs = ((fill_far, fill), (rest_far, rest), (displacement_far, displacement), (velocity_far, velocity))
+def pack_body(fill_far, rest_far, shift_far, own, fill, rest, shift, sems):
+    pairs = ((fill_far, fill), (rest_far, rest), (shift_far, shift))
     copies = [pltpu.make_async_copy(a, b, sems.at[i]) for i, (a, b) in enumerate(pairs)]
     for copy in copies:
         copy.start()
     for copy in copies:
         copy.wait()
     lane = lax.broadcasted_iota(jnp.int32, (1, N), 1)
-    state[...] = jnp.zeros_like(state)
     for t in range(2):
         for j in range(3):
-            spot, shift = rest[j, 0, t : t + 1], displacement[j, 0, t : t + 1]
-            speed = velocity[j, 0, t : t + 1]
-            own[t, j : j + 1] = spot
-            own[t, 3 + j : 4 + j] = spot + shift
-            state[0, 4 * t + 4 + j : 4 * t + 5 + j] = shift + 0.2 * speed
-            state[1, 4 * t + 4 + j : 4 * t + 5 + j] = speed
+            own[t, j : j + 1] = rest[j, 0, t : t + 1]
+            own[t, 3 + j : 4 + j] = rest[j, 0, t : t + 1] + shift[j, 0, t : t + 1]
         own[t, 6:7] = jnp.where(lane < fill[0, t], 1.0, 0.0)
         own[t, 7:8] = jnp.ones((1, N), F32)
 
@@ -218,8 +213,14 @@
     push[...] = 0.04 * by_other(col_sum, 0)
 
 
-def first_rest_body(tiles, left, right, homes, state, shear, bulk, row_in, *refs):
-    inner, outer, (push, row_sum, col_sum) = refs[:3], refs[3:6], refs[6:]
+def first_rest_body(tiles, left, right, homes, shift, speed, shear, bulk, row_in, *refs):
+    inner, outer, (push, state, row_sum, col_sum) = refs[:3], refs[3:6], refs[6:]
+    state[...] = jnp.zeros_like(state)
+    for h in range(2):
+        for j in range(3):
+            q = 4 * h + 4 + j
+            state[0, q : q + 1] = shift[j, 0, h : h + 1] + 0.2 * speed[j, 0, h : h + 1]
+            state[1, q : q + 1] = speed[j, 0, h : h + 1]
     first_forces((1, 2), tiles, left, right, homes, shear, bulk, inner, outer, row_in, row_sum, col_sum)
     push[0] = 0.04 * (by_own(row_sum) + by_other(col_sum, 0)) + state[0]
     push[1] = 0.04 * by_other(col_sum, 1)
@@ -304,7 +305,7 @@
 def second_side_body(
     tiles, left, right, pull, mixed, firm, len_i, len_o, lev_i, lev_o, shear, rows, homes, swell, kernel, rest, *refs
 ):
-    push, third, bulk, row_sum, stretch_n, rows_n, swl, kernel_n, rest_n, col_sum = refs
+    push, third, bulk, row_sum, stretch_n, rows_n, kernel_n, rest_n, swl, col_sum = refs
     move(rows_n, tiles, left, right, pull, 0, 0)
     stretches(
         (0,), rows_n, homes, swell, swl, mixed, firm, (len_i, lev_i), (len_o, lev_o), stretch_n, kernel_n, rest_n
@@ -315,21 +316,23 @@
         bulk[h] = 0.1175 * dilatation
 
     def geo(i, h, e):
-        return ((kernel, rest), 6 + 3 * h + e) if i else ((kernel_n, rest_n), 3 * h + e)
+        return (kernel, rest), 6 + 3 * h + e
+
+    second_forces((2,), lambda i: (rows, 1), homes, bulk, len_i, len_o, geo, None, row_sum, col_sum)
+    push[...] = by_other(col_sum, 0)
+
+
+def second_own_body(
+    len_i, len_o, bulk, rows, rows_n, homes, kernel, rest, kernel_n, rest_n, row_in, push, row_sum, col_sum
+):
+    def geo(i, h, e):
+        return ((kernel, rest) if i else (kernel_n, rest_n)), 3 * h + e
 
     second_forces(
-        (0, 2), lambda i: (rows, 1) if i else (rows_n, 0), homes, bulk, len_i, len_o, geo, None, row_sum, col_sum
-    )
-    for n in range(2):
-        push[n] = by_other(col_sum, n)
-
-
-def second_own_body(len_i, len_o, bulk, rows, homes, kernel, rest, row_in, push, row_sum, col_sum):
-    def geo(i, h, e):
-        return (kernel, rest), 3 * h + e
-
-    second_forces((1,), lambda i: (rows, 0), homes, bulk, len_i, len_o, geo, row_in, row_sum, col_sum)
-    push[...] = by_own(row_sum) + by_other(col_sum, 0)
+        (0, 1), lambda i: (rows if i else rows_n, 0), homes, bulk, len_i, len_o, geo, row_in, row_sum, col_sum
+    )
+    push[0] = by_other(col_sum, 0)
+    push[1] = by_own(row_sum) + by_other(col_sum, 1)
 
 
 def settle_body(held, third, len_i, len_o, stretch_n, stretch, new):
@@ -416,14 +419,14 @@
     column_sums = [pltpu.VMEM((128 * n, N), F32) for n in range(3)]
     row_sums = pltpu.VMEM((6, N, N), F32)
     hbm = pl.BlockSpec(memory_space=pl.ANY)
-    own, state = call(
+    (own,) = call(
         pack_body,
-        [block(2, 8, N), block(2, 16, N)],
-        (tile_fill, rest_points, displacement, velocity),
+        [block(2, 8, N)],
+        (tile_fill, rest_points, displacement),
         scratch=[pltpu.SMEM(tile_fill.shape, jnp.int32)]
-        + [pltpu.VMEM(rest_points.shape, F32)] * 3
-        + [pltpu.SemaphoreType.DMA((4,))],
-        specs=[hbm] * 4,
+        + [pltpu.VMEM(rest_points.shape, F32)] * 2
+        + [pltpu.SemaphoreType.DMA((3,))],
+        specs=[hbm] * 3,
         limit=None,
     )
     far = to_far(own)
@@ -444,10 +447,10 @@
         work=4_000_000,
     )
     got = to_near(push)
-    (push,) = call(
+    push, state = call(
         first_rest_body,
-        [block(2, 16, N)],
-        (tiles, left, right, homes, state, shear, bulk, rows, *three_i, outer[0], outer[3], outer[4]),
+        [block(2, 16, N), block(2, 16, N)],
+        (tiles, left, right, homes, displacement, velocity, shear, bulk, rows, *three_i, outer[0], outer[3], outer[4]),
         scratch=[row_sums, column_sums[2]],
         work=4_000_000,
     )
@@ -472,23 +475,23 @@
         work=4_000_000,
     )
     pull_near, swell = lax.optimization_barrier((pull_near, swell))
-    push, third, bulk, rows, stretch_near = call(
+    push, third, bulk, rows, stretch_near, moved_near, kernel_near, rest_near = call(
         second_side_body,
-        [block(2, 16, N), pages, pages, big, big],
+        [block(16, N), pages, pages, big, big, block(4, 8, N), big, big],
         (tiles, left, right, pull_near, *geometry, shear, moved, homes, swell, kernel, rest),
-        scratch=[pltpu.VMEM((4, 8, N), F32), pltpu.VMEM((2, N, N), F32), row_sums, row_sums, column_sums[2]],
+        scratch=[pltpu.VMEM((2, N, N), F32), column_sums[1]],
         work=4_000_000,
     )
-    far = to_far(push[1])
-    near = to_near(push[0])
+    far = to_far(push)
     (push,) = call(
         second_own_body,
-        [block(16, N)],
-        (inner[0], outer[0], bulk, moved, homes, kernel, rest, rows),
-        scratch=[row_sums, column_sums[1]],
+        [block(2, 16, N)],
+        (inner[0], outer[0], bulk, moved, moved_near, homes, kernel, rest, kernel_near, rest_near, rows),
+        scratch=[row_sums, column_sums[2]],
         work=4_000_000,
     )
-    near, far, push = lax.optimization_barrier((near, far, push))
+    near = to_near(push[0])
+    near, far, push = lax.optimization_barrier((near, far, push[1]))
     total = add_over_col(push + near + jnp.where(inside, far, 0.0))
     (held,) = call(
         settle_body,

time: 46.6 us -> 47.3 us (1.015)
  the two profiles are of different devices: /device:TPU:66 before, /device:TPU:34 now
where the time goes in v4:
time: 47.3 us; the launch traced here: 47.1 us
  waiting for transfers between devices  17.7 us (37%)
  starting transfers between devices  17.1 us (36%)
  Pallas kernels  10 us (21%)
  local copies, waits for them, and re-layouts  1.3 us (3%)
  between operations  0.79 us (2%)
    pallas_call x11, Pallas kernels, call(): pl.pallas_call(body, out_shape=outs, in_specs=specs or [VMEM] * len(opera...  10 us
    ppermute x3, waiting for transfers between devices, to_far(): return lax.ppermute(values, ('slab', 'col'), slab_far)  8.23 us
    ppermute x3, starting transfers between devices, over_col(): near = lax.ppermute(jnp.where(c_odd, to_left, to_right), 'col', col_near)  7.55 us
    ppermute x3, starting transfers between devices, over_col(): lax.ppermute(jnp.where(c_odd, to_right, to_left), ('slab', 'col'), col_far)  4.59 us
    ppermute x3, starting transfers between devices, to_far(): return lax.ppermute(values, ('slab', 'col'), slab_far)  4.48 us
    ppermute x3, waiting for transfers between devices, over_col(): lax.ppermute(jnp.where(c_odd, to_right, to_left), ('slab', 'col'), col_far)  4.2 us
    ppermute x3, waiting for transfers between devices, over_col(): near = lax.ppermute(jnp.where(c_odd, to_left, to_right), 'col', col_near)  3.79 us
    ppermute x4, waiting for transfers between devices, to_near(): return lax.ppermute(values, 'slab', slab_near)  1.52 us
  transfers between devices with their start and end apart: 13, of which 11 were waited for; matrix products, arithmetic and copies ran while one was open for 0% of the time, Pallas kernels for 12%

profile of v4, /device:TPU:34, one launch (start us, length us, event | category | flops | bytes accessed | tf_op | source)
XLA Modules:
  0.0 47.1 jit_solution(14575815298418848335)
XLA Ops:
  0.6 1.3 %shard_map.76 = f32[2,8,128]{2,1,0:T(8,128)} custom-call(s32[1,2]{1,0:T(1,128)} %fill_far.1, f32[3,1,2,128]{3,2,1,0:T(2,128)} %rest_far.1, f32[3,1,2,128]{3,2,1,0:T(2,128)} %shift.1), custom_call_target="tpu_custom_call" | custom-call | tf_op jit(solution)/shard_map/pallas_call | solution.py:30
  2.0 2.5 %collective-permute-start.1 = (f32[2,8,128]{2,1,0:T(8,128)}, f32[2,8,128]{2,1,0:T(8,128)S(1)}, u32[]{:S(2)}, u32[]{:S(2)}) collective-permute-start(f32[2,8,128]{2,1,0:T(8,128)} %shard_map.76), channel_id=1, source_target_pairs={{0,2},{1,3},{2,0},{3,1},{4,6},{5,7},{6,4},{7,5},{8,16},{9,17},{10,... | collective-permute-start | bytes 24584 | tf_op jit(solution)/shard_map/ppermute | solution.py:403
  4.5 1.3 %copy-done = bf16[2,1,2,9,128,128]{5,4,3,2,1,0:T(8,128)(2,1)S(1)} copy-done((bf16[2,1,2,9,128,128]{5,4,3,2,1,0:T(8,128)(2,1)S(1)}, bf16[2,1,2,9,128,128]{5,4,3,2,1,0:T(8,128)(2,1)}, u32[]{:S(2)}) %copy-start) | copy-done | bytes 1179672
  6.2 1.3 %collective-permute-done.1 = f32[2,8,128]{2,1,0:T(8,128)S(1)} collective-permute-done((f32[2,8,128]{2,1,0:T(8,128)}, f32[2,8,128]{2,1,0:T(8,128)S(1)}, u32[]{:S(2)}, u32[]{:S(2)}) %collective-permute-start.1) | collective-permute-done | bytes 8224 | tf_op jit(solution)/shard_map/ppermute | solution.py:403
  7.5 1.7 %collective-permute-start.3 = (f32[3,8,128]{2,1,0:T(8,128)S(1)}, f32[3,8,128]{2,1,0:T(8,128)S(1)}, u32[]{:S(2)}, u32[]{:S(2)}) collective-permute-start(f32[3,8,128]{2,1,0:T(8,128)S(1)} %select_bitcast_fusion), channel_id=1, source_target_pairs={{0,8},{1,2},{2,1},{3,4},{4,3},{5,6},{6,5},{7,15},{8,0},{9,10},{10,... | collective-permute-start | bytes 36872 | tf_op jit(solution)/shard_map/ppermute | solution.py:406
  9.3 3.2 %collective-permute-start.2 = (f32[3,8,128]{2,1,0:T(8,128)S(1)}, f32[3,8,128]{2,1,0:T(8,128)S(1)}, u32[]{:S(2)}, u32[]{:S(2)}) collective-permute-start(f32[3,8,128]{2,1,0:T(8,128)S(1)} %fusion), channel_id=1, source_target_pairs={{0,1},{1,0},{2,3},{3,2},{4,5},{5,4},{6,7},{7,6},{8,9},{9,8},{10,11... | collective-permute-start | bytes 36872 | tf_op jit(solution)/shard_map/ppermute | solution.py:407
  12.5 1.5 %shard_map.78 = (f32[2,7,128,128]{3,2,1,0:T(8,128)S(1)}, f32[2,128,128]{2,1,0:T(8,128)S(1)}, f32[2,128,128]{2,1,0:T(8,128)S(1)}, f32[12,128,128]{2,1,0:T(8,128)S...) custom-call(f32[3,2,8,128]{3,2,1,0:T(8,128)S(1)} %pad_maximum_fusion, ...), custom_call_target="tpu_custom_call" | custom-call | flops 6000000 | bytes 65536 | tf_op jit(solution)/shard_map/pallas_call | solution.py:30
  14.5 1.0 %shard_map.79 = (f32[16,128]{1,0:T(8,128)S(1)}, f32[2,128,128]{2,1,0:T(8,128)S(1)}, f32[2,128,128]{2,1,0:T(8,128)S(1)}, f32[2,128,128]{2,1,0:T(8,128)S(1)}, f32[...) custom-call(f32[3,2,8,128]{3,2,1,0:T(8,128)S(1)} %pad_maximum_fusion, ...), custom_call_target="tpu_custom_call" | custom-call | flops 4000000 | bytes 65536 | tf_op jit(solution)/shard_map/pallas_call | solution.py:30
  15.5 0.7 %shard_map.80 = (f32[2,16,128]{2,1,0:T(8,128)S(1)}, f32[2,16,128]{2,1,0:T(8,128)S(1)}) custom-call(f32[3,2,8,128]{3,2,1,0:T(8,128)S(1)} %pad_maximum_fusion.tiles, f32[3,8,128]{2,1,0:T(8,128)S(1)} %get-tuple-element.132.left, f32[3,8,128]{2,1,0:T(8,128)S(1)} %get-tuple-element.131.right, f32[2,7,128,128]{3,2,1,0:T(8,128)S(1)} %get-tuple-element.76.homes, ...), custom_call_target="tpu_custom_call" | custom-call | flops 4000000 | bytes 65536 | tf_op jit(solution)/shard_map/pallas_call | solution.py:30
  16.7 2.0 %collective-permute-start.5 = (f32[2,16,128]{2,1,0:T(8,128)S(1)}, f32[2,16,128]{2,1,0:T(8,128)S(1)}, u32[]{:S(2)}, u32[]{:S(2)}) collective-permute-start(f32[2,16,128]{2,1,0:T(8,128)S(1)} %pad_maximum_fusion.2), channel_id=1, source_target_pairs={{0,2},{1,3},{2,0},{3,1},{4,6},{5,7},{6,4},{7,5},{8,16},{9,17},{10,... | collective-permute-start | bytes 49160 | tf_op jit(solution)/shard_map/ppermute | solution.py:403
  18.7 0.7 %shard_map.81 = (bf16[2,2,3,3,128,128]{5,4,3,2,1,0:T(8,128)(2,1)S(1)}, f32[18,128,128]{2,1,0:T(8,128)S(1)}, f32[18,128,128]{2,1,0:T(8,128)S(1)}) custom-call(bf16[2,2,3,3,128,128]{5,4,3,2,1,0:T(8,128)(2,1)S(1)} %get-tuple-element.91.held, f32[2,128,128]{2,1,0:T(8,128)S(1)} %get-tuple-element.92.third, f32[2,128,128]{2,1,0:T(8,128)S(1)} %get-tuple-element.83.shear, ...), custom_call_target="tpu_custom_call" | custom-call | flops 4000000 | bytes 65536 | tf_op jit(solution)/shard_map/pallas_call | solution.py:30
  19.4 2.7 %collective-permute-done.5 = f32[2,16,128]{2,1,0:T(8,128)S(1)} collective-permute-done((f32[2,16,128]{2,1,0:T(8,128)S(1)}, f32[2,16,128]{2,1,0:T(8,128)S(1)}, u32[]{:S(2)}, u32[]{:S(2)}) %collective-permute-start.5) | collective-permute-done | bytes 16416 | tf_op jit(solution)/shard_map/ppermute | solution.py:403
  22.1 2.8 %collective-permute-start.7 = (f32[2,8,128]{2,1,0:T(8,128)S(1)}, f32[2,8,128]{2,1,0:T(8,128)S(1)}, u32[]{:S(2)}, u32[]{:S(2)}) collective-permute-start(f32[2,8,128]{2,1,0:T(8,128)S(1)} %get-tuple-element.137), channel_id=1, source_target_pairs={{0,8},{1,2},{2,1},{3,4},{4,3},{5,6},{6,5},{7,15},{8,0},{9,10},{10,... | collective-permute-start | bytes 24584 | tf_op jit(solution)/shard_map/ppermute | solution.py:406
  24.9 2.1 %collective-permute-start.6 = (f32[2,8,128]{2,1,0:T(8,128)S(1)}, f32[2,8,128]{2,1,0:T(8,128)S(1)}, u32[]{:S(2)}, u32[]{:S(2)}) collective-permute-start(f32[2,8,128]{2,1,0:T(8,128)S(1)} %get-tuple-element.138), channel_id=1, source_target_pairs={{0,1},{1,0},{2,3},{3,2},{4,5},{5,4},{6,7},{7,6},{8,9},{9,8},{10,11... | collective-permute-start | bytes 24584 | tf_op jit(solution)/shard_map/ppermute | solution.py:407
  27.0 1.2 %collective-permute-done.7 = f32[2,8,128]{2,1,0:T(8,128)S(1)} collective-permute-done((f32[2,8,128]{2,1,0:T(8,128)S(1)}, f32[2,8,128]{2,1,0:T(8,128)S(1)}, u32[]{:S(2)}, u32[]{:S(2)}) %collective-permute-start.7) | collective-permute-done | bytes 8224 | tf_op jit(solution)/shard_map/ppermute | solution.py:406
  28.2 1.9 %collective-permute-done.6 = f32[2,8,128]{2,1,0:T(8,128)S(1)} collective-permute-done((f32[2,8,128]{2,1,0:T(8,128)S(1)}, f32[2,8,128]{2,1,0:T(8,128)S(1)}, u32[]{:S(2)}, u32[]{:S(2)}) %collective-permute-start.6) | collective-permute-done | bytes 8224 | tf_op jit(solution)/shard_map/ppermute | solution.py:407
  30.2 0.9 %shard_map.82 = (f32[8,8,128]{2,1,0:T(8,128)S(1)}, f32[2,3,128,128]{3,2,1,0:T(8,128)S(1)}, f32[2,16,128]{2,1,0:T(8,128)S(1)}, f32[2,128,128]{2,1,0:T(8,128)S(1)}...) custom-call(f32[3,2,8,128]{3,2,1,0:T(8,128)S(1)} %pad_maximum_fusion.tiles, ...), custom_call_target="tpu_custom_call" | custom-call | flops 4000000 | bytes 65536 | tf_op jit(solution)/shard_map/pallas_call | solution.py:30
  31.3 0.7 %shard_map.83 = (f32[16,128]{1,0:T(8,128)S(1)}, f32[2,128,128]{2,1,0:T(8,128)S(1)}, f32[2,128,128]{2,1,0:T(8,128)S(1)}, f32[6,128,128]{2,1,0:T(8,128)S(1)}, f32[...) custom-call(f32[3,2,8,128]{3,2,1,0:T(8,128)S(1)} %pad_maximum_fusion, ...), custom_call_target="tpu_custom_call" | custom-call | flops 4000000 | bytes 65536 | tf_op jit(solution)/shard_map/pallas_call | solution.py:30
  33.1 0.9 %collective-permute-done.9 = f32[16,128]{1,0:T(8,128)S(1)} collective-permute-done((f32[16,128]{1,0:T(8,128)S(1)}, f32[16,128]{1,0:T(8,128)S(1)}, u32[]{:S(2)}, u32[]{:S(2)}) %collective-permute-start.9) | collective-permute-done | bytes 8224 | tf_op jit(solution)/shard_map/ppermute | solution.py:400
  34.0 4.3 %collective-permute-done.10 = f32[16,128]{1,0:T(8,128)S(1)} collective-permute-done((f32[16,128]{1,0:T(8,128)S(1)}, f32[16,128]{1,0:T(8,128)S(1)}, u32[]{:S(2)}, u32[]{:S(2)}) %collective-permute-start.10) | collective-permute-done | bytes 8224 | tf_op jit(solution)/shard_map/ppermute | solution.py:403
  38.3 2.2 %collective-permute-start.11 = (f32[8,128]{1,0:T(8,128)S(1)}, f32[8,128]{1,0:T(8,128)S(1)}, u32[]{:S(2)}, u32[]{:S(2)}) collective-permute-start(f32[8,128]{1,0:T(8,128)S(1)} %get-tuple-element.141), channel_id=1, source_target_pairs={{0,1},{1,0},{2,3},{3,2},{4,5},{5,4},{6,7},{7,6},{8,9},{9,8},{10,11... | collective-permute-start | bytes 12296 | tf_op jit(solution)/shard_map/ppermute | solution.py:407
  40.5 1.5 %shard_map.86 = bf16[2,1,2,9,128,128]{5,4,3,2,1,0:T(8,128)(2,1)} custom-call(bf16[2,2,3,3,128,128]{5,4,3,2,1,0:T(8,128)(2,1)S(1)} %get-tuple-element.125.held, f32[2,128,128]{2,1,0:T(8,128)S(1)} %get-tuple-element.126.third, f32[12,128,128]{2,1,0:T(8,128)S(1)} %get-tuple-element.72.refs_0_.len_i, f32[6,128,128]{2,1,0:T(8,128)S(1)} %get-tuple-element.81.refs_3_.len_o, ...), custom_call_target="tpu_custom_call" | custom-call | flops 3000000 | bytes 65536 | tf_op jit(solution)/shard_map/pallas_call | solution.py:30
  42.0 1.4 %collective-permute-done.11 = f32[8,128]{1,0:T(8,128)S(1)} collective-permute-done((f32[8,128]{1,0:T(8,128)S(1)}, f32[8,128]{1,0:T(8,128)S(1)}, u32[]{:S(2)}, u32[]{:S(2)}) %collective-permute-start.11) | collective-permute-done | bytes 4128 | tf_op jit(solution)/shard_map/ppermute | solution.py:407
  43.5 3.0 %collective-permute-done.12 = f32[8,128]{1,0:T(8,128)S(1)} collective-permute-done((f32[8,128]{1,0:T(8,128)S(1)}, f32[8,128]{1,0:T(8,128)S(1)}, u32[]{:S(2)}, u32[]{:S(2)}) %collective-permute-start.12) | collective-permute-done | bytes 4128 | tf_op jit(solution)/shard_map/ppermute | solution.py:406
  (41 shorter events, 3.4 us)
Async XLA Ops:
  2.0 5.5 %copy-start.3 = (f32[2,8,128]{2,1,0:T(8,128)S(1)}, f32[2,8,128]{2,1,0:T(8,128)}, u32[]{:S(2)}) copy-start(f32[2,8,128]{2,1,0:T(8,128)} %shard_map.76) | copy-start | bytes 24580
  2.0 5.5 %collective-permute-start.1 = (f32[2,8,128]{2,1,0:T(8,128)}, f32[2,8,128]{2,1,0:T(8,128)S(1)}, u32[]{:S(2)}, u32[]{:S(2)}) collective-permute-start(f32[2,8,128]{2,1,0:T(8,128)} %shard_map.76), channel_id=1, source_target_pairs={{0,2},{1,3},{2,0},{3,1},{4,6},{5,7},{6,4},{7,5},{8,16},{9,17},{10,... | collective-permute-start | bytes 24584 | tf_op jit(solution)/shard_map/ppermute | solution.py:403
  4.5 3.0 %collective-permute-start = (f32[2,8,128]{2,1,0:T(8,128)}, f32[2,8,128]{2,1,0:T(8,128)S(1)}, u32[]{:S(2)}, u32[]{:S(2)}) collective-permute-start(f32[2,8,128]{2,1,0:T(8,128)} %shard_map.76), channel_id=1, source_target_pairs={{0,8},{8,0},{16,24},{24,16},{32,40},{40,32},{48,56},{56,48},{64,72... | collective-permute-start | bytes 24584 | tf_op jit(solution)/shard_map/ppermute | solution.py:400
  4.5 1.3 %copy-start = (bf16[2,1,2,9,128,128]{5,4,3,2,1,0:T(8,128)(2,1)S(1)}, bf16[2,1,2,9,128,128]{5,4,3,2,1,0:T(8,128)(2,1)}, u32[]{:S(2)}) copy-start(bf16[2,1,2,9,128,128]{5,4,3,2,1,0:T(8,128)(2,1)} %states.1) | copy-start | bytes 3538948
  7.5 6.4 %collective-permute-start.3 = (f32[3,8,128]{2,1,0:T(8,128)S(1)}, f32[3,8,128]{2,1,0:T(8,128)S(1)}, u32[]{:S(2)}, u32[]{:S(2)}) collective-permute-start(f32[3,8,128]{2,1,0:T(8,128)S(1)} %select_bitcast_fusion), channel_id=1, source_target_pairs={{0,8},{1,2},{2,1},{3,4},{4,3},{5,6},{6,5},{7,15},{8,0},{9,10},{10,... | collective-permute-start | bytes 36872 | tf_op jit(solution)/shard_map/ppermute | solution.py:406
  9.3 5.2 %collective-permute-start.2 = (f32[3,8,128]{2,1,0:T(8,128)S(1)}, f32[3,8,128]{2,1,0:T(8,128)S(1)}, u32[]{:S(2)}, u32[]{:S(2)}) collective-permute-start(f32[3,8,128]{2,1,0:T(8,128)S(1)} %fusion), channel_id=1, source_target_pairs={{0,1},{1,0},{2,3},{3,2},{4,5},{5,4},{6,7},{7,6},{8,9},{9,8},{10,11... | collective-permute-start | bytes 36872 | tf_op jit(solution)/shard_map/ppermute | solution.py:407
  14.5 1.1 %copy-start.1 = (f32[3,1,2,128]{3,2,1,0:T(2,128)S(1)}, f32[3,1,2,128]{3,2,1,0:T(2,128)}, u32[]{:S(2)}) copy-start(f32[3,1,2,128]{3,2,1,0:T(2,128)} %shift.1) | copy-start | bytes 9220
  14.5 1.1 %copy-start.2 = (f32[3,1,2,128]{3,2,1,0:T(2,128)S(1)}, f32[3,1,2,128]{3,2,1,0:T(2,128)}, u32[]{:S(2)}) copy-start(f32[3,1,2,128]{3,2,1,0:T(2,128)} %speed.1) | copy-start | bytes 9220
  15.4 1.3 %collective-permute-start.4 = (f32[16,128]{1,0:T(8,128)S(1)}, f32[16,128]{1,0:T(8,128)S(1)}, u32[]{:S(2)}, u32[]{:S(2)}) collective-permute-start(f32[16,128]{1,0:T(8,128)S(1)} %get-tuple-element.82), channel_id=1, source_target_pairs={{0,8},{8,0},{16,24},{24,16},{32,40},{40,32},{48,56},{56,48},{64,72... | collective-permute-start | bytes 24584 | tf_op jit(solution)/shard_map/ppermute | solution.py:400
  16.7 5.4 %collective-permute-start.5 = (f32[2,16,128]{2,1,0:T(8,128)S(1)}, f32[2,16,128]{2,1,0:T(8,128)S(1)}, u32[]{:S(2)}, u32[]{:S(2)}) collective-permute-start(f32[2,16,128]{2,1,0:T(8,128)S(1)} %pad_maximum_fusion.2), channel_id=1, source_target_pairs={{0,2},{1,3},{2,0},{3,1},{4,6},{5,7},{6,4},{7,5},{8,16},{9,17},{10,... | collective-permute-start | bytes 49160 | tf_op jit(solution)/shard_map/ppermute | solution.py:403
  22.1 6.1 %collective-permute-start.7 = (f32[2,8,128]{2,1,0:T(8,128)S(1)}, f32[2,8,128]{2,1,0:T(8,128)S(1)}, u32[]{:S(2)}, u32[]{:S(2)}) collective-permute-start(f32[2,8,128]{2,1,0:T(8,128)S(1)} %get-tuple-element.137), channel_id=1, source_target_pairs={{0,8},{1,2},{2,1},{3,4},{4,3},{5,6},{6,5},{7,15},{8,0},{9,10},{10,... | collective-permute-start | bytes 24584 | tf_op jit(solution)/shard_map/ppermute | solution.py:406
  24.9 5.2 %collective-permute-start.6 = (f32[2,8,128]{2,1,0:T(8,128)S(1)}, f32[2,8,128]{2,1,0:T(8,128)S(1)}, u32[]{:S(2)}, u32[]{:S(2)}) collective-permute-start(f32[2,8,128]{2,1,0:T(8,128)S(1)} %get-tuple-element.138), channel_id=1, source_target_pairs={{0,1},{1,0},{2,3},{3,2},{4,5},{5,4},{6,7},{7,6},{8,9},{9,8},{10,11... | collective-permute-start | bytes 24584 | tf_op jit(solution)/shard_map/ppermute | solution.py:407
  30.1 1.3 %collective-permute-start.8 = (f32[16,128]{1,0:T(8,128)S(1)}, f32[16,128]{1,0:T(8,128)S(1)}, u32[]{:S(2)}, u32[]{:S(2)}) collective-permute-start(f32[16,128]{1,0:T(8,128)S(1)} %fusion.2), channel_id=1, source_target_pairs={{0,8},{8,0},{16,24},{24,16},{32,40},{40,32},{48,56},{56,48},{64,72... | collective-permute-start | bytes 24584 | tf_op jit(solution)/shard_map/ppermute | solution.py:400
  32.7 1.2 %collective-permute-start.9 = (f32[16,128]{1,0:T(8,128)S(1)}, f32[16,128]{1,0:T(8,128)S(1)}, u32[]{:S(2)}, u32[]{:S(2)}) collective-permute-start(f32[16,128]{1,0:T(8,128)S(1)} %get-tuple-element.136), channel_id=1, source_target_pairs={{0,8},{8,0},{16,24},{24,16},{32,40},{40,32},{48,56},{56,48},{64,72... | collective-permute-start | bytes 24584 | tf_op jit(solution)/shard_map/ppermute | solution.py:400
  33.1 5.2 %collective-permute-start.10 = (f32[16,128]{1,0:T(8,128)S(1)}, f32[16,128]{1,0:T(8,128)S(1)}, u32[]{:S(2)}, u32[]{:S(2)}) collective-permute-start(f32[16,128]{1,0:T(8,128)S(1)} %get-tuple-element.118), channel_id=1, source_target_pairs={{0,2},{1,3},{2,0},{3,1},{4,6},{5,7},{6,4},{7,5},{8,16},{9,17},{10,... | collective-permute-start | bytes 24584 | tf_op jit(solution)/shard_map/ppermute | solution.py:403
  38.3 5.2 %collective-permute-start.11 = (f32[8,128]{1,0:T(8,128)S(1)}, f32[8,128]{1,0:T(8,128)S(1)}, u32[]{:S(2)}, u32[]{:S(2)}) collective-permute-start(f32[8,128]{1,0:T(8,128)S(1)} %get-tuple-element.141), channel_id=1, source_target_pairs={{0,1},{1,0},{2,3},{3,2},{4,5},{5,4},{6,7},{7,6},{8,9},{9,8},{10,11... | collective-permute-start | bytes 12296 | tf_op jit(solution)/shard_map/ppermute | solution.py:407
  40.5 6.0 %collective-permute-start.12 = (f32[8,128]{1,0:T(8,128)S(1)}, f32[8,128]{1,0:T(8,128)S(1)}, u32[]{:S(2)}, u32[]{:S(2)}) collective-permute-start(f32[8,128]{1,0:T(8,128)S(1)} %get-tuple-element.142), channel_id=1, source_target_pairs={{0,8},{1,2},{2,1},{3,4},{4,3},{5,6},{6,5},{7,15},{8,0},{9,10},{10,... | collective-permute-start | bytes 12296 | tf_op jit(solution)/shard_map/ppermute | solution.py:406

commit v5 on v4

--- a/solution.py
+++ b/solution.py
@@ -9,7 +9,7 @@
 
 
 N = 128
-CHUNK = 16
+CHUNK = 32
 F32 = jnp.float32
 VMEM = pl.BlockSpec(memory_space=pltpu.VMEM)
 BLOCKS = [(i, h, e) for i in range(3) for h in range(2) for e in range(3)]
@@ -25,7 +25,7 @@
     return jax.ShapeDtypeStruct(shape, F32)
 
 
-def call(body, outs, operands, scratch=(), specs=None, work=0, limit=24):
+def call(body, outs, operands, scratch=(), specs=None, work=0, limit=24, aliases=None):
     cost = pl.CostEstimate(flops=work, bytes_accessed=1 << 16, transcendentals=0) if work else None
     return pl.pallas_call(
         body,
@@ -35,6 +35,7 @@
         scratch_shapes=list(scratch),
         compiler_params=pltpu.CompilerParams(vmem_limit_bytes=limit and limit * 1024 * 1024),
         cost_estimate=cost,
+        input_output_aliases=aliases or {},
     )(*operands)
 
 
@@ -43,7 +44,7 @@
         body(pl.ds(pl.multiple_of(i * CHUNK, CHUNK), CHUNK))
         return carry
 
-    lax.fori_loop(0, N // CHUNK, step, 0)
+    lax.fori_loop(0, N // CHUNK, step, 0, unroll=2)
 
 
 def first_offset(i):
@@ -95,9 +96,8 @@
     each_chunk(body)
 
 
-def measure(at, blocks, target, home, mixed, volume, swell, length_, lever_, weight_, pull_, rest_, stretch_):
-    for n, (i, h, e) in enumerate(blocks):
-        t = target(i, h, e)
+def measure(at, items, home, mixed, volume, swell, length_, lever_, weight_, pull_, rest_, stretch_):
+    for t, h, n, m in items:
         bond = [t[j : j + 1] - home[h][j] for j in range(3)]
         length = root(bond[0] * bond[0] + bond[1] * bond[1] + bond[2] * bond[2])
         close = jnp.maximum(t[6:7] - length, 0.0)
@@ -112,7 +112,7 @@
         lever_[n, at] = lever
         weight_[n, at] = weight
         pull_[n, at] = weight * lax.rsqrt(squared + 0.01)
-        rest_[n, at] = 0.8475 * stretch - mixed[BLOCKS.index((i, h, e)), at]
+        rest_[n, at] = 0.8475 * stretch - mixed[m, at]
         stretch_[n, at] = stretch
 
 
@@ -124,12 +124,34 @@
         home = [[homes[h, j, at] for j in range(6)] for h in range(2)]
         volume = [jnp.zeros((CHUNK, N), F32)] * 2
         swell = [jnp.zeros((CHUNK, N), F32)] * 2
-        measure(at, INNER, lambda i, h, e: tiles.at[i, h + e - 1], home, mixed, volume, swell, *geo)
+        items = [(tiles.at[i, h + e - 1], h, n, BLOCKS.index((i, h, e))) for n, (i, h, e) in enumerate(INNER)]
+        measure(at, items, home, mixed, volume, swell, *geo)
         for h in range(2):
             volume_[h, at] = volume[h]
             swell_[h, at] = swell[h]
 
     each_chunk(body)
+
+
+def measure_side(h, ghost, mixed, homes, volume_in, swell_in, volume_out, swell_out, geo):
+    def body(at):
+        volume, swell = [volume_in[h, at]], [swell_in[h, at]]
+        home = [[homes[h, j, at] for j in range(6)]]
+        items = [(ghost.at[i], 0, 2 * i + h, 6 * i + 5 * h) for i in range(3)]
+        measure(at, items, home, mixed, volume, swell, *geo)
+        volume_out[h, at] = volume[0]
+        swell_out[h, at] = swell[0]
+        volume_out[1 - h, at] = volume_in[1 - h, at]
+        swell_out[1 - h, at] = swell_in[1 - h, at]
+
+    each_chunk(body)
+
+
+def outer_body(columns, arrived, mixed, homes, volume_in, swell_in, volume_out, swell_out, *refs):
+    geo, ghost = refs[:6], refs[6]
+    c = lax.axis_index("col")
+    ghost[...] = jnp.where((c > 0) & (c < columns - 1), arrived[...], 0.0)
+    measure_side(c % 2, ghost, mixed, homes, volume_in, swell_in, volume_out, swell_out, geo)
 
 
 def press(which, force_of, place, homes, first_home, row_in, row_out, col_sum):
@@ -147,7 +169,7 @@
                         part = strength * (place(i, h, e, j) - home[j])
                         total[j] = total[j] + part
                         q = 128 * n + 32 * (h + e) + 8 * j
-                        col_sum[q : q + 8] += part[0:8] + part[8:16]
+                        col_sum[q : q + 8] += (part[0:8] + part[8:16]) + (part[16:24] + part[24:32])
             for j in range(3):
                 row_out[3 * h + j, at] = total[j]
 
@@ -183,22 +205,11 @@
     press(which, force_of, place, homes, 3, row_in, row_out, col_sum)
 
 
-def first_body(tiles, left, right, mixed, homes, volume_, swell_, *refs):
-    inner, (push, third_, shear_, bulk, row_sum), refs = refs[:3], refs[3:8], refs[8:]
+def first_body(tiles, left, right, ghost, mixed, homes, volume_, swell_, *refs):
+    inner, (push, third_, shear_, bulk, row_sum), refs = refs[:3], refs[9:14], refs[14:]
     outer, (vol, swl, col_sum) = refs[:6], refs[6:]
-
-    def measure_outer(at):
-        home = [[homes[h, j, at] for j in range(6)] for h in range(2)]
-        volume = [volume_[h, at] for h in range(2)]
-        swell = [swell_[h, at] for h in range(2)]
-        measure(
-            at, OUTER, lambda i, h, e: tile_of(tiles, left, right, i, h, e), home, mixed, volume, swell, *outer
-        )
-        for h in range(2):
-            vol[h, at] = volume[h]
-            swl[h, at] = swell[h]
-
-    each_chunk(measure_outer)
+    near = 1 - lax.axis_index("col") % 2
+    measure_side(near, ghost, mixed, homes, volume_, swell_, vol, swl, outer)
     for h in range(2):
         here = homes[h, 6]
         mass = jnp.maximum(here * jnp.sum(vol[h], axis=1, keepdims=True), 1.0)
@@ -392,7 +403,8 @@
     s, c = lax.axis_index("slab"), lax.axis_index("col")
     c_odd, low, high = c % 2 == 1, c > 0, c < columns - 1
     inside = (s > 0) & (s < slabs - 1)
-    c_odd, low, high, inside = lax.optimization_barrier((c_odd, low, high, inside))
+    between = low & high
+    c_odd, between, inside = lax.optimization_barrier((c_odd, between, inside))
     slab_near, slab_far = swap_pairs(slabs, 0), row_swaps(slabs, columns)
     col_near, col_far = swap_pairs(columns, 0), inner_swaps(slabs, columns)
 
@@ -405,13 +417,14 @@
     def over_col(to_left, to_right):
         far = lax.ppermute(jnp.where(c_odd, to_right, to_left), ("slab", "col"), col_far)
         near = lax.ppermute(jnp.where(c_odd, to_left, to_right), "col", col_near)
-        from_left = jnp.where(low, jnp.where(c_odd, near, far), 0.0)
-        from_right = jnp.where(high, jnp.where(c_odd, far, near), 0.0)
-        return from_left, from_right
+        inland = jnp.where(between, far, 0.0)
+        from_left = jnp.where(c_odd, near, inland)
+        from_right = jnp.where(c_odd, inland, near)
+        return from_left, from_right, near, far
 
     def add_over_col(sums):
         lo, hi = sums[..., :8, :], sums[..., 8:, :]
-        from_left, from_right = over_col(lo, hi)
+        from_left, from_right, _, _ = over_col(lo, hi)
         return jnp.concatenate([lo + from_left, hi + from_right], axis=-2)
 
     history = jax.ShapeDtypeStruct((2, 2, 3, 3, N, N), back_extension.dtype)
@@ -434,15 +447,23 @@
     held, mixed = call(recall_body, [history, block(18, N, N)], (back_extension,), work=2_000_000)
     near, far, held, mixed = lax.optimization_barrier((near, far, held, mixed))
     tiles = jnp.stack([near, own, jnp.where(inside, far, 0.0)])
-    left, right = over_col(tiles[:, 0], tiles[:, 1])
+    left, right, ghost_near, ghost_far = over_col(tiles[:, 0], tiles[:, 1])
     homes, volume, swell, *inner = call(
         inner_body, [block(2, 7, N, N), pages, pages] + [block(12, N, N)] * 6, (tiles, mixed), work=6_000_000
     )
     three_i = (inner[0], inner[3], inner[4])
+    volume, swell, *outer = call(
+        functools.partial(outer_body, columns),
+        [pages, pages] + [big] * 6,
+        (ghost_far, mixed, homes, volume, swell),
+        scratch=[pltpu.VMEM((3, 8, N), F32)],
+        work=2_000_000,
+    )
     push, third, shear, bulk, rows, *outer = call(
         first_body,
         [block(16, N), pages, pages, pages, big] + [big] * 6,
-        (tiles, left, right, mixed, homes, volume, swell, *three_i),
+        (tiles, left, right, ghost_near, mixed, homes, volume, swell, *three_i, *outer),
+        aliases={11 + k: 5 + k for k in range(6)},
         scratch=[pltpu.VMEM((2, N, N), F32)] * 2 + [column_sums[1]],
         work=4_000_000,
     )

time: 47.3 us -> 46.8 us (0.989)
  the two profiles are of different devices: /device:TPU:34 before, /device:TPU:38 now
where the time goes in v5:
time: 46.8 us; the launch traced here: 46.6 us
  waiting for transfers between devices  21.6 us (46%)
  starting transfers between devices  13.2 us (28%)
  Pallas kernels  9.64 us (21%)
  local copies, waits for them, and re-layouts  1.3 us (3%)
  between operations  0.79 us (2%)
    pallas_call x12, Pallas kernels, call(): pl.pallas_call(body, out_shape=outs, in_specs=specs or [VMEM] * len(opera...  9.64 us
    ppermute x3, waiting for transfers between devices, to_far(): return lax.ppermute(values, ('slab', 'col'), slab_far)  9.44 us
    ppermute x3, starting transfers between devices, over_col(): lax.ppermute(jnp.where(c_odd, to_right, to_left), ('slab', 'col'), col_far)  7.43 us
    ppermute x3, waiting for transfers between devices, over_col(): lax.ppermute(jnp.where(c_odd, to_right, to_left), ('slab', 'col'), col_far)  5.98 us
    ppermute x3, waiting for transfers between devices, over_col(): near = lax.ppermute(jnp.where(c_odd, to_left, to_right), 'col', col_near)  4.49 us
    ppermute x3, starting transfers between devices, to_far(): return lax.ppermute(values, ('slab', 'col'), slab_far)  3.27 us
    ppermute x3, starting transfers between devices, over_col(): near = lax.ppermute(jnp.where(c_odd, to_left, to_right), 'col', col_near)  2.03 us
    ppermute x4, waiting for transfers between devices, to_near(): return lax.ppermute(values, 'slab', slab_near)  1.69 us
  transfers between devices with their start and end apart: 13, of which 12 were waited for; matrix products, arithmetic and copies ran while one was open for 0% of the time, Pallas kernels for 12%

profile of v5, /device:TPU:38, one launch (start us, length us, event | category | flops | bytes accessed | tf_op | source)
XLA Modules:
  0.0 46.6 jit_solution(10112641320903788144)
XLA Ops:
  0.6 1.3 %shard_map.76 = f32[2,8,128]{2,1,0:T(8,128)} custom-call(s32[1,2]{1,0:T(1,128)} %fill_far.1, f32[3,1,2,128]{3,2,1,0:T(2,128)} %rest_far.1, f32[3,1,2,128]{3,2,1,0:T(2,128)} %shift.1), custom_call_target="tpu_custom_call" | custom-call | tf_op jit(solution)/shard_map/pallas_call | solution.py:30
  2.0 2.8 %collective-permute-start.1 = (f32[2,8,128]{2,1,0:T(8,128)}, f32[2,8,128]{2,1,0:T(8,128)S(1)}, u32[]{:S(2)}, u32[]{:S(2)}) collective-permute-start(f32[2,8,128]{2,1,0:T(8,128)} %shard_map.76), channel_id=1, source_target_pairs={{0,2},{1,3},{2,0},{3,1},{4,6},{5,7},{6,4},{7,5},{8,16},{9,17},{10,... | collective-permute-start | bytes 24584 | tf_op jit(solution)/shard_map/ppermute | solution.py:415
  4.8 1.3 %copy-done = bf16[2,1,2,9,128,128]{5,4,3,2,1,0:T(8,128)(2,1)S(1)} copy-done((bf16[2,1,2,9,128,128]{5,4,3,2,1,0:T(8,128)(2,1)S(1)}, bf16[2,1,2,9,128,128]{5,4,3,2,1,0:T(8,128)(2,1)}, u32[]{:S(2)}) %copy-start) | copy-done | bytes 1179672
  6.4 1.1 %collective-permute-done.1 = f32[2,8,128]{2,1,0:T(8,128)S(1)} collective-permute-done((f32[2,8,128]{2,1,0:T(8,128)}, f32[2,8,128]{2,1,0:T(8,128)S(1)}, u32[]{:S(2)}, u32[]{:S(2)}) %collective-permute-start.1) | collective-permute-done | bytes 8224 | tf_op jit(solution)/shard_map/ppermute | solution.py:415
  7.5 2.8 %collective-permute-start.3 = (f32[3,8,128]{2,1,0:T(8,128)S(1)}, f32[3,8,128]{2,1,0:T(8,128)S(1)}, u32[]{:S(2)}, u32[]{:S(2)}) collective-permute-start(f32[3,8,128]{2,1,0:T(8,128)S(1)} %select_bitcast_fusion), channel_id=1, source_target_pairs={{0,8},{1,2},{2,1},{3,4},{4,3},{5,6},{6,5},{7,15},{8,0},{9,10},{10,... | collective-permute-start | bytes 36872 | tf_op jit(solution)/shard_map/ppermute | solution.py:418
  10.7 1.4 %shard_map.78 = (f32[2,7,128,128]{3,2,1,0:T(8,128)S(1)}, f32[2,128,128]{2,1,0:T(8,128)S(1)}, f32[2,128,128]{2,1,0:T(8,128)S(1)}, f32[12,128,128]{2,1,0:T(8,128)S...) custom-call(f32[3,2,8,128]{3,2,1,0:T(8,128)S(1)} %pad_maximum_fusion, ...), custom_call_target="tpu_custom_call" | custom-call | flops 6000000 | bytes 65536 | tf_op jit(solution)/shard_map/pallas_call | solution.py:30
  12.1 1.6 %collective-permute-done.3.arrived = f32[3,8,128]{2,1,0:T(8,128)S(1)} collective-permute-done((f32[3,8,128]{2,1,0:T(8,128)S(1)}, f32[3,8,128]{2,1,0:T(8,128)S(1)}, u32[]{:S(2)}, u32[]{:S(2)}) %collective-permute-start.3) | collective-permute-done | bytes 12320 | tf_op jit(solution)/shard_map/ppermute | solution.py:418
  13.7 1.9 %collective-permute-done.2.ghost = f32[3,8,128]{2,1,0:T(8,128)S(1)} collective-permute-done((f32[3,8,128]{2,1,0:T(8,128)S(1)}, f32[3,8,128]{2,1,0:T(8,128)S(1)}, u32[]{:S(2)}, u32[]{:S(2)}) %collective-permute-start.2) | collective-permute-done | bytes 12320 | tf_op jit(solution)/shard_map/ppermute | solution.py:419
  15.8 0.7 %shard_map.80 = (f32[16,128]{1,0:T(8,128)S(1)}, f32[2,128,128]{2,1,0:T(8,128)S(1)}, f32[2,128,128]{2,1,0:T(8,128)S(1)}, f32[2,128,128]{2,1,0:T(8,128)S(1)}, f32[...) custom-call(f32[3,2,8,128]{3,2,1,0:T(8,128)S(1)} %pad_maximum_fusion, ...), custom_call_target="tpu_custom_call", output_to_operand_aliasing={{5}: (11, {}), {6}: (12, {}), {7}: (13, {}), {8}: (14, {}),... | custom-call | flops 4000000 | bytes 65536 | tf_op jit(solution)/shard_map/pallas_call | solution.py:30
  16.6 0.7 %shard_map.81 = (f32[2,16,128]{2,1,0:T(8,128)S(1)}, f32[2,16,128]{2,1,0:T(8,128)S(1)}) custom-call(f32[3,2,8,128]{3,2,1,0:T(8,128)S(1)} %pad_maximum_fusion.tiles, f32[3,8,128]{2,1,0:T(8,128)S(1)} %get-tuple-element.146.left, f32[3,8,128]{2,1,0:T(8,128)S(1)} %get-tuple-element.145.right, f32[2,7,128,128]{3,2,1,0:T(8,128)S(1)} %get-tuple-element.82.homes, ...), custom_call_target="tpu_custom_call" | custom-call | flops 4000000 | bytes 65536 | tf_op jit(solution)/shard_map/pallas_call | solution.py:30
  18.2 0.7 %shard_map.82 = (bf16[2,2,3,3,128,128]{5,4,3,2,1,0:T(8,128)(2,1)S(1)}, f32[18,128,128]{2,1,0:T(8,128)S(1)}, f32[18,128,128]{2,1,0:T(8,128)S(1)}) custom-call(bf16[2,2,3,3,128,128]{5,4,3,2,1,0:T(8,128)(2,1)S(1)} %get-tuple-element.105.held, f32[2,128,128]{2,1,0:T(8,128)S(1)} %get-tuple-element.106.third, f32[2,128,128]{2,1,0:T(8,128)S(1)} %get-tuple-element.97.shear, ...), custom_call_target="tpu_custom_call" | custom-call | flops 4000000 | bytes 65536 | tf_op jit(solution)/shard_map/pallas_call | solution.py:30
  19.0 4.2 %collective-permute-done.5 = f32[2,16,128]{2,1,0:T(8,128)S(1)} collective-permute-done((f32[2,16,128]{2,1,0:T(8,128)S(1)}, f32[2,16,128]{2,1,0:T(8,128)S(1)}, u32[]{:S(2)}, u32[]{:S(2)}) %collective-permute-start.5) | collective-permute-done | bytes 16416 | tf_op jit(solution)/shard_map/ppermute | solution.py:415
  23.2 1.7 %collective-permute-start.7 = (f32[2,8,128]{2,1,0:T(8,128)S(1)}, f32[2,8,128]{2,1,0:T(8,128)S(1)}, u32[]{:S(2)}, u32[]{:S(2)}) collective-permute-start(f32[2,8,128]{2,1,0:T(8,128)S(1)} %get-tuple-element.151), channel_id=1, source_target_pairs={{0,8},{1,2},{2,1},{3,4},{4,3},{5,6},{6,5},{7,15},{8,0},{9,10},{10,... | collective-permute-start | bytes 24584 | tf_op jit(solution)/shard_map/ppermute | solution.py:418
  24.9 1.4 %collective-permute-start.6 = (f32[2,8,128]{2,1,0:T(8,128)S(1)}, f32[2,8,128]{2,1,0:T(8,128)S(1)}, u32[]{:S(2)}, u32[]{:S(2)}) collective-permute-start(f32[2,8,128]{2,1,0:T(8,128)S(1)} %get-tuple-element.152), channel_id=1, source_target_pairs={{0,1},{1,0},{2,3},{3,2},{4,5},{5,4},{6,7},{7,6},{8,9},{9,8},{10,11... | collective-permute-start | bytes 24584 | tf_op jit(solution)/shard_map/ppermute | solution.py:419
  26.3 3.0 %collective-permute-done.7 = f32[2,8,128]{2,1,0:T(8,128)S(1)} collective-permute-done((f32[2,8,128]{2,1,0:T(8,128)S(1)}, f32[2,8,128]{2,1,0:T(8,128)S(1)}, u32[]{:S(2)}, u32[]{:S(2)}) %collective-permute-start.7) | collective-permute-done | bytes 8224 | tf_op jit(solution)/shard_map/ppermute | solution.py:418
  29.3 0.8 %collective-permute-done.6 = f32[2,8,128]{2,1,0:T(8,128)S(1)} collective-permute-done((f32[2,8,128]{2,1,0:T(8,128)S(1)}, f32[2,8,128]{2,1,0:T(8,128)S(1)}, u32[]{:S(2)}, u32[]{:S(2)}) %collective-permute-start.6) | collective-permute-done | bytes 8224 | tf_op jit(solution)/shard_map/ppermute | solution.py:419
  30.2 0.9 %shard_map.83 = (f32[8,8,128]{2,1,0:T(8,128)S(1)}, f32[2,3,128,128]{3,2,1,0:T(8,128)S(1)}, f32[2,16,128]{2,1,0:T(8,128)S(1)}, f32[2,128,128]{2,1,0:T(8,128)S(1)}...) custom-call(f32[3,2,8,128]{3,2,1,0:T(8,128)S(1)} %pad_maximum_fusion.tiles, ...), custom_call_target="tpu_custom_call" | custom-call | flops 4000000 | bytes 65536 | tf_op jit(solution)/shard_map/pallas_call | solution.py:30
  31.9 0.6 %shard_map.85 = f32[2,16,128]{2,1,0:T(8,128)S(1)} custom-call(f32[12,128,128]{2,1,0:T(8,128)S(1)} %get-tuple-element.79.refs_0_.len_i, f32[6,128,128]{2,1,0:T(8,128)S(1)} %get-tuple-element.95.refs_3_.len_o, f32[2,128,128]{2,1,0:T(8,128)S(1)} %get-tuple-element.127.bulk, f32[8,8,128]{2,1,0:T(8,128)S(1)} %get-tuple-element.122.rows, ...), custom_call_target="tpu_custom_call" | custom-call | flops 4000000 | bytes 65536 | tf_op jit(solution)/shard_map/pallas_call | solution.py:30
  32.9 0.9 %collective-permute-done.9 = f32[16,128]{1,0:T(8,128)S(1)} collective-permute-done((f32[16,128]{1,0:T(8,128)S(1)}, f32[16,128]{1,0:T(8,128)S(1)}, u32[]{:S(2)}, u32[]{:S(2)}) %collective-permute-start.9) | collective-permute-done | bytes 8224 | tf_op jit(solution)/shard_map/ppermute | solution.py:412
  33.8 4.2 %collective-permute-done.10 = f32[16,128]{1,0:T(8,128)S(1)} collective-permute-done((f32[16,128]{1,0:T(8,128)S(1)}, f32[16,128]{1,0:T(8,128)S(1)}, u32[]{:S(2)}, u32[]{:S(2)}) %collective-permute-start.10) | collective-permute-done | bytes 8224 | tf_op jit(solution)/shard_map/ppermute | solution.py:415
  38.1 2.8 %collective-permute-start.12 = (f32[8,128]{1,0:T(8,128)S(1)}, f32[8,128]{1,0:T(8,128)S(1)}, u32[]{:S(2)}, u32[]{:S(2)}) collective-permute-start(f32[8,128]{1,0:T(8,128)S(1)} %get-tuple-element.155), channel_id=1, source_target_pairs={{0,8},{1,2},{2,1},{3,4},{4,3},{5,6},{6,5},{7,15},{8,0},{9,10},{10,... | collective-permute-start | bytes 12296 | tf_op jit(solution)/shard_map/ppermute | solution.py:418
  41.2 1.5 %shard_map.87 = bf16[2,1,2,9,128,128]{5,4,3,2,1,0:T(8,128)(2,1)} custom-call(bf16[2,2,3,3,128,128]{5,4,3,2,1,0:T(8,128)(2,1)S(1)} %get-tuple-element.139.held, f32[2,128,128]{2,1,0:T(8,128)S(1)} %get-tuple-element.140.third, f32[12,128,128]{2,1,0:T(8,128)S(1)} %get-tuple-element.79.refs_0_.len_i, f32[6,128,128]{2,1,0:T(8,128)S(1)} %get-tuple-element.95.refs_3_.len_o, ...), custom_call_target="tpu_custom_call" | custom-call | flops 3000000 | bytes 65536 | tf_op jit(solution)/shard_map/pallas_call | solution.py:30
  42.7 1.4 %collective-permute-done.12 = f32[8,128]{1,0:T(8,128)S(1)} collective-permute-done((f32[8,128]{1,0:T(8,128)S(1)}, f32[8,128]{1,0:T(8,128)S(1)}, u32[]{:S(2)}, u32[]{:S(2)}) %collective-permute-start.12) | collective-permute-done | bytes 4128 | tf_op jit(solution)/shard_map/ppermute | solution.py:418
  44.1 1.9 %collective-permute-done.11 = f32[8,128]{1,0:T(8,128)S(1)} collective-permute-done((f32[8,128]{1,0:T(8,128)S(1)}, f32[8,128]{1,0:T(8,128)S(1)}, u32[]{:S(2)}, u32[]{:S(2)}) %collective-permute-start.11) | collective-permute-done | bytes 4128 | tf_op jit(solution)/shard_map/ppermute | solution.py:419
  (42 shorter events, 4.2 us)
Async XLA Ops:
  2.0 5.5 %copy-start.3 = (f32[2,8,128]{2,1,0:T(8,128)S(1)}, f32[2,8,128]{2,1,0:T(8,128)}, u32[]{:S(2)}) copy-start(f32[2,8,128]{2,1,0:T(8,128)} %shard_map.76) | copy-start | bytes 24580
  2.0 5.5 %collective-permute-start.1 = (f32[2,8,128]{2,1,0:T(8,128)}, f32[2,8,128]{2,1,0:T(8,128)S(1)}, u32[]{:S(2)}, u32[]{:S(2)}) collective-permute-start(f32[2,8,128]{2,1,0:T(8,128)} %shard_map.76), channel_id=1, source_target_pairs={{0,2},{1,3},{2,0},{3,1},{4,6},{5,7},{6,4},{7,5},{8,16},{9,17},{10,... | collective-permute-start | bytes 24584 | tf_op jit(solution)/shard_map/ppermute | solution.py:415
  4.8 2.7 %collective-permute-start = (f32[2,8,128]{2,1,0:T(8,128)}, f32[2,8,128]{2,1,0:T(8,128)S(1)}, u32[]{:S(2)}, u32[]{:S(2)}) collective-permute-start(f32[2,8,128]{2,1,0:T(8,128)} %shard_map.76), channel_id=1, source_target_pairs={{0,8},{8,0},{16,24},{24,16},{32,40},{40,32},{48,56},{56,48},{64,72... | collective-permute-start | bytes 24584 | tf_op jit(solution)/shard_map/ppermute | solution.py:412
  4.8 1.3 %copy-start = (bf16[2,1,2,9,128,128]{5,4,3,2,1,0:T(8,128)(2,1)S(1)}, bf16[2,1,2,9,128,128]{5,4,3,2,1,0:T(8,128)(2,1)}, u32[]{:S(2)}) copy-start(bf16[2,1,2,9,128,128]{5,4,3,2,1,0:T(8,128)(2,1)} %states.1) | copy-start | bytes 3538948
  7.5 6.2 %collective-permute-start.3 = (f32[3,8,128]{2,1,0:T(8,128)S(1)}, f32[3,8,128]{2,1,0:T(8,128)S(1)}, u32[]{:S(2)}, u32[]{:S(2)}) collective-permute-start(f32[3,8,128]{2,1,0:T(8,128)S(1)} %select_bitcast_fusion), channel_id=1, source_target_pairs={{0,8},{1,2},{2,1},{3,4},{4,3},{5,6},{6,5},{7,15},{8,0},{9,10},{10,... | collective-permute-start | bytes 36872 | tf_op jit(solution)/shard_map/ppermute | solution.py:418
  10.3 5.2 %collective-permute-start.2 = (f32[3,8,128]{2,1,0:T(8,128)S(1)}, f32[3,8,128]{2,1,0:T(8,128)S(1)}, u32[]{:S(2)}, u32[]{:S(2)}) collective-permute-start(f32[3,8,128]{2,1,0:T(8,128)S(1)} %fusion), channel_id=1, source_target_pairs={{0,1},{1,0},{2,3},{3,2},{4,5},{5,4},{6,7},{7,6},{8,9},{9,8},{10,11... | collective-permute-start | bytes 36872 | tf_op jit(solution)/shard_map/ppermute | solution.py:419
  15.8 0.8 %copy-start.1 = (f32[3,1,2,128]{3,2,1,0:T(2,128)S(1)}, f32[3,1,2,128]{3,2,1,0:T(2,128)}, u32[]{:S(2)}) copy-start(f32[3,1,2,128]{3,2,1,0:T(2,128)} %shift.1) | copy-start | bytes 9220
  15.8 0.8 %copy-start.2 = (f32[3,1,2,128]{3,2,1,0:T(2,128)S(1)}, f32[3,1,2,128]{3,2,1,0:T(2,128)}, u32[]{:S(2)}) copy-start(f32[3,1,2,128]{3,2,1,0:T(2,128)} %speed.1) | copy-start | bytes 9220
  16.5 1.3 %collective-permute-start.4 = (f32[16,128]{1,0:T(8,128)S(1)}, f32[16,128]{1,0:T(8,128)S(1)}, u32[]{:S(2)}, u32[]{:S(2)}) collective-permute-start(f32[16,128]{1,0:T(8,128)S(1)} %get-tuple-element.96), channel_id=1, source_target_pairs={{0,8},{8,0},{16,24},{24,16},{32,40},{40,32},{48,56},{56,48},{64,72... | collective-permute-start | bytes 24584 | tf_op jit(solution)/shard_map/ppermute | solution.py:412
  17.8 5.4 %collective-permute-start.5 = (f32[2,16,128]{2,1,0:T(8,128)S(1)}, f32[2,16,128]{2,1,0:T(8,128)S(1)}, u32[]{:S(2)}, u32[]{:S(2)}) collective-permute-start(f32[2,16,128]{2,1,0:T(8,128)S(1)} %pad_maximum_fusion.2), channel_id=1, source_target_pairs={{0,2},{1,3},{2,0},{3,1},{4,6},{5,7},{6,4},{7,5},{8,16},{9,17},{10,... | collective-permute-start | bytes 49160 | tf_op jit(solution)/shard_map/ppermute | solution.py:415
  23.2 6.1 %collective-permute-start.7 = (f32[2,8,128]{2,1,0:T(8,128)S(1)}, f32[2,8,128]{2,1,0:T(8,128)S(1)}, u32[]{:S(2)}, u32[]{:S(2)}) collective-permute-start(f32[2,8,128]{2,1,0:T(8,128)S(1)} %get-tuple-element.151), channel_id=1, source_target_pairs={{0,8},{1,2},{2,1},{3,4},{4,3},{5,6},{6,5},{7,15},{8,0},{9,10},{10,... | collective-permute-start | bytes 24584 | tf_op jit(solution)/shard_map/ppermute | solution.py:418
  24.9 5.2 %collective-permute-start.6 = (f32[2,8,128]{2,1,0:T(8,128)S(1)}, f32[2,8,128]{2,1,0:T(8,128)S(1)}, u32[]{:S(2)}, u32[]{:S(2)}) collective-permute-start(f32[2,8,128]{2,1,0:T(8,128)S(1)} %get-tuple-element.152), channel_id=1, source_target_pairs={{0,1},{1,0},{2,3},{3,2},{4,5},{5,4},{6,7},{7,6},{8,9},{9,8},{10,11... | collective-permute-start | bytes 24584 | tf_op jit(solution)/shard_map/ppermute | solution.py:419
  30.1 1.3 %collective-permute-start.8 = (f32[16,128]{1,0:T(8,128)S(1)}, f32[16,128]{1,0:T(8,128)S(1)}, u32[]{:S(2)}, u32[]{:S(2)}) collective-permute-start(f32[16,128]{1,0:T(8,128)S(1)} %fusion.2), channel_id=1, source_target_pairs={{0,8},{8,0},{16,24},{24,16},{32,40},{40,32},{48,56},{56,48},{64,72... | collective-permute-start | bytes 24584 | tf_op jit(solution)/shard_map/ppermute | solution.py:412
  32.6 1.2 %collective-permute-start.9 = (f32[16,128]{1,0:T(8,128)S(1)}, f32[16,128]{1,0:T(8,128)S(1)}, u32[]{:S(2)}, u32[]{:S(2)}) collective-permute-start(f32[16,128]{1,0:T(8,128)S(1)} %get-tuple-element.150), channel_id=1, source_target_pairs={{0,8},{8,0},{16,24},{24,16},{32,40},{40,32},{48,56},{56,48},{64,72... | collective-permute-start | bytes 24584 | tf_op jit(solution)/shard_map/ppermute | solution.py:412
  32.9 5.2 %collective-permute-start.10 = (f32[16,128]{1,0:T(8,128)S(1)}, f32[16,128]{1,0:T(8,128)S(1)}, u32[]{:S(2)}, u32[]{:S(2)}) collective-permute-start(f32[16,128]{1,0:T(8,128)S(1)} %get-tuple-element.132), channel_id=1, source_target_pairs={{0,2},{1,3},{2,0},{3,1},{4,6},{5,7},{6,4},{7,5},{8,16},{9,17},{10,... | collective-permute-start | bytes 24584 | tf_op jit(solution)/shard_map/ppermute | solution.py:415
  38.1 6.1 %collective-permute-start.12 = (f32[8,128]{1,0:T(8,128)S(1)}, f32[8,128]{1,0:T(8,128)S(1)}, u32[]{:S(2)}, u32[]{:S(2)}) collective-permute-start(f32[8,128]{1,0:T(8,128)S(1)} %get-tuple-element.155), channel_id=1, source_target_pairs={{0,8},{1,2},{2,1},{3,4},{4,3},{5,6},{6,5},{7,15},{8,0},{9,10},{10,... | collective-permute-start | bytes 12296 | tf_op jit(solution)/shard_map/ppermute | solution.py:418
  40.9 5.1 %collective-permute-start.11 = (f32[8,128]{1,0:T(8,128)S(1)}, f32[8,128]{1,0:T(8,128)S(1)}, u32[]{:S(2)}, u32[]{:S(2)}) collective-permute-start(f32[8,128]{1,0:T(8,128)S(1)} %get-tuple-element.156), channel_id=1, source_target_pairs={{0,1},{1,0},{2,3},{3,2},{4,5},{5,4},{6,7},{7,6},{8,9},{9,8},{10,11... | collective-permute-start | bytes 12296 | tf_op jit(solution)/shard_map/ppermute | solution.py:419
